TPU v7x, 128 devices: a whole 4x4x4 slice. The times are simulated.
128 devices in a mesh: gx: 8 (over x, core), yz: 16 (over y, z).
Axes of the slice: x: 4, y: 4, z: 4, core: 2. Of those that a mesh axis runs over, the one named last changes fastest.
Arguments:
- ref_pos: float32 [4096, 3, 128], P(('gx', 'yz')), may hold values from 0 to 1
- disp: float32 [4096, 3, 128], P(('gx', 'yz')), may hold values from -1.2 to 1.2
- volume: float32 [4096, 128], P(('gx', 'yz')), may hold values from 0.5 to 2
- lame: float32 [4096, 2, 128], P(('gx', 'yz')), may hold values from 0.3 to 3
- pad_count: int32 [4096], P(('gx', 'yz')), may hold values from 0 to 63
- nbr_owner: int32 [4096, 8, 1], P(('gx', 'yz')), may hold values from 0 to 127; in each aligned block of 256 rows (0 to 255, 256 to 511, ..., all dimensions but the last counted through in order) at most 4 rows name the same one
- nbr_local: int32 [4096, 8], P(('gx', 'yz')), may hold values from 0 to 31
- contact_block: int32 [4096, 2], P(('gx', 'yz')), may hold values from 0 to 4095, as said below
Outputs:
- force: float32 [4096, 3, 128], P(('gx', 'yz'))
- piola: float32 [4096, 9, 128], P(('gx', 'yz'))
Inputs may be any that keep to these rules, and one draw needn't show every extreme that they name: `nbr_owner`: among the 256 entries of one device's blocks no owner device is named more than 4 times; in every draw some device names some owner exactly 4 times. `contact_block`: each entry names one of the last 4 blocks of the device one step lower along gx with the same yz index, or one of the first 4 blocks of the device one step higher along gx with the same yz index.
All inputs are finite; a program needn't handle non-finite values.
Results may differ from a plain program's by a relative error of at most 0.0003.
Values sent between devices are 32-bit elements; how exact they have to be, the bound alone decides.
No kernel may reach another device: no remote copies, remote signals or barrier semaphores. Data moves between devices by JAX's collectives and lax.ppermute only.
A program may use at most 64 MiB of HBM per device.

v0:
```python
import math

import jax
import jax.numpy as jnp
from jax import lax
from jax.sharding import PartitionSpec as P

SH = 4


support_sq = 0.5
contact_sq = 0.1
penalty = 200.0
group_blocks = 4
highest = lax.Precision.HIGHEST


def padded(cells, sides, width):
    for axis, dim in sides:
        count = lax.axis_size(axis)
        ends = count - 1
        head = lax.slice_in_dim(cells, 0, width, axis=dim)
        tail = lax.slice_in_dim(cells, cells.shape[dim] - width, cells.shape[dim], axis=dim)
        cells = jnp.concatenate(
            [
                lax.ppermute(tail, axis, [(i, (i + 1) % count) for i in range(ends)]),
                cells,
                lax.ppermute(head, axis, [((i + 1) % count, i) for i in range(ends)]),
            ],
            axis=dim,
        )
    return cells


def block_terms(own_data, lame_block, neighbours, partners):
    block_len = own_data.shape[-1]
    fanout = neighbours.shape[0]
    identity = jnp.eye(3, dtype=own_data.dtype)[:, :, None]
    anchor = own_data[0:3]
    moved = own_data[3:6]
    weight = own_data[6]
    inside = (weight > 0).astype(own_data.dtype)
    offset = anchor[:, None, :, None] - jnp.transpose(neighbours[:, 0:3], (1, 0, 2))[:, :, None, :]
    radius = jnp.sum(offset * offset, axis=0)
    kernel = jnp.square(jnp.maximum(1.0 - radius / support_sq, 0.0))
    slope = -3.0 / math.sqrt(fanout * block_len) * kernel[None] * offset
    far_weight = neighbours[:, 6]
    column = jnp.einsum("ckij,kj->ci", slope, far_weight, precision=highest)
    spread = jnp.einsum(
        "ckij,kaj->aci", slope, far_weight[:, None, :] * neighbours[:, 3:6], precision=highest
    )
    deform = identity + spread - moved[:, None, :] * column[None, :, :]
    strain = 0.5 * (jnp.einsum("cai,cbi->abi", deform, deform, precision=highest) - identity)
    trace = strain[0, 0] + strain[1, 1] + strain[2, 2]
    second = lame_block[0] * trace * identity + 2.0 * lame_block[1] * strain
    piola = jnp.einsum("aci,cbi->abi", deform, second, precision=highest) * inside
    own_force = weight * jnp.einsum("abi,bi->ai", piola, column, precision=highest)
    returned_part = -far_weight[:, None, :] * jnp.einsum(
        "bkij,abi->kaj", slope, weight * piola, precision=highest
    )
    current = anchor + moved
    separation = (
        current[:, None, :, None] - jnp.transpose(partners[:, 0:3], (1, 0, 2))[:, :, None, :]
    )
    intersection = jnp.square(
        jnp.maximum(contact_sq - jnp.sum(separation * separation, axis=0), 0.0)
    )
    contact_push = (
        penalty
        * inside
        * jnp.einsum(
            "ckij,kj->ci", separation * intersection[None], partners[:, 3], precision=highest
        )
    )
    return (piola.reshape(9, block_len), own_force + contact_push, returned_part)


def group_terms(inputs):
    return jax.vmap(block_terms)(*inputs)


def per_device(ref_pos, disp, volume, lame, pad_count, nbr_owner, nbr_local, contact_block):
    blocks, _, block_len = ref_pos.shape
    fanout = nbr_local.shape[1]
    across = lax.axis_size("gx")
    depth_axis = lax.axis_size("yz")
    devices = across * depth_axis
    capacity = 2 * blocks * fanout // devices
    usable = (jnp.arange(block_len)[None, :] < (block_len - pad_count)[:, None]).astype(jnp.float32)
    weight = volume * usable
    packed = jnp.concatenate([ref_pos, disp, weight[:, None, :]], axis=1)
    surface = jnp.concatenate([ref_pos + disp, weight[:, None, :]], axis=1)
    owners = nbr_owner[:, :, 0].reshape(-1)
    wanted = nbr_local.reshape(-1)
    position = jnp.arange(owners.shape[0])
    before = (owners[:, None] == owners[None, :]) & (position[:, None] > position[None, :])
    ranking = jnp.sum(before.astype(jnp.int32), axis=1)
    slots = owners * capacity + ranking
    requests = jnp.full((devices * capacity,), -1, jnp.int32).at[slots].set(wanted)
    slot_ids = lax.all_to_all(
        requests.reshape(devices, capacity), ("gx", "yz"), split_axis=0, concat_axis=0, tiled=True
    )
    picked_rows = packed[jnp.maximum(slot_ids, 0)]
    fetched = lax.all_to_all(picked_rows, ("gx", "yz"), split_axis=0, concat_axis=0, tiled=True)
    fetched = fetched.reshape(devices * capacity, 7, block_len)
    neighbours = fetched[slots].reshape(blocks, fanout, 7, block_len)
    extended = padded(surface, (("gx", 0),), SH)
    partner_local = contact_block % blocks
    partner_row = contact_block // blocks // depth_axis
    mine = lax.axis_index("gx")
    partner_index = jnp.where(
        partner_row < mine, partner_local - (blocks - SH), SH + blocks + partner_local
    )
    partners = extended[partner_index]
    groups = blocks // group_blocks

    def split_up(array):
        return array.reshape((groups, group_blocks) + array.shape[1:])

    piola, forces, returned_part = lax.map(
        group_terms, (split_up(packed), split_up(lame), split_up(neighbours), split_up(partners))
    )
    piola = piola.reshape(blocks, 9, block_len)
    forces = forces.reshape(blocks, 3, block_len)
    outgoing = (
        jnp.zeros((devices * capacity, 3, block_len), jnp.float32)
        .at[slots]
        .set(returned_part.reshape(-1, 3, block_len))
    )
    received = lax.all_to_all(
        outgoing.reshape(devices, capacity, 3, block_len),
        ("gx", "yz"),
        split_axis=0,
        concat_axis=0,
        tiled=True,
    )
    received = received.reshape(devices * capacity, 3, block_len)
    flat_ids = slot_ids.reshape(-1)
    returned = (
        jnp.zeros_like(forces)
        .at[jnp.maximum(flat_ids, 0)]
        .add(jnp.where(flat_ids[:, None, None] >= 0, received, 0.0))
    )
    return (forces + returned, piola)


def solution(mesh):
    return jax.shard_map(
        per_device,
        mesh=mesh,
        in_specs=(
            P(("gx", "yz"), None, None),
            P(("gx", "yz"), None, None),
            P(("gx", "yz"), None),
            P(("gx", "yz"), None, None),
            P(("gx", "yz")),
            P(("gx", "yz"), None, None),
            P(("gx", "yz"), None),
            P(("gx", "yz"), None),
        ),
        out_specs=(P(("gx", "yz"), None, None), P(("gx", "yz"), None, None)),
        check_vma=False,
    )
```

profile of v0, /device:TPU:1, one launch (start us, length us, event | category | flops | bytes accessed | tf_op | source)
XLA Modules:
  0.0 425.1 jit_solution(16857519210022546746)
XLA Ops:
  5.5 11.5 %all-to-all-start = ((s32[128,1,4]{2,1,0:T(1,128)}), s32[128,1,4]{2,1,0:T(1,128)S(1)}, u32[]{:S(2)}, u32[]{:S(2)}) async-start(s32[128,1,4]{2,1,0:T(1,128)} %bitcast.44), calls=%async_computation | async-start | bytes 131072 | tf_op jit(solution)/shard_map/all_to_all | solution.py:100
  20.2 6.4 %all-to-all-done = s32[128,1,4]{2,1,0:T(1,128)S(1)} async-done(((s32[128,1,4]{2,1,0:T(1,128)}), s32[128,1,4]{2,1,0:T(1,128)S(1)}, u32[]{:S(2)}, u32[]{:S(2)}) %all-to-all-start) | async-done | bytes 2080 | tf_op jit(solution)/shard_map/all_to_all | solution.py:100
  31.4 4.6 %all-to-all-start.1 = ((f32[128,4,7,128]{3,1,2,0:T(4,128)}), f32[128,4,7,128]{3,1,2,0:T(4,128)S(1)}, u32[]{:S(2)}, u32[]{:S(2)}) async-start(f32[128,4,7,128]{3,1,2,0:T(4,128)} %copy.124), calls=%async_computation.1 | async-start | bytes 3670016 | tf_op jit(solution)/shard_map/all_to_all | solution.py:104
  42.6 11.8 %collective-permute-done = f32[4,4,128]{2,0,1:T(4,128)S(1)} collective-permute-done((f32[4,4,128]{2,0,1:T(4,128)S(1)}, f32[4,4,128]{2,0,1:T(4,128)S(1)}, u32[]{:S(2)}, u32[]{:S(2)}) %collective-permute-start) | collective-permute-done | bytes 8224 | tf_op jit(solution)/shard_map/ppermute | solution.py:26
  67.8 297.8 %while.16 = (s32[]{:T(128)}, f32[8,4,9,128]{3,1,0,2:T(4,128)}, f32[8,4,3,128]{3,2,1,0:T(4,128)S(1)}, f32[8,4,8,3,128]{4,3,2,1,0:T(4,128)}, f32[8,4,2,128]{3,2,1,...) while((s32[]{:T(128)}, f32[8,4,9,128]{3,1,0,2:T(4,128)}, ...), condition=%wide.region_5.6_spmd, body=%wide.region_2.5_spmd.sunk | while | flops 155748880 | bytes 33131908 | solution.py:120
  70.7 5.8 %fusion.73 = f32[4,1,3,128,1]{3,1,4,2,0:T(1,128)S(1)} fusion(f32[4,8,128,128]{3,2,1,0:T(8,128)S(1)} %multiply_multiply_fusion.2, f32[4,3,8,128]{3,1,2,0:T(4,128)S(1)} %slice_bitcast_fusion.9, f32[4,3,128]{2,1,0:T(4,128)S(1)} %get-tuple-element.241, f32[4,8,7,128]{3,2,1,0:T(8,128)S(1)} %dynamic-slice_bitcast_fusion.6), kind=kOutput, calls=%fused_computation.34.clone.1 | convolution fusion | flops 22020096 | bytes 2193408 | tf_op jit(solution)/shard_map/while/body/eval_jaxpr/vmap(ckij,kj->ci)/dot_general | solution.py:48
  77.2 5.3 %fusion.75 = f32[4,3,3,128]{3,1,2,0:T(4,128)S(1)} fusion(f32[4,8,128,128]{3,2,1,0:T(8,128)S(1)} %multiply_multiply_fusion.2, f32[4,3,8,128]{3,1,2,0:T(4,128)S(1)} %slice_bitcast_fusion.9, f32[4,3,128]{2,1,0:T(4,128)S(1)} %get-tuple-element.241, f32[4,8,7,128]{3,2,1,0:T(8,128)S(1)} %dynamic-slice_bitcast_fusion.6, f32[4,8,128]{2,1,0:T(8,128)S(1)} %bitcast.212, ...), kind=kOutput, calls=%fused_computation.33.clone.1 | convolution fusion | flops 59794944 | bytes 2289664 | tf_op jit(solution)/shard_map/while/body/eval_jaxpr/vmap(ckij,kaj->aci)/dot_general | solution.py:49
  83.0 4.3 fusion.76
  90.3 5.2 %multiply_reduce_fusion.2 = (f32[4,128,3]{2,1,0:T(8,128)S(1)}, f32[4,128,3,3]{3,2,1,0:T(4,128)S(1)}) fusion(f32[4,128,3]{2,1,0:T(8,128)} %copy.183, f32[4,128]{1,0:T(4,128)S(1)} %compare_convert_fusion.2, f32[4,3,3,128]{1,2,3,0:T(4,128)S(1)} %copy.187, f32[4,3,3,128]{2,1,3,0:T(4,128)S(1)} %copy.184), kind=kOutput, calls=%fused_computation.35.clone.1 | convolution fusion | flops 178176 | bytes 69632 | tf_op jit(solution)/shard_map/while/body/eval_jaxpr/vmap(aci,cbi->abi)/dot_general | solution.py:56
  97.1 4.2 fusion.82
  107.9 5.8 %fusion.73 = f32[4,1,3,128,1]{3,1,4,2,0:T(1,128)S(1)} fusion(f32[4,8,128,128]{3,2,1,0:T(8,128)S(1)} %multiply_multiply_fusion.2, f32[4,3,8,128]{3,1,2,0:T(4,128)S(1)} %slice_bitcast_fusion.9, f32[4,3,128]{2,1,0:T(4,128)S(1)} %get-tuple-element.241, f32[4,8,7,128]{3,2,1,0:T(8,128)S(1)} %dynamic-slice_bitcast_fusion.6), kind=kOutput, calls=%fused_computation.34.clone.1 | convolution fusion | flops 22020096 | bytes 2193408 | tf_op jit(solution)/shard_map/while/body/eval_jaxpr/vmap(ckij,kj->ci)/dot_general | solution.py:48
  114.4 5.3 %fusion.75 = f32[4,3,3,128]{3,1,2,0:T(4,128)S(1)} fusion(f32[4,8,128,128]{3,2,1,0:T(8,128)S(1)} %multiply_multiply_fusion.2, f32[4,3,8,128]{3,1,2,0:T(4,128)S(1)} %slice_bitcast_fusion.9, f32[4,3,128]{2,1,0:T(4,128)S(1)} %get-tuple-element.241, f32[4,8,7,128]{3,2,1,0:T(8,128)S(1)} %dynamic-slice_bitcast_fusion.6, f32[4,8,128]{2,1,0:T(8,128)S(1)} %bitcast.212, ...), kind=kOutput, calls=%fused_computation.33.clone.1 | convolution fusion | flops 59794944 | bytes 2289664 | tf_op jit(solution)/shard_map/while/body/eval_jaxpr/vmap(ckij,kaj->aci)/dot_general | solution.py:49
  120.2 4.3 fusion.76
  127.5 5.2 %multiply_reduce_fusion.2 = (f32[4,128,3]{2,1,0:T(8,128)S(1)}, f32[4,128,3,3]{3,2,1,0:T(4,128)S(1)}) fusion(f32[4,128,3]{2,1,0:T(8,128)} %copy.183, f32[4,128]{1,0:T(4,128)S(1)} %compare_convert_fusion.2, f32[4,3,3,128]{1,2,3,0:T(4,128)S(1)} %copy.187, f32[4,3,3,128]{2,1,3,0:T(4,128)S(1)} %copy.184), kind=kOutput, calls=%fused_computation.35.clone.1 | convolution fusion | flops 178176 | bytes 69632 | tf_op jit(solution)/shard_map/while/body/eval_jaxpr/vmap(aci,cbi->abi)/dot_general | solution.py:56
  134.3 4.2 fusion.82
  145.1 5.8 %fusion.73 = f32[4,1,3,128,1]{3,1,4,2,0:T(1,128)S(1)} fusion(f32[4,8,128,128]{3,2,1,0:T(8,128)S(1)} %multiply_multiply_fusion.2, f32[4,3,8,128]{3,1,2,0:T(4,128)S(1)} %slice_bitcast_fusion.9, f32[4,3,128]{2,1,0:T(4,128)S(1)} %get-tuple-element.241, f32[4,8,7,128]{3,2,1,0:T(8,128)S(1)} %dynamic-slice_bitcast_fusion.6), kind=kOutput, calls=%fused_computation.34.clone.1 | convolution fusion | flops 22020096 | bytes 2193408 | tf_op jit(solution)/shard_map/while/body/eval_jaxpr/vmap(ckij,kj->ci)/dot_general | solution.py:48
  151.6 5.3 %fusion.75 = f32[4,3,3,128]{3,1,2,0:T(4,128)S(1)} fusion(f32[4,8,128,128]{3,2,1,0:T(8,128)S(1)} %multiply_multiply_fusion.2, f32[4,3,8,128]{3,1,2,0:T(4,128)S(1)} %slice_bitcast_fusion.9, f32[4,3,128]{2,1,0:T(4,128)S(1)} %get-tuple-element.241, f32[4,8,7,128]{3,2,1,0:T(8,128)S(1)} %dynamic-slice_bitcast_fusion.6, f32[4,8,128]{2,1,0:T(8,128)S(1)} %bitcast.212, ...), kind=kOutput, calls=%fused_computation.33.clone.1 | convolution fusion | flops 59794944 | bytes 2289664 | tf_op jit(solution)/shard_map/while/body/eval_jaxpr/vmap(ckij,kaj->aci)/dot_general | solution.py:49
  157.4 4.3 fusion.76
  164.7 5.2 %multiply_reduce_fusion.2 = (f32[4,128,3]{2,1,0:T(8,128)S(1)}, f32[4,128,3,3]{3,2,1,0:T(4,128)S(1)}) fusion(f32[4,128,3]{2,1,0:T(8,128)} %copy.183, f32[4,128]{1,0:T(4,128)S(1)} %compare_convert_fusion.2, f32[4,3,3,128]{1,2,3,0:T(4,128)S(1)} %copy.187, f32[4,3,3,128]{2,1,3,0:T(4,128)S(1)} %copy.184), kind=kOutput, calls=%fused_computation.35.clone.1 | convolution fusion | flops 178176 | bytes 69632 | tf_op jit(solution)/shard_map/while/body/eval_jaxpr/vmap(aci,cbi->abi)/dot_general | solution.py:56
  171.5 4.2 fusion.82
  182.4 5.8 %fusion.73 = f32[4,1,3,128,1]{3,1,4,2,0:T(1,128)S(1)} fusion(f32[4,8,128,128]{3,2,1,0:T(8,128)S(1)} %multiply_multiply_fusion.2, f32[4,3,8,128]{3,1,2,0:T(4,128)S(1)} %slice_bitcast_fusion.9, f32[4,3,128]{2,1,0:T(4,128)S(1)} %get-tuple-element.241, f32[4,8,7,128]{3,2,1,0:T(8,128)S(1)} %dynamic-slice_bitcast_fusion.6), kind=kOutput, calls=%fused_computation.34.clone.1 | convolution fusion | flops 22020096 | bytes 2193408 | tf_op jit(solution)/shard_map/while/body/eval_jaxpr/vmap(ckij,kj->ci)/dot_general | solution.py:48
  188.9 5.3 %fusion.75 = f32[4,3,3,128]{3,1,2,0:T(4,128)S(1)} fusion(f32[4,8,128,128]{3,2,1,0:T(8,128)S(1)} %multiply_multiply_fusion.2, f32[4,3,8,128]{3,1,2,0:T(4,128)S(1)} %slice_bitcast_fusion.9, f32[4,3,128]{2,1,0:T(4,128)S(1)} %get-tuple-element.241, f32[4,8,7,128]{3,2,1,0:T(8,128)S(1)} %dynamic-slice_bitcast_fusion.6, f32[4,8,128]{2,1,0:T(8,128)S(1)} %bitcast.212, ...), kind=kOutput, calls=%fused_computation.33.clone.1 | convolution fusion | flops 59794944 | bytes 2289664 | tf_op jit(solution)/shard_map/while/body/eval_jaxpr/vmap(ckij,kaj->aci)/dot_general | solution.py:49
  194.6 4.3 %fusion.76 = f32[4,128,3,3]{3,2,1,0:T(4,128)S(1)} fusion(f32[4,3,3,128]{2,1,3,0:T(4,128)S(1)} %copy.184), kind=kOutput, calls=%fused_computation.107.clone.1 | convolution fusion | flops 165888 | bytes 36864 | tf_op jit(solution)/shard_map/while/body/eval_jaxpr/vmap(cai,cbi->abi)/dot_general | solution.py:53
  201.9 5.2 %multiply_reduce_fusion.2 = (f32[4,128,3]{2,1,0:T(8,128)S(1)}, f32[4,128,3,3]{3,2,1,0:T(4,128)S(1)}) fusion(f32[4,128,3]{2,1,0:T(8,128)} %copy.183, f32[4,128]{1,0:T(4,128)S(1)} %compare_convert_fusion.2, f32[4,3,3,128]{1,2,3,0:T(4,128)S(1)} %copy.187, f32[4,3,3,128]{2,1,3,0:T(4,128)S(1)} %copy.184), kind=kOutput, calls=%fused_computation.35.clone.1 | convolution fusion | flops 178176 | bytes 69632 | tf_op jit(solution)/shard_map/while/body/eval_jaxpr/vmap(aci,cbi->abi)/dot_general | solution.py:56
  208.7 4.3 %fusion.82 = f32[8,4,8,3,128]{4,3,2,1,0:T(4,128)} fusion(f32[8,4,8,3,128]{4,3,2,1,0:T(4,128)} %get-tuple-element.264, s32[]{:T(128)} %get-tuple-element.261, f32[4,8,128,128]{3,2,1,0:T(8,128)S(1)} %copy-done.1, f32[4,3,8,128]{3,1,2,0:T(4,128)S(1)} %slice_bitcast_fusion.9, f32[4,3,128]{2,1,0:T(4,128)S(1)} %get-tuple-element.241, ...), kind=kOutput, calls=%fused_computation.30.clone.1 | convolution fusion | flops 59781120 | bytes 2253312 | tf_op jit(solution)/shard_map/while/body/eval_jaxpr/vmap(bkij,abi->kaj)/dot_general | solution.py:58
  219.6 5.8 %fusion.73 = f32[4,1,3,128,1]{3,1,4,2,0:T(1,128)S(1)} fusion(f32[4,8,128,128]{3,2,1,0:T(8,128)S(1)} %multiply_multiply_fusion.2, f32[4,3,8,128]{3,1,2,0:T(4,128)S(1)} %slice_bitcast_fusion.9, f32[4,3,128]{2,1,0:T(4,128)S(1)} %get-tuple-element.241, f32[4,8,7,128]{3,2,1,0:T(8,128)S(1)} %dynamic-slice_bitcast_fusion.6), kind=kOutput, calls=%fused_computation.34.clone.1 | convolution fusion | flops 22020096 | bytes 2193408 | tf_op jit(solution)/shard_map/while/body/eval_jaxpr/vmap(ckij,kj->ci)/dot_general | solution.py:48
  226.1 5.3 %fusion.75 = f32[4,3,3,128]{3,1,2,0:T(4,128)S(1)} fusion(f32[4,8,128,128]{3,2,1,0:T(8,128)S(1)} %multiply_multiply_fusion.2, f32[4,3,8,128]{3,1,2,0:T(4,128)S(1)} %slice_bitcast_fusion.9, f32[4,3,128]{2,1,0:T(4,128)S(1)} %get-tuple-element.241, f32[4,8,7,128]{3,2,1,0:T(8,128)S(1)} %dynamic-slice_bitcast_fusion.6, f32[4,8,128]{2,1,0:T(8,128)S(1)} %bitcast.212, ...), kind=kOutput, calls=%fused_computation.33.clone.1 | convolution fusion | flops 59794944 | bytes 2289664 | tf_op jit(solution)/shard_map/while/body/eval_jaxpr/vmap(ckij,kaj->aci)/dot_general | solution.py:49
  231.9 4.3 %fusion.76 = f32[4,128,3,3]{3,2,1,0:T(4,128)S(1)} fusion(f32[4,3,3,128]{2,1,3,0:T(4,128)S(1)} %copy.184), kind=kOutput, calls=%fused_computation.107.clone.1 | convolution fusion | flops 165888 | bytes 36864 | tf_op jit(solution)/shard_map/while/body/eval_jaxpr/vmap(cai,cbi->abi)/dot_general | solution.py:53
  239.2 5.2 %multiply_reduce_fusion.2 = (f32[4,128,3]{2,1,0:T(8,128)S(1)}, f32[4,128,3,3]{3,2,1,0:T(4,128)S(1)}) fusion(f32[4,128,3]{2,1,0:T(8,128)} %copy.183, f32[4,128]{1,0:T(4,128)S(1)} %compare_convert_fusion.2, f32[4,3,3,128]{1,2,3,0:T(4,128)S(1)} %copy.187, f32[4,3,3,128]{2,1,3,0:T(4,128)S(1)} %copy.184), kind=kOutput, calls=%fused_computation.35.clone.1 | convolution fusion | flops 178176 | bytes 69632 | tf_op jit(solution)/shard_map/while/body/eval_jaxpr/vmap(aci,cbi->abi)/dot_general | solution.py:56
  246.0 4.2 fusion.82
  256.8 5.8 %fusion.73 = f32[4,1,3,128,1]{3,1,4,2,0:T(1,128)S(1)} fusion(f32[4,8,128,128]{3,2,1,0:T(8,128)S(1)} %multiply_multiply_fusion.2, f32[4,3,8,128]{3,1,2,0:T(4,128)S(1)} %slice_bitcast_fusion.9, f32[4,3,128]{2,1,0:T(4,128)S(1)} %get-tuple-element.241, f32[4,8,7,128]{3,2,1,0:T(8,128)S(1)} %dynamic-slice_bitcast_fusion.6), kind=kOutput, calls=%fused_computation.34.clone.1 | convolution fusion | flops 22020096 | bytes 2193408 | tf_op jit(solution)/shard_map/while/body/eval_jaxpr/vmap(ckij,kj->ci)/dot_general | solution.py:48
  263.3 5.3 %fusion.75 = f32[4,3,3,128]{3,1,2,0:T(4,128)S(1)} fusion(f32[4,8,128,128]{3,2,1,0:T(8,128)S(1)} %multiply_multiply_fusion.2, f32[4,3,8,128]{3,1,2,0:T(4,128)S(1)} %slice_bitcast_fusion.9, f32[4,3,128]{2,1,0:T(4,128)S(1)} %get-tuple-element.241, f32[4,8,7,128]{3,2,1,0:T(8,128)S(1)} %dynamic-slice_bitcast_fusion.6, f32[4,8,128]{2,1,0:T(8,128)S(1)} %bitcast.212, ...), kind=kOutput, calls=%fused_computation.33.clone.1 | convolution fusion | flops 59794944 | bytes 2289664 | tf_op jit(solution)/shard_map/while/body/eval_jaxpr/vmap(ckij,kaj->aci)/dot_general | solution.py:49
  269.1 4.3 fusion.76
  276.4 5.2 %multiply_reduce_fusion.2 = (f32[4,128,3]{2,1,0:T(8,128)S(1)}, f32[4,128,3,3]{3,2,1,0:T(4,128)S(1)}) fusion(f32[4,128,3]{2,1,0:T(8,128)} %copy.183, f32[4,128]{1,0:T(4,128)S(1)} %compare_convert_fusion.2, f32[4,3,3,128]{1,2,3,0:T(4,128)S(1)} %copy.187, f32[4,3,3,128]{2,1,3,0:T(4,128)S(1)} %copy.184), kind=kOutput, calls=%fused_computation.35.clone.1 | convolution fusion | flops 178176 | bytes 69632 | tf_op jit(solution)/shard_map/while/body/eval_jaxpr/vmap(aci,cbi->abi)/dot_general | solution.py:56
  283.2 4.2 fusion.82
  294.1 5.8 %fusion.73 = f32[4,1,3,128,1]{3,1,4,2,0:T(1,128)S(1)} fusion(f32[4,8,128,128]{3,2,1,0:T(8,128)S(1)} %multiply_multiply_fusion.2, f32[4,3,8,128]{3,1,2,0:T(4,128)S(1)} %slice_bitcast_fusion.9, f32[4,3,128]{2,1,0:T(4,128)S(1)} %get-tuple-element.241, f32[4,8,7,128]{3,2,1,0:T(8,128)S(1)} %dynamic-slice_bitcast_fusion.6), kind=kOutput, calls=%fused_computation.34.clone.1 | convolution fusion | flops 22020096 | bytes 2193408 | tf_op jit(solution)/shard_map/while/body/eval_jaxpr/vmap(ckij,kj->ci)/dot_general | solution.py:48
  300.5 5.3 %fusion.75 = f32[4,3,3,128]{3,1,2,0:T(4,128)S(1)} fusion(f32[4,8,128,128]{3,2,1,0:T(8,128)S(1)} %multiply_multiply_fusion.2, f32[4,3,8,128]{3,1,2,0:T(4,128)S(1)} %slice_bitcast_fusion.9, f32[4,3,128]{2,1,0:T(4,128)S(1)} %get-tuple-element.241, f32[4,8,7,128]{3,2,1,0:T(8,128)S(1)} %dynamic-slice_bitcast_fusion.6, f32[4,8,128]{2,1,0:T(8,128)S(1)} %bitcast.212, ...), kind=kOutput, calls=%fused_computation.33.clone.1 | convolution fusion | flops 59794944 | bytes 2289664 | tf_op jit(solution)/shard_map/while/body/eval_jaxpr/vmap(ckij,kaj->aci)/dot_general | solution.py:49
  306.3 4.3 %fusion.76 = f32[4,128,3,3]{3,2,1,0:T(4,128)S(1)} fusion(f32[4,3,3,128]{2,1,3,0:T(4,128)S(1)} %copy.184), kind=kOutput, calls=%fused_computation.107.clone.1 | convolution fusion | flops 165888 | bytes 36864 | tf_op jit(solution)/shard_map/while/body/eval_jaxpr/vmap(cai,cbi->abi)/dot_general | solution.py:53
  313.6 5.2 %multiply_reduce_fusion.2 = (f32[4,128,3]{2,1,0:T(8,128)S(1)}, f32[4,128,3,3]{3,2,1,0:T(4,128)S(1)}) fusion(f32[4,128,3]{2,1,0:T(8,128)} %copy.183, f32[4,128]{1,0:T(4,128)S(1)} %compare_convert_fusion.2, f32[4,3,3,128]{1,2,3,0:T(4,128)S(1)} %copy.187, f32[4,3,3,128]{2,1,3,0:T(4,128)S(1)} %copy.184), kind=kOutput, calls=%fused_computation.35.clone.1 | convolution fusion | flops 178176 | bytes 69632 | tf_op jit(solution)/shard_map/while/body/eval_jaxpr/vmap(aci,cbi->abi)/dot_general | solution.py:56
  331.3 5.8 %fusion.73 = f32[4,1,3,128,1]{3,1,4,2,0:T(1,128)S(1)} fusion(f32[4,8,128,128]{3,2,1,0:T(8,128)S(1)} %multiply_multiply_fusion.2, f32[4,3,8,128]{3,1,2,0:T(4,128)S(1)} %slice_bitcast_fusion.9, f32[4,3,128]{2,1,0:T(4,128)S(1)} %get-tuple-element.241, f32[4,8,7,128]{3,2,1,0:T(8,128)S(1)} %dynamic-slice_bitcast_fusion.6), kind=kOutput, calls=%fused_computation.34.clone.1 | convolution fusion | flops 22020096 | bytes 2193408 | tf_op jit(solution)/shard_map/while/body/eval_jaxpr/vmap(ckij,kj->ci)/dot_general | solution.py:48
  337.8 5.3 %fusion.75 = f32[4,3,3,128]{3,1,2,0:T(4,128)S(1)} fusion(f32[4,8,128,128]{3,2,1,0:T(8,128)S(1)} %multiply_multiply_fusion.2, f32[4,3,8,128]{3,1,2,0:T(4,128)S(1)} %slice_bitcast_fusion.9, f32[4,3,128]{2,1,0:T(4,128)S(1)} %get-tuple-element.241, f32[4,8,7,128]{3,2,1,0:T(8,128)S(1)} %dynamic-slice_bitcast_fusion.6, f32[4,8,128]{2,1,0:T(8,128)S(1)} %bitcast.212, ...), kind=kOutput, calls=%fused_computation.33.clone.1 | convolution fusion | flops 59794944 | bytes 2289664 | tf_op jit(solution)/shard_map/while/body/eval_jaxpr/vmap(ckij,kaj->aci)/dot_general | solution.py:49
  343.5 4.3 fusion.76
  350.8 5.2 %multiply_reduce_fusion.2 = (f32[4,128,3]{2,1,0:T(8,128)S(1)}, f32[4,128,3,3]{3,2,1,0:T(4,128)S(1)}) fusion(f32[4,128,3]{2,1,0:T(8,128)} %copy.183, f32[4,128]{1,0:T(4,128)S(1)} %compare_convert_fusion.2, f32[4,3,3,128]{1,2,3,0:T(4,128)S(1)} %copy.187, f32[4,3,3,128]{2,1,3,0:T(4,128)S(1)} %copy.184), kind=kOutput, calls=%fused_computation.35.clone.1 | convolution fusion | flops 178176 | bytes 69632 | tf_op jit(solution)/shard_map/while/body/eval_jaxpr/vmap(aci,cbi->abi)/dot_general | solution.py:56
  357.6 4.2 fusion.82
  365.8 16.4 %scatter_fusion = f32[512,3,128]{2,1,0:T(4,128)S(1)} fusion(f32[512,3,128]{2,1,0:T(4,128)S(1)} %broadcast_in_dim.85, s32[256]{0:T(256)} %bitcast.223, f32[256,3,128]{2,1,0:T(4,128)} %bitcast.54), kind=kCustom, calls=%fused_computation.4 | custom fusion | bytes 1180672 | tf_op jit(solution)/shard_map/scatter | solution.py:128
  383.3 5.3 %all-to-all-start.2 = ((f32[128,4,3,128]{3,1,2,0:T(4,128)}), f32[128,4,3,128]{3,1,2,0:T(4,128)S(1)}, u32[]{:S(2)}, u32[]{:S(2)}) async-start(f32[128,4,3,128]{3,1,2,0:T(4,128)} %copy.132), calls=%async_computation.2 | async-start | bytes 1572864 | tf_op jit(solution)/shard_map/all_to_all | solution.py:130
  388.9 16.1 %all-to-all-done.2 = f32[128,4,3,128]{3,1,2,0:T(4,128)S(1)} async-done(((f32[128,4,3,128]{3,1,2,0:T(4,128)}), f32[128,4,3,128]{3,1,2,0:T(4,128)S(1)}, u32[]{:S(2)}, u32[]{:S(2)}) %all-to-all-start.2) | async-done | bytes 786464 | tf_op jit(solution)/shard_map/all_to_all | solution.py:130
  407.1 17.3 %scatter_fusion.1 = f32[32,3,128]{2,1,0:T(4,128)S(1)} fusion(f32[32,3,128]{2,1,0:T(4,128)S(1)} %bitcast.199, s32[512]{0:T(512)S(1)} %copy-done.12, f32[512,3,128]{2,1,0:T(4,128)S(1)} %bitcast_select_fusion), kind=kCustom, calls=%fused_computation.5 | custom fusion | flops 196608 | bytes 2361344 | tf_op jit(solution)/shard_map/scatter-add | solution.py:142
  (420 shorter events, 139.1 us)
Async XLA Ops:
  3.4 38.4 %copy-start.13 = (s32[256,1]{0,1:T(1,128)}, s32[256,1]{0,1:T(1,128)S(1)}, u32[]{:S(2)}) copy-start(s32[256,1]{0,1:T(1,128)S(1)} %compare_select_fusion.1) | copy-start | bytes 3076
  5.5 21.0 %all-to-all-start = ((s32[128,1,4]{2,1,0:T(1,128)}), s32[128,1,4]{2,1,0:T(1,128)S(1)}, u32[]{:S(2)}, u32[]{:S(2)}) async-start(s32[128,1,4]{2,1,0:T(1,128)} %bitcast.44), calls=%async_computation | async-start | bytes 131072 | tf_op jit(solution)/shard_map/all_to_all | solution.py:100
  31.4 4.6 %copy-start.8 = (f32[32,3,128]{2,0,1:T(8,128)S(1)}, f32[32,3,128]{2,0,1:T(8,128)}, u32[]{:S(2)}) copy-start(f32[32,3,128]{2,0,1:T(8,128)} %param.11) | copy-start | bytes 147460
  31.4 4.6 %copy-start.9 = (f32[32,3,128]{2,0,1:T(8,128)S(1)}, f32[32,3,128]{2,0,1:T(8,128)}, u32[]{:S(2)}) copy-start(f32[32,3,128]{2,0,1:T(8,128)} %param.10) | copy-start | bytes 147460
  31.4 4.6 %copy-start.10 = (f32[32,128]{1,0:T(8,128)S(1)}, f32[32,128]{1,0:T(8,128)}, u32[]{:S(2)}) copy-start(f32[32,128]{1,0:T(8,128)} %param.12) | copy-start | bytes 49156
  31.4 10.2 %copy-start.14 = (s32[32,2]{0,1:T(2,128)S(1)}, s32[32,2]{0,1:T(2,128)}, u32[]{:S(2)}) copy-start(s32[32,2]{0,1:T(2,128)} %param.17) | copy-start | bytes 772
  31.4 31.4 %all-to-all-start.1 = ((f32[128,4,7,128]{3,1,2,0:T(4,128)}), f32[128,4,7,128]{3,1,2,0:T(4,128)S(1)}, u32[]{:S(2)}, u32[]{:S(2)}) async-start(f32[128,4,7,128]{3,1,2,0:T(4,128)} %copy.124), calls=%async_computation.1 | async-start | bytes 3670016 | tf_op jit(solution)/shard_map/all_to_all | solution.py:104
  36.1 18.3 %collective-permute-start = (f32[4,4,128]{2,0,1:T(4,128)S(1)}, f32[4,4,128]{2,0,1:T(4,128)S(1)}, u32[]{:S(2)}, u32[]{:S(2)}) collective-permute-start(f32[4,4,128]{2,0,1:T(4,128)S(1)} %get-tuple-element.177), channel_id=1, source_target_pairs={{0,16},{16,32},{32,48},{48,64},{64,80},{80,96},{96,112},{1,17},{17... | collective-permute-start | bytes 24584 | tf_op jit(solution)/shard_map/ppermute | solution.py:26
  39.7 18.0 %collective-permute-start.1 = (f32[4,4,128]{2,0,1:T(4,128)S(1)}, f32[4,4,128]{2,0,1:T(4,128)S(1)}, u32[]{:S(2)}, u32[]{:S(2)}) collective-permute-start(f32[4,4,128]{2,0,1:T(4,128)S(1)} %get-tuple-element.178), channel_id=1, source_target_pairs={{16,0},{32,16},{48,32},{64,48},{80,64},{96,80},{112,96},{17,1},{33... | collective-permute-start | bytes 24584 | tf_op jit(solution)/shard_map/ppermute | solution.py:28
  70.7 6.5 %copy-start = (f32[4,8,128,128]{3,2,1,0:T(8,128)}, f32[4,8,128,128]{3,2,1,0:T(8,128)S(1)}, u32[]{:S(2)}) copy-start(f32[4,8,128,128]{3,2,1,0:T(8,128)S(1)} %multiply_multiply_fusion.2) | copy-start | bytes 6291460 | tf_op jit(solution)/shard_map/while
  90.3 5.2 %copy-start.2 = (f32[4,1,128]{2,1,0:T(1,128)}, f32[4,1,128]{2,1,0:T(1,128)S(1)}, u32[]{:S(2)}) copy-start(f32[4,1,128]{2,1,0:T(1,128)S(1)} %get-tuple-element.242) | copy-start | bytes 6148 | tf_op jit(solution)/shard_map/while
  90.3 5.8 %copy-start.6 = (f32[4,8,1,128]{3,2,1,0:T(1,128)S(1)}, f32[4,8,1,128]{3,2,1,0:T(1,128)}, u32[]{:S(2)}) copy-start(f32[4,8,1,128]{3,2,1,0:T(1,128)} %get-tuple-element.251) | copy-start | bytes 49156 | tf_op jit(solution)/shard_map/while
  101.3 2.8 copy-start.3
  101.3 2.8 copy-start.7
  107.9 6.5 %copy-start = (f32[4,8,128,128]{3,2,1,0:T(8,128)}, f32[4,8,128,128]{3,2,1,0:T(8,128)S(1)}, u32[]{:S(2)}) copy-start(f32[4,8,128,128]{3,2,1,0:T(8,128)S(1)} %multiply_multiply_fusion.2) | copy-start | bytes 6291460 | tf_op jit(solution)/shard_map/while
  127.5 5.2 %copy-start.2 = (f32[4,1,128]{2,1,0:T(1,128)}, f32[4,1,128]{2,1,0:T(1,128)S(1)}, u32[]{:S(2)}) copy-start(f32[4,1,128]{2,1,0:T(1,128)S(1)} %get-tuple-element.242) | copy-start | bytes 6148 | tf_op jit(solution)/shard_map/while
  127.5 5.8 %copy-start.6 = (f32[4,8,1,128]{3,2,1,0:T(1,128)S(1)}, f32[4,8,1,128]{3,2,1,0:T(1,128)}, u32[]{:S(2)}) copy-start(f32[4,8,1,128]{3,2,1,0:T(1,128)} %get-tuple-element.251) | copy-start | bytes 49156 | tf_op jit(solution)/shard_map/while
  138.5 2.8 copy-start.3
  138.5 2.8 copy-start.7
  145.1 6.5 %copy-start = (f32[4,8,128,128]{3,2,1,0:T(8,128)}, f32[4,8,128,128]{3,2,1,0:T(8,128)S(1)}, u32[]{:S(2)}) copy-start(f32[4,8,128,128]{3,2,1,0:T(8,128)S(1)} %multiply_multiply_fusion.2) | copy-start | bytes 6291460 | tf_op jit(solution)/shard_map/while
  164.7 5.2 %copy-start.2 = (f32[4,1,128]{2,1,0:T(1,128)}, f32[4,1,128]{2,1,0:T(1,128)S(1)}, u32[]{:S(2)}) copy-start(f32[4,1,128]{2,1,0:T(1,128)S(1)} %get-tuple-element.242) | copy-start | bytes 6148 | tf_op jit(solution)/shard_map/while
  164.7 5.8 %copy-start.6 = (f32[4,8,1,128]{3,2,1,0:T(1,128)S(1)}, f32[4,8,1,128]{3,2,1,0:T(1,128)}, u32[]{:S(2)}) copy-start(f32[4,8,1,128]{3,2,1,0:T(1,128)} %get-tuple-element.251) | copy-start | bytes 49156 | tf_op jit(solution)/shard_map/while
  175.8 2.8 copy-start.7
  182.4 6.5 %copy-start = (f32[4,8,128,128]{3,2,1,0:T(8,128)}, f32[4,8,128,128]{3,2,1,0:T(8,128)S(1)}, u32[]{:S(2)}) copy-start(f32[4,8,128,128]{3,2,1,0:T(8,128)S(1)} %multiply_multiply_fusion.2) | copy-start | bytes 6291460 | tf_op jit(solution)/shard_map/while
  201.9 5.2 %copy-start.2 = (f32[4,1,128]{2,1,0:T(1,128)}, f32[4,1,128]{2,1,0:T(1,128)S(1)}, u32[]{:S(2)}) copy-start(f32[4,1,128]{2,1,0:T(1,128)S(1)} %get-tuple-element.242) | copy-start | bytes 6148 | tf_op jit(solution)/shard_map/while
  201.9 5.8 %copy-start.6 = (f32[4,8,1,128]{3,2,1,0:T(1,128)S(1)}, f32[4,8,1,128]{3,2,1,0:T(1,128)}, u32[]{:S(2)}) copy-start(f32[4,8,1,128]{3,2,1,0:T(1,128)} %get-tuple-element.251) | copy-start | bytes 49156 | tf_op jit(solution)/shard_map/while
  213.0 2.8 copy-start.7
  219.6 6.5 %copy-start = (f32[4,8,128,128]{3,2,1,0:T(8,128)}, f32[4,8,128,128]{3,2,1,0:T(8,128)S(1)}, u32[]{:S(2)}) copy-start(f32[4,8,128,128]{3,2,1,0:T(8,128)S(1)} %multiply_multiply_fusion.2) | copy-start | bytes 6291460 | tf_op jit(solution)/shard_map/while
  239.2 5.2 %copy-start.2 = (f32[4,1,128]{2,1,0:T(1,128)}, f32[4,1,128]{2,1,0:T(1,128)S(1)}, u32[]{:S(2)}) copy-start(f32[4,1,128]{2,1,0:T(1,128)S(1)} %get-tuple-element.242) | copy-start | bytes 6148 | tf_op jit(solution)/shard_map/while
  239.2 5.8 %copy-start.6 = (f32[4,8,1,128]{3,2,1,0:T(1,128)S(1)}, f32[4,8,1,128]{3,2,1,0:T(1,128)}, u32[]{:S(2)}) copy-start(f32[4,8,1,128]{3,2,1,0:T(1,128)} %get-tuple-element.251) | copy-start | bytes 49156 | tf_op jit(solution)/shard_map/while
  250.2 2.8 copy-start.3
  250.2 2.8 copy-start.7
  256.8 6.5 %copy-start = (f32[4,8,128,128]{3,2,1,0:T(8,128)}, f32[4,8,128,128]{3,2,1,0:T(8,128)S(1)}, u32[]{:S(2)}) copy-start(f32[4,8,128,128]{3,2,1,0:T(8,128)S(1)} %multiply_multiply_fusion.2) | copy-start | bytes 6291460 | tf_op jit(solution)/shard_map/while
  276.4 5.2 %copy-start.2 = (f32[4,1,128]{2,1,0:T(1,128)}, f32[4,1,128]{2,1,0:T(1,128)S(1)}, u32[]{:S(2)}) copy-start(f32[4,1,128]{2,1,0:T(1,128)S(1)} %get-tuple-element.242) | copy-start | bytes 6148 | tf_op jit(solution)/shard_map/while
  276.4 5.8 %copy-start.6 = (f32[4,8,1,128]{3,2,1,0:T(1,128)S(1)}, f32[4,8,1,128]{3,2,1,0:T(1,128)}, u32[]{:S(2)}) copy-start(f32[4,8,1,128]{3,2,1,0:T(1,128)} %get-tuple-element.251) | copy-start | bytes 49156 | tf_op jit(solution)/shard_map/while
  287.5 2.8 copy-start.7
  294.0 6.5 %copy-start = (f32[4,8,128,128]{3,2,1,0:T(8,128)}, f32[4,8,128,128]{3,2,1,0:T(8,128)S(1)}, u32[]{:S(2)}) copy-start(f32[4,8,128,128]{3,2,1,0:T(8,128)S(1)} %multiply_multiply_fusion.2) | copy-start | bytes 6291460 | tf_op jit(solution)/shard_map/while
  313.6 5.2 %copy-start.2 = (f32[4,1,128]{2,1,0:T(1,128)}, f32[4,1,128]{2,1,0:T(1,128)S(1)}, u32[]{:S(2)}) copy-start(f32[4,1,128]{2,1,0:T(1,128)S(1)} %get-tuple-element.242) | copy-start | bytes 6148 | tf_op jit(solution)/shard_map/while
  313.6 5.8 %copy-start.6 = (f32[4,8,1,128]{3,2,1,0:T(1,128)S(1)}, f32[4,8,1,128]{3,2,1,0:T(1,128)}, u32[]{:S(2)}) copy-start(f32[4,8,1,128]{3,2,1,0:T(1,128)} %get-tuple-element.251) | copy-start | bytes 49156 | tf_op jit(solution)/shard_map/while
  324.7 2.8 copy-start.3
  324.7 2.8 copy-start.7
  331.3 6.5 %copy-start = (f32[4,8,128,128]{3,2,1,0:T(8,128)}, f32[4,8,128,128]{3,2,1,0:T(8,128)S(1)}, u32[]{:S(2)}) copy-start(f32[4,8,128,128]{3,2,1,0:T(8,128)S(1)} %multiply_multiply_fusion.2) | copy-start | bytes 6291460 | tf_op jit(solution)/shard_map/while
  350.8 5.2 %copy-start.2 = (f32[4,1,128]{2,1,0:T(1,128)}, f32[4,1,128]{2,1,0:T(1,128)S(1)}, u32[]{:S(2)}) copy-start(f32[4,1,128]{2,1,0:T(1,128)S(1)} %get-tuple-element.242) | copy-start | bytes 6148 | tf_op jit(solution)/shard_map/while
  350.8 5.8 %copy-start.6 = (f32[4,8,1,128]{3,2,1,0:T(1,128)S(1)}, f32[4,8,1,128]{3,2,1,0:T(1,128)}, u32[]{:S(2)}) copy-start(f32[4,8,1,128]{3,2,1,0:T(1,128)} %get-tuple-element.251) | copy-start | bytes 49156 | tf_op jit(solution)/shard_map/while
  361.9 2.8 copy-start.7
  382.2 6.4 %copy-start.5 = (s32[128,1,4]{2,1,0:T(1,128)S(1)}, s32[128,1,4]{2,1,0:T(1,128)}, u32[]{:S(2)}) copy-start(s32[128,1,4]{2,1,0:T(1,128)} %copy-done.4) | copy-start | bytes 6148
  383.3 21.8 %all-to-all-start.2 = ((f32[128,4,3,128]{3,1,2,0:T(4,128)}), f32[128,4,3,128]{3,1,2,0:T(4,128)S(1)}, u32[]{:S(2)}, u32[]{:S(2)}) async-start(f32[128,4,3,128]{3,1,2,0:T(4,128)} %copy.132), calls=%async_computation.2 | async-start | bytes 1572864 | tf_op jit(solution)/shard_map/all_to_all | solution.py:130
  388.6 18.5 %copy-start.12 = (s32[512]{0:T(512)S(1)}, s32[512]{0:T(512)}, u32[]{:S(2)}) copy-start(s32[512]{0:T(512)} %copy-done.11) | copy-start | bytes 6148
  (14 other events, 25.1 us)
where the time goes:
time: 428 us; the launch traced here: 425 us
  matrix products  212 us (50%)
  local copies, waits for them, and re-layouts  92.3 us (22%)
  other arithmetic  51.2 us (12%)
  waiting for transfers between devices  41.4 us (10%)
  starting transfers between devices  26.8 us (6%)
    dot_general x8, matrix products, block_terms(): column = jnp.einsum('ckij,kj->ci', slope, far_weight, precision=highest)  46.7 us
    dot_general x8, matrix products, block_terms(): jnp.einsum('ckij,kaj->aci', slope, far_weight[:, None, :] * neighbours[:,...  42.7 us
    dot_general x8, matrix products, block_terms(): jnp.einsum('aci,cbi->abi', deform, second, precision=highest) * inside  41.6 us
    dot_general x8, matrix products, block_terms(): jnp.einsum('cai,cbi->abi', deform, deform, precision=highest) - identity  34 us
    dot_general x8, matrix products, block_terms(): jnp.einsum('bkij,abi->kaj', slope, weight * piola, precision=highest)  33.9 us
    squeeze x24, local copies, waits for them, and re-layouts, per_device(): lax.map(group_terms, (split_up(packed), split_up(lame), split_up(neighbou...  19 us
    scatter-add x1, other arithmetic, per_device(): returned = jnp.zeros_like(forces).at[jnp.maximum(flat_ids, 0)].add(jnp.wh...  17.3 us
    scatter x1, local copies, waits for them, and re-layouts, per_device(): outgoing = jnp.zeros((devices * capacity, 3, block_len), jnp.float32).at[...  16.4 us
  transfers between devices with their start and end apart: 5, of which 5 were waited for; matrix products, arithmetic and copies ran while one was open for 1% of the time, Pallas kernels for 0%

commit v1 on v0

v1 whole, which is shorter than its diff:
```python
import functools
import math

import jax
import jax.numpy as jnp
from jax import lax
from jax.experimental import pallas as pl
from jax.experimental.pallas import tpu as pltpu
from jax.sharding import PartitionSpec as P

SH = 4
SUPPORT_SQ = 0.5
CONTACT_SQ = 0.1
PENALTY = 200.0
GROUP = 8
ROWS = 7
F32 = jnp.float32
BF16 = jnp.bfloat16
AXES = ("gx", "yz")
NT = (((1,), (1,)), ((), ()))
NN = (((1,), (0,)), ((), ()))


def high(x):
    return x.astype(BF16).astype(F32)


def parts(x, count):
    out = []
    for _ in range(count - 1):
        h = high(x)
        out.append(h)
        x = x - h
    out.append(high(x))
    return out


def mm(a, b, dims):
    return lax.dot_general(a, b, dims, preferred_element_type=F32)


def contact_kernel(pos_ref, disp_ref, mask_ref, shell_ref, pick_ref, out_ref, wide, cur):
    blocks, lanes = mask_ref.shape
    count = shell_ref.shape[0]
    for c in range(3):
        cur[c] = pos_ref[c] + disp_ref[c]
    for s in range(count):
        turned = jnp.transpose(jnp.concatenate([shell_ref[s], shell_ref[s]], axis=0))
        for c in range(4):
            wide[s, c] = jnp.broadcast_to(turned[:, c : c + 1], (lanes, lanes))

    def block(b, _):
        own = [jnp.broadcast_to(cur[c, pl.ds(b, 1), :], (8, lanes)) for c in range(3)]
        total = [jnp.zeros((8, lanes), F32) for _ in range(3)]
        for k in range(2):
            s = pick_ref[b, k]
            for r in range(lanes // 8):
                rows = pl.ds(r * 8, 8)
                gap = [own[c] - wide[s, c, rows, :] for c in range(3)]
                near = jnp.maximum(
                    CONTACT_SQ - (gap[0] * gap[0] + gap[1] * gap[1] + gap[2] * gap[2]), 0.0
                )
                push = near * near * wide[s, 3, rows, :]
                total = [total[c] + push * gap[c] for c in range(3)]
        scale = PENALTY * mask_ref[pl.ds(b, 1), :]
        for c in range(3):
            out_ref[c, pl.ds(b, 1), :] = scale * jnp.sum(total[c], axis=0, keepdims=True)
        return 0

    lax.fori_loop(0, blocks, block, 0)


def main_kernel(
    slot_ref, pos_ref, disp_ref, weight_ref, lame_ref, contact_ref, got_ref,
    piola_ref, force_ref, back_ref,
    pick, far, bs, fs, a_s, at, b_all, f_all, k_hi, k_lo, ss, gs, ts,
):
    blocks, lanes = weight_ref.shape
    fanout = far.shape[2]
    wide = fanout * lanes
    coeff = -3.0 / math.sqrt(wide)
    inv = 1.0 / SUPPORT_SQ
    back_ref[...] = jnp.zeros_like(back_ref)
    ones = jnp.ones((8, lanes), F32)
    zero = jnp.zeros((8, lanes), F32)
    for f in range(21, 32):
        bs[pl.ds(f, 8, stride=32), :] = ones if f < 24 else zero
    for f in range(18, 32):
        a_s[pl.ds(f, 8, stride=32), :] = ones if f < 21 else zero
    for f in range(12, 32):
        if f < 16 or f >= 28:
            gs[pl.ds(f, 8, stride=32), :] = zero

    def own_side(g, _):
        start = pl.multiple_of(g * GROUP, GROUP)
        rows = pl.ds(start, GROUP)
        near = [pos_ref[c, rows, :] for c in range(3)]
        near = [x - x[:, 0:1] for x in near]
        norm = near[0] * near[0] + near[1] * near[1] + near[2] * near[2]
        for c in range(3):
            h, m, l = [2.0 * inv * p for p in parts(near[c], 3)]
            for f, v in ((0, h), (3, h), (6, m), (9, m), (12, h), (15, l)):
                a_s[pl.ds(f + c, 8, stride=32), :] = v
        for f, v in enumerate(parts(1.0 - inv * norm, 3)):
            a_s[pl.ds(21 + f, 8, stride=32), :] = v
        for q in range(GROUP):
            at[start + q] = jnp.transpose(a_s[pl.ds(q * 32, 32), :]).astype(BF16)
        return 0

    lax.fori_loop(0, blocks // GROUP, own_side, 0)

    def far_side(b, _):
        for k in range(fanout):
            first = slot_ref[b * fanout + k] * ROWS
            for c in range(ROWS):
                pick[c, pl.ds(k, 1), :] = got_ref[pl.ds(first + c, 1), :]
        there = [pick[c] - pos_ref[c, pl.ds(b, 1), 0:1] for c in range(3)]
        moved = [pick[3 + c] for c in range(3)]
        weight = pick[6]
        for c in range(3):
            far[b, c] = there[c]
        far[b, 3] = weight
        norm = there[0] * there[0] + there[1] * there[1] + there[2] * there[2]
        for c in range(3):
            h, m, l = parts(there[c], 3)
            for f, v in ((0, h), (3, m), (6, h), (9, m), (12, l), (15, h)):
                bs[pl.ds(f + c, 8, stride=32), :] = v
        for f, v in enumerate(parts(-inv * norm, 3)):
            bs[pl.ds(18 + f, 8, stride=32), :] = v
        heavy = [weight * x for x in moved]
        feats = [weight] + [weight * x for x in there] + heavy
        feats += [h * x for h in heavy for x in there]
        for f, v in enumerate(feats):
            h, l = parts(v, 2)
            fs[pl.ds(f, 8, stride=32), :] = h
            fs[pl.ds(16 + f, 8, stride=32), :] = l
        for k in range(fanout):
            cols = pl.ds(k * lanes, lanes)
            b_all[b, :, cols] = bs[pl.ds(k * 32, 32), :].astype(BF16)
            f_all[b, :, cols] = fs[pl.ds(k * 32, 32), :].astype(BF16)
        return 0

    lax.fori_loop(0, blocks, far_side, 0)

    def group(g, _):
        start = pl.multiple_of(g * GROUP, GROUP)
        rows = pl.ds(start, GROUP)

        def forward(q, _):
            b = start + q
            near = jnp.maximum(mm(at[b], b_all[b], NN), 0.0)
            near = near * near
            hi = near.astype(BF16)
            lo = (near - hi.astype(F32)).astype(BF16)
            k_hi[q] = hi
            k_lo[q] = lo
            sums = mm(f_all[b], hi, NT)
            sums = sums[0:16] + sums[16:32] + mm(f_all[b, 0:16, :], lo, NT)
            ss[pl.ds(pl.multiple_of(q * 16, 16), 16), :] = sums
            return 0

        lax.fori_loop(0, GROUP, forward, 0, unroll=2)

        total = [ss[pl.ds(f, GROUP, stride=16), :] for f in range(16)]
        weight = weight_ref[rows, :]
        inside = (weight > 0).astype(F32)
        here = [pos_ref[c, rows, :] for c in range(3)]
        here = [x - x[:, 0:1] for x in here]
        moved = [disp_ref[c, rows, :] for c in range(3)]
        column = [coeff * (here[c] * total[0] - total[1 + c]) for c in range(3)]
        deform = [
            [
                (1.0 if a == c else 0.0)
                + coeff * (here[c] * total[4 + a] - total[7 + 3 * a + c])
                - moved[a] * column[c]
                for c in range(3)
            ]
            for a in range(3)
        ]
        strain = [[None] * 3 for _ in range(3)]
        for a in range(3):
            for c in range(a, 3):
                v = sum(deform[k][a] * deform[k][c] for k in range(3))
                strain[a][c] = strain[c][a] = 0.5 * (v - (1.0 if a == c else 0.0))
        trace = lame_ref[0, rows, :] * (strain[0][0] + strain[1][1] + strain[2][2])
        twice = 2.0 * lame_ref[1, rows, :]
        second = [
            [(trace if a == c else 0.0) + twice * strain[a][c] for c in range(3)] for a in range(3)
        ]
        scaled = [[None] * 3 for _ in range(3)]
        for a in range(3):
            for c in range(3):
                v = sum(deform[a][k] * second[k][c] for k in range(3)) * inside
                piola_ref[3 * a + c, rows, :] = v
                scaled[a][c] = weight * v
        feats = [scaled[a][c] for a in range(3) for c in range(3)]
        for a in range(3):
            own = sum(scaled[a][c] * column[c] for c in range(3))
            force_ref[a, rows, :] = own + contact_ref[a, rows, :]
            feats.append(sum(scaled[a][c] * here[c] for c in range(3)))
        for f, v in enumerate(feats):
            h, l = parts(v, 2)
            gs[pl.ds(f, 8, stride=32), :] = h
            gs[pl.ds(16 + f, 8, stride=32), :] = l

        def backward(q, _):
            b = start + q
            feat = gs[pl.ds(pl.multiple_of(q * 32, 32), 32), :].astype(BF16)
            sums = mm(feat, k_hi[q], NN)
            sums = sums[0:16] + sums[16:32] + mm(feat[0:16], k_lo[q], NN)
            for k in range(fanout):
                ts[pl.ds(k * 16, 16), :] = sums[:, k * lanes : (k + 1) * lanes]
            back = [ts[pl.ds(f, fanout, stride=16), :] for f in range(12)]
            there = [far[b, c] for c in range(3)]
            scale = -coeff * far[b, 3]
            for a in range(3):
                v = back[9 + a] - sum(there[c] * back[3 * a + c] for c in range(3))
                pick[a] = scale * v
            for k in range(fanout):
                first = slot_ref[b * fanout + k] * 3
                for a in range(3):
                    back_ref[pl.ds(first + a, 1), :] = pick[a, pl.ds(k, 1), :]
            return 0

        lax.fori_loop(0, GROUP, backward, 0)
        return 0

    lax.fori_loop(0, blocks // GROUP, group, 0)


def gather_sum_kernel(code_ref, got_ref, force_ref, out_ref):
    comps, blocks, lanes = force_ref.shape
    rows = got_ref.shape[0]
    target = lax.broadcasted_iota(jnp.int32, (comps * blocks, rows), 0)
    chosen = (target == code_ref[...]).astype(F32).astype(BF16)
    out = force_ref[...].reshape(comps * blocks, lanes)
    for part in parts(got_ref[...], 3):
        out = out + mm(chosen, part.astype(BF16), NN)
    out_ref[...] = out.reshape(comps, blocks, lanes)


def vmem(count):
    return [pl.BlockSpec(memory_space=pltpu.VMEM)] * count


SMEM = pl.BlockSpec(memory_space=pltpu.SMEM)


def per_device(ref_pos, disp, volume, lame, pad_count, nbr_owner, nbr_local, contact_block):
    blocks, _, lanes = ref_pos.shape
    fanout = nbr_local.shape[1]
    across = lax.axis_size("gx")
    deep = lax.axis_size("yz")
    devices = across * deep
    cap = 2 * blocks * fanout // devices
    slots_all = devices * cap
    usable = (jnp.arange(lanes)[None, :] < (lanes - pad_count)[:, None]).astype(F32)
    weight = volume * usable
    mask = (weight > 0).astype(F32)

    owners = nbr_owner[:, :, 0].reshape(-1)
    wanted = nbr_local.reshape(-1)
    position = jnp.arange(owners.shape[0])
    before = (owners[:, None] == owners[None, :]) & (position[:, None] > position[None, :])
    slots = owners * cap + jnp.sum(before.astype(jnp.int32), axis=1)
    requests = jnp.full((slots_all,), -1, jnp.int32).at[slots].set(wanted)
    slot_ids = lax.all_to_all(
        requests.reshape(devices, cap), AXES, split_axis=0, concat_axis=0, tiled=True
    )

    packed = jnp.concatenate([ref_pos, disp, weight[:, None, :]], axis=1)
    picked = packed[jnp.maximum(slot_ids, 0)].reshape(devices, ROWS, cap, lanes)
    got = lax.all_to_all(picked, AXES, split_axis=0, concat_axis=0, tiled=True)
    got = got.reshape(slots_all * ROWS, lanes)

    surface = jnp.concatenate([ref_pos + disp, weight[:, None, :]], axis=1)
    up = [(i, i + 1) for i in range(across - 1)]
    down = [(i + 1, i) for i in range(across - 1)]
    below = lax.ppermute(surface[blocks - SH :], "gx", up)
    above = lax.ppermute(surface[:SH], "gx", down)
    shell = jnp.concatenate([below, above], axis=0)
    local = contact_block % blocks
    row = contact_block // blocks // deep
    pick = jnp.where(row < lax.axis_index("gx"), local - (blocks - SH), SH + local)

    pos_t = jnp.transpose(ref_pos, (1, 0, 2))
    disp_t = jnp.transpose(disp, (1, 0, 2))
    lame_t = jnp.transpose(lame, (1, 0, 2))
    contact = pl.pallas_call(
        contact_kernel,
        out_shape=jax.ShapeDtypeStruct((3, blocks, lanes), F32),
        in_specs=vmem(4) + [SMEM],
        out_specs=vmem(1)[0],
        scratch_shapes=[
            pltpu.VMEM((2 * SH, 4, lanes, lanes), F32),
            pltpu.VMEM((3, blocks, lanes), F32),
        ],
        cost_estimate=pl.CostEstimate(flops=20_000_000, bytes_accessed=200_000, transcendentals=0),
        name="contact",
    )(pos_t, disp_t, mask, shell, pick)

    wide = fanout * lanes
    piola, force, back = pl.pallas_call(
        main_kernel,
        out_shape=(
            jax.ShapeDtypeStruct((9, blocks, lanes), F32),
            jax.ShapeDtypeStruct((3, blocks, lanes), F32),
            jax.ShapeDtypeStruct((slots_all * 3, lanes), F32),
        ),
        in_specs=[SMEM] + vmem(6),
        out_specs=tuple(vmem(3)),
        scratch_shapes=[
            pltpu.VMEM((8, fanout, lanes), F32),
            pltpu.VMEM((blocks, 4, fanout, lanes), F32),
            pltpu.VMEM((fanout * 32, lanes), F32),
            pltpu.VMEM((fanout * 32, lanes), F32),
            pltpu.VMEM((GROUP * 32, lanes), F32),
            pltpu.VMEM((blocks, lanes, 32), BF16),
            pltpu.VMEM((blocks, 32, wide), BF16),
            pltpu.VMEM((blocks, 32, wide), BF16),
            pltpu.VMEM((GROUP, lanes, wide), BF16),
            pltpu.VMEM((GROUP, lanes, wide), BF16),
            pltpu.VMEM((GROUP * 16, lanes), F32),
            pltpu.VMEM((GROUP * 32, lanes), F32),
            pltpu.VMEM((fanout * 16, lanes), F32),
        ],
        cost_estimate=pl.CostEstimate(
            flops=60_000_000, bytes_accessed=4_000_000, transcendentals=0
        ),
        name="pairs",
    )(slots, pos_t, disp_t, weight, lame_t, contact, got)

    received = lax.all_to_all(
        back.reshape(devices, 3, cap, lanes), AXES, split_axis=0, concat_axis=0, tiled=True
    )
    ids = slot_ids.reshape(-1, 1)
    code = jnp.where(ids >= 0, ids + blocks * jnp.arange(3)[None, :], -1).reshape(1, -1)
    force = pl.pallas_call(
        gather_sum_kernel,
        out_shape=jax.ShapeDtypeStruct((3, blocks, lanes), F32),
        in_specs=vmem(3),
        out_specs=vmem(1)[0],
        name="returned",
    )(code, received.reshape(slots_all * 3, lanes), force)
    return (jnp.transpose(force, (1, 0, 2)), jnp.transpose(piola, (1, 0, 2)))


def solution(mesh):
    return jax.shard_map(
        per_device,
        mesh=mesh,
        in_specs=(
            P(AXES, None, None),
            P(AXES, None, None),
            P(AXES, None),
            P(AXES, None, None),
            P(AXES),
            P(AXES, None, None),
            P(AXES, None),
            P(AXES, None),
        ),
        out_specs=(P(AXES, None, None), P(AXES, None, None)),
        check_vma=False,
    )
```

time: 428 us -> 122 us (0.29)
  matrix products: 212 us -> 0 us
  local copies, waits for them, and re-layouts: 92.3 us -> 13.9 us
  other arithmetic: 51.2 us -> 5.99 us
  Pallas kernels: 0 us -> 35 us
  waiting for transfers between devices: 41.4 us -> 35.3 us
    dot_general x48 -> x0, matrix products: 212 us -> none  [the longest x8 46.7 us: block_terms(): column = jnp.einsum('ckij,kj->ci', slope, far_weight, precision=highest)]
    pallas_call x0 -> x3, Pallas kernels: none -> 35 us  [the longest x1 26.9 us: per_device(): pl.pallas_call(main_kernel, out_shape=(jax.ShapeDtypeStruct((9, blocks, l...]
    squeeze x24 -> x0, local copies, waits for them, and re-layouts: 19 us -> none  [per_device(): lax.map(group_terms, (split_up(packed), split_up(lame), split_up(neighbou...]
    scatter-add x1 -> x0, other arithmetic: 17.3 us -> none  [per_device(): returned = jnp.zeros_like(forces).at[jnp.maximum(flat_ids, 0)].add(jnp.wh...]
    scatter x2 -> x1, local copies, waits for them, and re-layouts: 17.8 us -> 1.4 us  [per_device(): requests = jnp.full((slots_all,), -1, jnp.int32).at[slots].set(wanted)]
    while x104 -> x0, local copies, waits for them, and re-layouts: 14.6 us -> none
    mul x42 -> x2, other arithmetic: 14.9 us -> 0.7 us  [the longest x1 0.69 us: per_device(): slots = owners * cap + jnp.sum(before.astype(jnp.int32), axis=1)]
    reduce_sum x17 -> x1, other arithmetic: 8.54 us -> 0.18 us  [per_device(): slots = owners * cap + jnp.sum(before.astype(jnp.int32), axis=1)]
  transfers between devices with their start and end apart: 5 -> 5, of which waited for: 5 -> 4; matrix products, arithmetic and copies ran while one was open for 1% -> 6% of each run, Pallas kernels for 0% -> 5%
where the time goes in v1:
time: 122 us
  waiting for transfers between devices  35.3 us (29%)
  Pallas kernels  35 us (29%)
  starting transfers between devices  30.6 us (25%)
  local copies, waits for them, and re-layouts  13.9 us (11%)
  other arithmetic  5.99 us (5%)
    pallas_call x1, Pallas kernels, per_device(): pl.pallas_call(main_kernel, out_shape=(jax.ShapeDtypeStruct((9, blocks, l...  26.9 us
    all_to_all x1, waiting for transfers between devices, per_device(): lax.all_to_all(back.reshape(devices, 3, cap, lanes), AXES, split_axis=0,...  15.3 us
    all_to_all x1, starting transfers between devices, per_device(): lax.all_to_all(requests.reshape(devices, cap), AXES, split_axis=0, concat...  11.5 us
    ppermute x1, waiting for transfers between devices, per_device(): below = lax.ppermute(surface[blocks - SH:], 'gx', up)  11 us
    all_to_all x1, starting transfers between devices, per_device(): lax.all_to_all(back.reshape(devices, 3, cap, lanes), AXES, split_axis=0,...  9.09 us
    unnamed x20, local copies, waits for them, and re-layouts  6.04 us
    pallas_call x1, Pallas kernels, per_device(): pl.pallas_call(contact_kernel, out_shape=jax.ShapeDtypeStruct((3, blocks,...  6 us
    all_to_all x1, waiting for transfers between devices, per_device(): lax.all_to_all(requests.reshape(devices, cap), AXES, split_axis=0, concat...  5.75 us
  transfers between devices with their start and end apart: 5, of which 4 were waited for; matrix products, arithmetic and copies ran while one was open for 6% of the time, Pallas kernels for 5%

profile of v1, /device:TPU:1, one launch (start us, length us, event | category | flops | bytes accessed | tf_op | source)
XLA Modules:
  0.0 121.6 jit_solution(10962276871721965009)
XLA Ops:
  0.6 0.7 broadcast_multiply_fusion
  1.3 0.8 copy.63
  2.1 0.1 copy.62
  2.2 0.1 mul.33
  2.2 0.8 copy.64
  3.0 0.1 reshape.139
  3.1 0.1 eq.17
  3.2 0.2 convert_reduce_fusion
  3.4 1.4 %scatter_custom_fusion = s32[512]{0:T(512)S(1)} fusion(s32[256]{0:T(256)S(1)} %bitcast.33, s32[256]{0:T(256)S(1)} %reshape.139, s32[]{:T(128)} %constant.52.clone.1), kind=kCustom, calls=%fused_computation.37 | custom fusion | bytes 2052 | tf_op jit(solution)/shard_map/scatter | solution.py:266
  4.8 0.7 all_to_all.12
  5.5 11.5 %all-to-all-start = ((s32[128,1,4]{2,1,0:T(1,128)}), s32[128,1,4]{2,1,0:T(1,128)S(1)}, u32[]{:S(2)}, u32[]{:S(2)}) async-start(s32[128,1,4]{2,1,0:T(1,128)} %bitcast.2), calls=%async_computation | async-start | bytes 131072 | tf_op jit(solution)/shard_map/all_to_all | solution.py:267
  17.0 0.7 broadcast_subtract_fusion
  17.7 0.8 copy.73
  18.5 0.8 copy.74
  19.4 1.4 %compare_convert_fusion = (f32[32,128]{1,0:T(8,128)}, f32[32,128]{1,0:T(8,128)S(1)}) fusion(f32[32,128]{1,0:T(8,128)} %param.10, s32[32]{0:T(128)S(1)} %broadcast_subtract_fusion), kind=kLoop, calls=%fused_computation.29 | loop fusion | flops 16384 | bytes 49280 | tf_op jit(solution)/shard_map/convert_element_type | solution.py:259
  20.8 0.0 copy-start.4
  20.8 5.8 %all-to-all-done = s32[128,1,4]{2,1,0:T(1,128)S(1)} async-done(((s32[128,1,4]{2,1,0:T(1,128)}), s32[128,1,4]{2,1,0:T(1,128)S(1)}, u32[]{:S(2)}, u32[]{:S(2)}) %all-to-all-start) | async-done | bytes 2080 | tf_op jit(solution)/shard_map/all_to_all | solution.py:267
  26.6 0.5 broadcast.108
  27.1 1.0 maximum_reduce_fusion
  28.1 0.1 reshape.129
  28.2 1.9 %gather_fusion = f32[512,7,128]{2,1,0:T(8,128)S(1)} fusion(f32[32,7,128]{2,1,0:T(8,128)S(1)} %pad_maximum_fusion, s32[1024]{0:T(1024)S(1)} %pad_clamp_fusion), kind=kCustom, calls=%fused_computation | custom fusion | bytes 3672064 | tf_op jit(solution)/shard_map/gather | solution.py:272
  30.1 1.9 %reshape.123 = f32[128,7,4,128]{3,2,1,0:T(4,128)} reshape(f32[512,7,128]{2,1,0:T(8,128)S(1)} %gather_fusion) | data formatting | bytes 3670016 | tf_op jit(solution)/shard_map/reshape | solution.py:272
  32.0 4.6 %all-to-all-start.1 = ((f32[128,7,4,128]{3,2,1,0:T(4,128)}), f32[128,7,4,128]{3,2,1,0:T(4,128)S(1)}, u32[]{:S(2)}, u32[]{:S(2)}) async-start(f32[128,7,4,128]{3,2,1,0:T(4,128)} %reshape.123), calls=%async_computation.1 | async-start | bytes 3670016 | tf_op jit(solution)/shard_map/all_to_all | solution.py:273
  36.5 0.0 copy-done.2
  36.6 0.0 copy-done.3
  36.6 0.0 copy-done.4
  36.7 3.5 %collective-permute-start = (f32[4,4,128]{2,1,0:T(4,128)S(1)}, f32[4,4,128]{2,1,0:T(4,128)S(1)}, u32[]{:S(2)}, u32[]{:S(2)}) collective-permute-start(f32[4,4,128]{2,1,0:T(4,128)S(1)} %get-tuple-element.12), channel_id=1, source_target_pairs={{0,16},{16,32},{32,48},{48,64},{64,80},{80,96},{96,112},{1,17},{17... | collective-permute-start | bytes 24584 | tf_op jit(solution)/shard_map/ppermute | solution.py:279
  40.2 1.9 %collective-permute-start.1 = (f32[4,4,128]{2,1,0:T(4,128)S(1)}, f32[4,4,128]{2,1,0:T(4,128)S(1)}, u32[]{:S(2)}, u32[]{:S(2)}) collective-permute-start(f32[4,4,128]{2,1,0:T(4,128)S(1)} %get-tuple-element.13), channel_id=1, source_target_pairs={{16,0},{32,16},{48,32},{64,48},{80,64},{96,80},{112,96},{17,1},{33... | collective-permute-start | bytes 24584 | tf_op jit(solution)/shard_map/ppermute | solution.py:280
  42.1 0.0 copy-done.6
  42.2 0.1 copy.69
  42.2 0.6 add_select_fusion.4.pick_ref
  42.9 0.5 multiply_add_fusion.slot_ref
  43.4 0.0 copy-done.5
  43.4 0.6 copy.77
  44.0 11.0 %collective-permute-done = f32[4,4,128]{2,1,0:T(4,128)S(1)} collective-permute-done((f32[4,4,128]{2,1,0:T(4,128)S(1)}, f32[4,4,128]{2,1,0:T(4,128)S(1)}, u32[]{:S(2)}, u32[]{:S(2)}) %collective-permute-start) | collective-permute-done | bytes 8224 | tf_op jit(solution)/shard_map/ppermute | solution.py:279
  55.0 3.3 %collective-permute-done.1 = f32[4,4,128]{2,1,0:T(4,128)S(1)} collective-permute-done((f32[4,4,128]{2,1,0:T(4,128)S(1)}, f32[4,4,128]{2,1,0:T(4,128)S(1)}, u32[]{:S(2)}, u32[]{:S(2)}) %collective-permute-start.1) | collective-permute-done | bytes 8224 | tf_op jit(solution)/shard_map/ppermute | solution.py:280
  58.2 0.6 pad_maximum_fusion.1.shell_ref
  58.9 6.0 %contact.1.contact_ref = f32[3,32,128]{2,1,0:T(8,128)} custom-call(f32[3,32,128]{2,1,0:T(8,128)} %bitcast.24, f32[3,32,128]{2,1,0:T(8,128)} %bitcast.26, f32[32,128]{1,0:T(8,128)} %get-tuple-element.10.mask_ref, f32[8,4,128]{2,1,0:T(4,128)} %pad_maximum_fusion.1.shell_ref, s32[32,2]{1,0:T(8,128)} %add_select_fusion.4.pick_ref), custom_call_target="tpu_custom_call" | custom-call | flops 20000000 | bytes 200000 | tf_op jit(solution)/shard_map/contact/pallas_call | solution.py:289
  64.9 0.0 all-to-all-done.1
  64.9 1.2 %copy-done = f32[128,7,4,128]{3,2,1,0:T(4,128)} copy-done((f32[128,7,4,128]{3,2,1,0:T(4,128)}, f32[128,7,4,128]{3,2,1,0:T(4,128)S(1)}, u32[]{:S(2)}) %copy-start) | copy-done | bytes 1835032
  66.1 26.9 %pairs.1 = (f32[9,32,128]{2,1,0:T(8,128)}, f32[3,32,128]{2,1,0:T(8,128)}, f32[1536,128]{1,0:T(8,128)}) custom-call(s32[256]{0:T(256)} %multiply_add_fusion.slot_ref, f32[3,32,128]{2,1,0:T(8,128)} %bitcast.25, f32[3,32,128]{2,1,0:T(8,128)} %bitcast.27, f32[32,128]{1,0:T(8,128)} %copy-done.4, f32[2,32,128]{2,1,0:T(8,128)} %bitcast.30, ...), custom_call_target="tpu_custom_call" | custom-call | flops 60000000 | bytes 4000000 | tf_op jit(solution)/shard_map/pairs/pallas_call | solution.py:303
  92.9 9.1 %all-to-all-start.2 = ((f32[128,3,4,128]{3,2,1,0:T(4,128)}), f32[128,3,4,128]{3,2,1,0:T(4,128)S(1)}, u32[]{:S(2)}, u32[]{:S(2)}) async-start(f32[128,3,4,128]{3,2,1,0:T(4,128)} %bitcast.23), calls=%async_computation.2 | async-start | bytes 1572864 | tf_op jit(solution)/shard_map/all_to_all | solution.py:333
  102.1 0.1 reshape.122
  102.2 0.2 add_select_fusion
  102.4 0.8 select_n.45.code_ref
  103.2 15.3 %all-to-all-done.2 = f32[128,3,4,128]{3,2,1,0:T(4,128)S(1)} async-done(((f32[128,3,4,128]{3,2,1,0:T(4,128)}), f32[128,3,4,128]{3,2,1,0:T(4,128)S(1)}, u32[]{:S(2)}, u32[]{:S(2)}) %all-to-all-start.2) | async-done | bytes 786464 | tf_op jit(solution)/shard_map/all_to_all | solution.py:333
  118.5 0.9 copy-done.1
  119.4 2.2 %returned.1 = f32[3,32,128]{2,1,0:T(8,128)} custom-call(s32[1,1536]{1,0:T(1,128)} %select_n.45.code_ref, f32[1536,128]{1,0:T(8,128)} %bitcast.22, f32[3,32,128]{2,1,0:T(8,128)} %get-tuple-element.6.force_ref), custom_call_target="tpu_custom_call" | custom-call | tf_op jit(solution)/shard_map/returned/pallas_call | solution.py:338
  (14 shorter events, 0.1 us)
Async XLA Ops:
  5.5 21.0 %all-to-all-start = ((s32[128,1,4]{2,1,0:T(1,128)}), s32[128,1,4]{2,1,0:T(1,128)S(1)}, u32[]{:S(2)}, u32[]{:S(2)}) async-start(s32[128,1,4]{2,1,0:T(1,128)} %bitcast.2), calls=%async_computation | async-start | bytes 131072 | tf_op jit(solution)/shard_map/all_to_all | solution.py:267
  20.8 15.9 %copy-start.4 = (f32[32,128]{1,0:T(8,128)}, f32[32,128]{1,0:T(8,128)S(1)}, u32[]{:S(2)}) copy-start(f32[32,128]{1,0:T(8,128)S(1)} %get-tuple-element.11.weight_ref) | copy-start | bytes 49156
  32.0 4.6 %copy-start.2 = (f32[32,3,128]{2,0,1:T(8,128)S(1)}, f32[32,3,128]{2,0,1:T(8,128)}, u32[]{:S(2)}) copy-start(f32[32,3,128]{2,0,1:T(8,128)} %param.8) | copy-start | bytes 147460
  32.0 4.6 %copy-start.3 = (f32[32,3,128]{2,0,1:T(8,128)S(1)}, f32[32,3,128]{2,0,1:T(8,128)}, u32[]{:S(2)}) copy-start(f32[32,3,128]{2,0,1:T(8,128)} %param.9) | copy-start | bytes 147460
  32.0 10.2 %copy-start.6 = (s32[32,2]{0,1:T(2,128)S(1)}, s32[32,2]{0,1:T(2,128)}, u32[]{:S(2)}) copy-start(s32[32,2]{0,1:T(2,128)} %param.15) | copy-start | bytes 772
  32.0 11.4 %copy-start.5 = (f32[32,2,128]{2,1,0:T(2,128)S(1)}, f32[32,2,128]{2,1,0:T(2,128)}, u32[]{:S(2)}) copy-start(f32[32,2,128]{2,1,0:T(2,128)} %param.11) | copy-start | bytes 98308
  32.0 32.9 %all-to-all-start.1 = ((f32[128,7,4,128]{3,2,1,0:T(4,128)}), f32[128,7,4,128]{3,2,1,0:T(4,128)S(1)}, u32[]{:S(2)}, u32[]{:S(2)}) async-start(f32[128,7,4,128]{3,2,1,0:T(4,128)} %reshape.123), calls=%async_computation.1 | async-start | bytes 3670016 | tf_op jit(solution)/shard_map/all_to_all | solution.py:273
  36.7 18.3 %collective-permute-start = (f32[4,4,128]{2,1,0:T(4,128)S(1)}, f32[4,4,128]{2,1,0:T(4,128)S(1)}, u32[]{:S(2)}, u32[]{:S(2)}) collective-permute-start(f32[4,4,128]{2,1,0:T(4,128)S(1)} %get-tuple-element.12), channel_id=1, source_target_pairs={{0,16},{16,32},{32,48},{48,64},{64,80},{80,96},{96,112},{1,17},{17... | collective-permute-start | bytes 24584 | tf_op jit(solution)/shard_map/ppermute | solution.py:279
  40.2 18.0 %collective-permute-start.1 = (f32[4,4,128]{2,1,0:T(4,128)S(1)}, f32[4,4,128]{2,1,0:T(4,128)S(1)}, u32[]{:S(2)}, u32[]{:S(2)}) collective-permute-start(f32[4,4,128]{2,1,0:T(4,128)S(1)} %get-tuple-element.13), channel_id=1, source_target_pairs={{16,0},{32,16},{48,32},{64,48},{80,64},{96,80},{112,96},{17,1},{33... | collective-permute-start | bytes 24584 | tf_op jit(solution)/shard_map/ppermute | solution.py:280
  64.9 1.2 %copy-start = (f32[128,7,4,128]{3,2,1,0:T(4,128)}, f32[128,7,4,128]{3,2,1,0:T(4,128)S(1)}, u32[]{:S(2)}) copy-start(f32[128,7,4,128]{3,2,1,0:T(4,128)S(1)} %all-to-all-done.1) | copy-start | bytes 5505028
  92.9 25.6 %all-to-all-start.2 = ((f32[128,3,4,128]{3,2,1,0:T(4,128)}), f32[128,3,4,128]{3,2,1,0:T(4,128)S(1)}, u32[]{:S(2)}, u32[]{:S(2)}) async-start(f32[128,3,4,128]{3,2,1,0:T(4,128)} %bitcast.23), calls=%async_computation.2 | async-start | bytes 1572864 | tf_op jit(solution)/shard_map/all_to_all | solution.py:333
  118.5 0.9 copy-start.1

commit v2 on v1

v2 whole, which is shorter than its diff:
```python
import math

import jax
import jax.numpy as jnp
from jax import lax
from jax.experimental import pallas as pl
from jax.experimental.pallas import tpu as pltpu
from jax.sharding import PartitionSpec as P

SH = 4
SUPPORT_SQ = 0.5
CONTACT_SQ = 0.1
PENALTY = 200.0
GROUP = 8
ROWS = 7
SIDE = 48
F32 = jnp.float32
BF16 = jnp.bfloat16
AXES = ("gx", "yz")
NT = (((1,), (1,)), ((), ()))
NN = (((1,), (0,)), ((), ()))


def high(x):
    return x.astype(BF16).astype(F32)


def parts(x, count):
    out = []
    for _ in range(count - 1):
        h = high(x)
        out.append(h)
        x = x - h
    out.append(high(x))
    return out


def mm(a, b, dims):
    return lax.dot_general(a, b, dims, preferred_element_type=F32)


def plan_kernel(owner_ref, local_ref, ask_ref, start_ref, rows, *, cap):
    fanout, blocks = local_ref.shape
    devices, width = ask_ref.shape
    total = fanout * blocks
    for k in range(fanout):
        cols = pl.ds(k * blocks, blocks)
        rows[0:1, cols] = owner_ref[k]
        rows[1:2, cols] = local_ref[k : k + 1, :]
    owner = rows[0:1, :]
    local = (rows[1:2, :] + 1).astype(F32)
    named = owner == lax.broadcasted_iota(jnp.int32, (devices, total), 0)
    hot = named.astype(F32)
    earlier = lax.broadcasted_iota(jnp.int32, (total, total), 0) < lax.broadcasted_iota(
        jnp.int32, (total, total), 1
    )
    rank = mm(hot.astype(BF16), earlier.astype(F32).astype(BF16), NN)
    lane = lax.broadcasted_iota(jnp.int32, (width, total), 0)
    ask = jnp.zeros((devices, width), F32)
    for s in range(cap):
        chosen = jnp.where(rank == float(s), hot, 0.0).astype(BF16)
        ask = ask + mm(chosen, jnp.where(lane == s, local, 0.0).astype(BF16), NT)
    ask_ref[...] = ask.astype(jnp.int32) - 1
    place = jnp.sum(hot * rank, axis=0, keepdims=True).astype(jnp.int32)
    start_ref[0:1, :] = owner * (cap * ROWS) + place
    start_ref[1:2, :] = owner * (cap * 3) + place


def provide_kernel(ask_ref, pos_ref, disp_ref, weight_ref, out_ref, wide, *, cap):
    devices = ask_ref.shape[0]
    blocks, lanes = weight_ref.shape
    depth = 3 * blocks
    cols = []
    for c in range(ROWS):
        x = weight_ref[...] if c == 6 else (pos_ref if c < 3 else disp_ref)[c % 3]
        cols.append(jnp.concatenate(parts(x, 3), axis=0).astype(BF16))
    data = jnp.concatenate(cols, axis=1)
    for s in range(cap):
        wide[pl.ds(s, devices, stride=cap), :] = jnp.broadcast_to(
            ask_ref[:, s : s + 1], (devices, lanes)
        )
    step = 64
    local = lax.broadcasted_iota(jnp.int32, (step, depth), 1) % blocks
    for i in range(devices * cap // step):
        hot = (wide[pl.ds(i * step, step), 0:depth] == local).astype(F32).astype(BF16)
        got = mm(hot, data, NN)
        for j in range(step // cap):
            r = i * (step // cap) + j
            for c in range(ROWS):
                out_ref[pl.ds((r * ROWS + c) * cap, cap), :] = got[
                    j * cap : (j + 1) * cap, c * lanes : (c + 1) * lanes
                ]


def own_kernel(pos_ref, at_ref, centre_ref, side):
    _, blocks, lanes = pos_ref.shape
    inv = 1.0 / SUPPORT_SQ
    side[...] = jnp.zeros_like(side)
    centre_ref[...] = jnp.zeros_like(centre_ref)
    ones = jnp.ones((GROUP, lanes), F32)
    for d in (0, 3, 5):
        side[pl.ds(d * 8 + 7, GROUP, stride=SIDE), :] = ones

    def group(g, _):
        start = pl.multiple_of(g * GROUP, GROUP)
        norm = jnp.zeros((GROUP, lanes), F32)
        for c in range(3):
            x = pos_ref[c, pl.ds(start, GROUP), :]
            mid = jnp.broadcast_to(x[:, 0:1], x.shape)
            x = x - mid
            centre_ref[pl.ds(start * 8 + c, GROUP, stride=8), :] = mid
            norm = norm + x * x
            h, m, l = [2.0 * inv * p for p in parts(x, 3)]
            for d, v in enumerate((h, m, l, h, m, h)):
                side[pl.ds(d * 8 + c, GROUP, stride=SIDE), :] = v
        for d, v in enumerate(parts(1.0 - inv * norm, 3)):
            side[pl.ds(d * 8 + 3, GROUP, stride=SIDE), :] = v
        for q in range(GROUP):
            at_ref[start + q] = jnp.transpose(side[pl.ds(q * SIDE, SIDE), :]).astype(BF16)
        return 0

    lax.fori_loop(0, blocks // GROUP, group, 0)


def contact_kernel(pos_ref, disp_ref, weight_ref, below_ref, above_ref, pick_ref, out_ref, wide, cur):
    blocks, lanes = weight_ref.shape
    half = below_ref.shape[0]
    for c in range(3):
        cur[c] = pos_ref[c] + disp_ref[c]
    for s in range(2 * half):
        block = below_ref[s] if s < half else above_ref[s - half]
        turned = jnp.transpose(jnp.concatenate([block, block], axis=0))
        for c in range(4):
            wide[s, c] = jnp.broadcast_to(turned[:, c : c + 1], (lanes, lanes))

    def block(b, _):
        own = [jnp.broadcast_to(cur[c, pl.ds(b, 1), :], (8, lanes)) for c in range(3)]
        total = [jnp.zeros((8, lanes), F32) for _ in range(3)]
        for k in range(2):
            s = pick_ref[b, k]
            for r in range(lanes // 8):
                rows = pl.ds(r * 8, 8)
                gap = [own[c] - wide[s, c, rows, :] for c in range(3)]
                near = jnp.maximum(
                    CONTACT_SQ - (gap[0] * gap[0] + gap[1] * gap[1] + gap[2] * gap[2]), 0.0
                )
                push = near * near * wide[s, 3, rows, :]
                total = [total[c] + push * gap[c] for c in range(3)]
        scale = PENALTY * (weight_ref[pl.ds(b, 1), :] > 0).astype(F32)
        for c in range(3):
            out_ref[c, pl.ds(b, 1), :] = scale * jnp.sum(total[c], axis=0, keepdims=True)
        return 0

    lax.fori_loop(0, blocks, block, 0)


def main_kernel(
    start_ref, pos_ref, disp_ref, weight_ref, lame_ref, contact_ref, at_ref, centre_ref, got_ref,
    piola_ref, force_ref, back_ref,
    raw, far, b_all, f_all, k_all, ss, gs,
):
    blocks, lanes = weight_ref.shape
    fanout = far.shape[1]
    cap = 4
    coeff = -3.0 / math.sqrt(fanout * lanes)
    inv = 1.0 / SUPPORT_SQ
    back_ref[...] = jnp.zeros_like(back_ref)
    gs[...] = jnp.zeros_like(gs)
    raw[...] = jnp.zeros_like(raw)
    row = lax.broadcasted_iota(jnp.int32, (8, lanes), 0)

    def far_side(b, _):
        centre = centre_ref[pl.ds(pl.multiple_of(b * 8, 8), 8), :]
        for k in range(fanout):
            raw[k, 0:ROWS, :] = got_ref[pl.ds(start_ref[0, k * blocks + b], ROWS, stride=cap), :]
        for k in range(fanout):
            t = raw[k] - centre
            far[b, k] = t
            square = t * t
            norm = square[0:1] + square[1:2] + square[2:3]
            place = jnp.where(row == 3, 1.0, jnp.where(row == 7, -inv * norm, t))
            h, m, l = parts(place, 3)
            cols = pl.ds(k * lanes, lanes)
            b_all[b, :, cols] = jnp.concatenate([h, h, h, m, m, l], axis=0).astype(BF16)
            weight = t[6:7]
            plain = jnp.where(row == 6, 1.0, t)
            feats = [weight * plain] + [(weight * t[3 + a : 4 + a]) * plain for a in range(3)]
            split = [parts(v, 2) for v in feats]
            f_all[b, :, cols] = jnp.concatenate(
                [v[0] for v in split] + [v[1] for v in split], axis=0
            ).astype(BF16)
        return 0

    lax.fori_loop(0, blocks, far_side, 0, unroll=2)

    def group(g, _):
        start = pl.multiple_of(g * GROUP, GROUP)
        rows = pl.ds(start, GROUP)

        def forward(q, _):
            b = start + q
            sums = jnp.zeros((64, 2 * lanes), F32)
            for k in range(0, fanout, 2):
                cols = pl.ds(k * lanes, 2 * lanes)
                near = jnp.maximum(mm(at_ref[b], b_all[b, :, cols], NN), 0.0)
                near = near * near
                hi = near.astype(BF16)
                lo = (near - hi.astype(F32)).astype(BF16)
                both = jnp.concatenate([hi, lo], axis=0)
                k_all[q, :, cols] = both
                sums = sums + mm(f_all[b, :, cols], both, NT)
            sums = sums[:, 0:lanes] + sums[:, lanes:]
            ss[pl.ds(pl.multiple_of(q * 32, 32), 32), :] = sums[0:32] + sums[32:64]
            return 0

        lax.fori_loop(0, GROUP, forward, 0, unroll=4)

        def total(f):
            return ss[pl.ds(f, GROUP, stride=32), :]

        mass = total(6)
        weight = weight_ref[rows, :]
        inside = (weight > 0).astype(F32)
        here = [pos_ref[c, rows, :] for c in range(3)]
        here = [x - x[:, 0:1] for x in here]
        moved = [disp_ref[c, rows, :] for c in range(3)]
        column = [coeff * (here[c] * mass - total(c)) for c in range(3)]
        deform = [
            [
                (1.0 if a == c else 0.0)
                + coeff * (here[c] * total(3 + a) - total(8 + 8 * a + c))
                - moved[a] * column[c]
                for c in range(3)
            ]
            for a in range(3)
        ]
        strain = [[None] * 3 for _ in range(3)]
        for a in range(3):
            for c in range(a, 3):
                v = sum(deform[k][a] * deform[k][c] for k in range(3))
                strain[a][c] = strain[c][a] = 0.5 * (v - (1.0 if a == c else 0.0))
        trace = lame_ref[0, rows, :] * (strain[0][0] + strain[1][1] + strain[2][2])
        twice = 2.0 * lame_ref[1, rows, :]
        second = [
            [(trace if a == c else 0.0) + twice * strain[a][c] for c in range(3)] for a in range(3)
        ]
        scaled = [[None] * 3 for _ in range(3)]
        for a in range(3):
            for c in range(3):
                v = sum(deform[a][k] * second[k][c] for k in range(3)) * inside
                piola_ref[3 * a + c, rows, :] = v
                scaled[a][c] = weight * v
        for a in range(3):
            own = sum(scaled[a][c] * column[c] for c in range(3))
            force_ref[a, rows, :] = own + contact_ref[a, rows, :]
            feats = scaled[a] + [sum(scaled[a][c] * here[c] for c in range(3))]
            for f, v in enumerate(feats):
                h, l = parts(v, 2)
                gs[pl.ds(f * 8 + a, GROUP, stride=32), :] = h
                gs[pl.ds(f * 8 + 4 + a, GROUP, stride=32), :] = l

        def backward(q, _):
            b = start + q
            feat = gs[pl.ds(pl.multiple_of(q * 32, 32), 32), :].astype(BF16)
            feat = jnp.concatenate([feat, feat], axis=1)
            for k in range(0, fanout, 2):
                sums = mm(feat, k_all[q, :, pl.ds(k * lanes, 2 * lanes)], NN)
                for j in range(2):
                    t = far[b, k + j]
                    back = [sums[8 * f : 8 * f + 8, j * lanes : (j + 1) * lanes] for f in range(4)]
                    v = back[3] - sum(t[c : c + 1] * back[c] for c in range(3))
                    v = (-coeff * t[6:7]) * v
                    first = start_ref[1, (k + j) * blocks + b]
                    back_ref[pl.ds(first, 3, stride=cap), :] = v[0:3] + v[4:7]
            return 0

        lax.fori_loop(0, GROUP, backward, 0, unroll=4)
        return 0

    lax.fori_loop(0, blocks // GROUP, group, 0)


def returned_kernel(code_ref, got_ref, force_ref, out_ref):
    comps, blocks, lanes = force_ref.shape
    rows = got_ref.shape[0]
    target = lax.broadcasted_iota(jnp.int32, (comps * blocks, rows), 0)
    chosen = (target == code_ref[...]).astype(F32).astype(BF16)
    out = force_ref[...].reshape(comps * blocks, lanes)
    for part in parts(got_ref[...], 2):
        out = out + mm(chosen, part.astype(BF16), NN)
    out_ref[...] = out.reshape(comps, blocks, lanes)


def vmem(count):
    return [pl.BlockSpec(memory_space=pltpu.VMEM)] * count


SMEM = pl.BlockSpec(memory_space=pltpu.SMEM)


def call(body, name, out, in_specs, scratch=(), mib=8, flops=1_000_000, size=1_000_000):
    many = isinstance(out, tuple)
    return pl.pallas_call(
        body,
        out_shape=out,
        in_specs=in_specs,
        out_specs=tuple(vmem(len(out))) if many else vmem(1)[0],
        scratch_shapes=list(scratch),
        compiler_params=pltpu.CompilerParams(vmem_limit_bytes=mib * 2**20),
        cost_estimate=pl.CostEstimate(flops=flops, bytes_accessed=size, transcendentals=0),
        name=name,
    )


def main_call(start, pos_t, disp_t, weight, lame_t, contact, at, centre, got):
    blocks, lanes = weight.shape
    fanout = start.shape[1] // blocks
    wide = fanout * lanes
    back = got.shape[0] // ROWS * 3
    return call(
        main_kernel,
        "pairs",
        (
            jax.ShapeDtypeStruct((9, blocks, lanes), F32),
            jax.ShapeDtypeStruct((3, blocks, lanes), F32),
            jax.ShapeDtypeStruct((back, lanes), F32),
        ),
        [SMEM] + vmem(8),
        [
            pltpu.VMEM((fanout, 8, lanes), F32),
            pltpu.VMEM((blocks, fanout, 8, lanes), F32),
            pltpu.VMEM((blocks, SIDE, wide), BF16),
            pltpu.VMEM((blocks, 64, wide), BF16),
            pltpu.VMEM((GROUP, 2 * lanes, wide), BF16),
            pltpu.VMEM((GROUP * 32, lanes), F32),
            pltpu.VMEM((GROUP * 32, lanes), F32),
        ],
        mib=28,
        flops=60_000_000,
        size=4_000_000,
    )(start, pos_t, disp_t, weight, lame_t, contact, at, centre, got)


def per_device(ref_pos, disp, volume, lame, pad_count, nbr_owner, nbr_local, contact_block):
    blocks, _, lanes = ref_pos.shape
    fanout = nbr_local.shape[1]
    across = lax.axis_size("gx")
    deep = lax.axis_size("yz")
    devices = across * deep
    cap = 2 * blocks * fanout // devices
    total = blocks * fanout
    shape = jax.ShapeDtypeStruct

    ask, start = call(
        lambda *refs: plan_kernel(*refs, cap=cap),
        "plan",
        (shape((devices, 16), jnp.int32), shape((2, total), jnp.int32)),
        vmem(2),
        [pltpu.VMEM((8, total), jnp.int32)],
    )(jnp.transpose(nbr_owner, (1, 2, 0)), jnp.transpose(nbr_local))
    asked = lax.all_to_all(ask, AXES, split_axis=0, concat_axis=0, tiled=True)

    usable = (jnp.arange(lanes)[None, :] < (lanes - pad_count)[:, None]).astype(F32)
    weight = volume * usable
    pos_t = jnp.transpose(ref_pos, (1, 0, 2))
    disp_t = jnp.transpose(disp, (1, 0, 2))
    lame_t = jnp.transpose(lame, (1, 0, 2))

    surface = jnp.concatenate([ref_pos + disp, weight[:, None, :]], axis=1)
    up = [(i, i + 1) for i in range(across - 1)]
    down = [(i + 1, i) for i in range(across - 1)]
    below = lax.ppermute(surface[blocks - SH :], "gx", up)
    above = lax.ppermute(surface[:SH], "gx", down)
    local = contact_block % blocks
    row = contact_block // blocks // deep
    pick = jnp.where(row < lax.axis_index("gx"), local - (blocks - SH), SH + local)

    at, centre = call(
        own_kernel,
        "own",
        (shape((blocks, lanes, SIDE), BF16), shape((blocks * 8, lanes), F32)),
        vmem(1),
        [pltpu.VMEM((GROUP * SIDE, lanes), F32)],
    )(pos_t)

    picked = call(
        lambda *refs: provide_kernel(*refs, cap=cap),
        "provide",
        shape((devices * cap * ROWS, lanes), F32),
        vmem(4),
        [pltpu.VMEM((devices * cap, lanes), jnp.int32)],
    )(asked, pos_t, disp_t, weight)
    got = lax.all_to_all(
        picked.reshape(devices, ROWS, cap, lanes), AXES, split_axis=0, concat_axis=0, tiled=True
    ).reshape(devices * cap * ROWS, lanes)

    contact = call(
        contact_kernel,
        "contact",
        shape((3, blocks, lanes), F32),
        vmem(5) + [SMEM],
        [pltpu.VMEM((2 * SH, 4, lanes, lanes), F32), pltpu.VMEM((3, blocks, lanes), F32)],
        flops=20_000_000,
    )(pos_t, disp_t, weight, below, above, pick)

    piola, force, back = main_call(
        start, pos_t, disp_t, weight, lame_t, contact, at, centre, got
    )
    received = lax.all_to_all(
        back.reshape(devices, 3, cap, lanes), AXES, split_axis=0, concat_axis=0, tiled=True
    )
    ids = asked[:, None, 0:cap]
    code = jnp.where(ids >= 0, ids + blocks * jnp.arange(3)[None, :, None], -1).reshape(1, -1)
    force = call(returned_kernel, "returned", shape((3, blocks, lanes), F32), vmem(3))(
        code, received.reshape(devices * cap * 3, lanes), force
    )
    return (jnp.transpose(force, (1, 0, 2)), jnp.transpose(piola, (1, 0, 2)))


def solution(mesh):
    return jax.shard_map(
        per_device,
        mesh=mesh,
        in_specs=(
            P(AXES, None, None),
            P(AXES, None, None),
            P(AXES, None),
            P(AXES, None, None),
            P(AXES),
            P(AXES, None, None),
            P(AXES, None),
            P(AXES, None),
        ),
        out_specs=(P(AXES, None, None), P(AXES, None, None)),
        check_vma=False,
    )
```

time: 122 us -> 106 us (0.87)
  local copies, waits for them, and re-layouts: 13.9 us -> 5.42 us
  Pallas kernels: 35 us -> 27.6 us
  other arithmetic: 5.99 us -> 1.67 us
  waiting for transfers between devices: 35.3 us -> 39.4 us
    pallas_call x3 -> x6, Pallas kernels: 35 us -> 27.6 us  [the longest x1 19.2 us: main_call(): call(main_kernel, 'pairs', (jax.ShapeDtypeStruct((9, blocks, lanes), F32)...]
    all_to_all x2, waiting for transfers between devices: 5.75 us -> 8.27 us  [the longest x1 8.08 us: per_device(): asked = lax.all_to_all(ask, AXES, split_axis=0, concat_axis=0, tiled=True)]
    reshape x3 -> x0, local copies, waits for them, and re-layouts: 2.08 us -> none  [the longest x1 1.89 us: per_device(): picked = packed[jnp.maximum(slot_ids, 0)].reshape(devices, ROWS, cap, lanes)]
    gather x1 -> x0, local copies, waits for them, and re-layouts: 1.88 us -> none  [per_device(): picked = packed[jnp.maximum(slot_ids, 0)].reshape(devices, ROWS, cap, lanes)]
    scatter x1 -> x0, local copies, waits for them, and re-layouts: 1.4 us -> none  [per_device(): requests = jnp.full((slots_all,), -1, jnp.int32).at[slots].set(wanted)]
    convert_element_type x1 -> x0, other arithmetic: 1.39 us -> none  [per_device(): mask = (weight > 0).astype(F32)]
    all_to_all x2 -> x0, local copies, waits for them, and re-layouts: 1.25 us -> none  [per_device(): lax.all_to_all(requests.reshape(devices, cap), AXES, split_axis=0, concat...]
    unnamed x20 -> x22, local copies, waits for them, and re-layouts: 6.04 us -> 5.2 us
  transfers between devices with their start and end apart: 5 -> 5, of which waited for: 4 -> 5; matrix products, arithmetic and copies ran while one was open for 6% -> 2% of each run, Pallas kernels for 5% -> 6%
where the time goes in v2:
time: 106 us; the launch traced here: 105 us
  waiting for transfers between devices  39.4 us (37%)
  starting transfers between devices  30.4 us (29%)
  Pallas kernels  27.6 us (26%)
  local copies, waits for them, and re-layouts  5.42 us (5%)
  other arithmetic  1.67 us (2%)
    pallas_call x1, Pallas kernels, main_call(): call(main_kernel, 'pairs', (jax.ShapeDtypeStruct((9, blocks, lanes), F32)...  19.2 us
    all_to_all x1, waiting for transfers between devices, per_device(): lax.all_to_all(back.reshape(devices, 3, cap, lanes), AXES, split_axis=0,...  16.1 us
    ppermute x1, waiting for transfers between devices, per_device(): below = lax.ppermute(surface[blocks - SH:], 'gx', up)  11.7 us
    all_to_all x1, starting transfers between devices, per_device(): asked = lax.all_to_all(ask, AXES, split_axis=0, concat_axis=0, tiled=True)  11.5 us
    all_to_all x1, starting transfers between devices, per_device(): lax.all_to_all(back.reshape(devices, 3, cap, lanes), AXES, split_axis=0,...  8.91 us
    all_to_all x1, waiting for transfers between devices, per_device(): asked = lax.all_to_all(ask, AXES, split_axis=0, concat_axis=0, tiled=True)  8.08 us
    unnamed x22, local copies, waits for them, and re-layouts  5.2 us
    pallas_call x1, Pallas kernels, per_device(): call(contact_kernel, 'contact', shape((3, blocks, lanes), F32), vmem(5) +...  4.99 us
  transfers between devices with their start and end apart: 5, of which 5 were waited for; matrix products, arithmetic and copies ran while one was open for 2% of the time, Pallas kernels for 6%

profile of v2, /device:TPU:1, one launch (start us, length us, event | category | flops | bytes accessed | tf_op | source)
XLA Modules:
  0.0 105.3 jit_solution(7710924348657861008)
XLA Ops:
  0.6 0.0 copy-start.6
  0.6 0.7 copy-done.6
  1.3 0.0 copy-start.7
  1.3 0.7 copy-done.7
  2.0 1.1 %plan.1 = (s32[128,16]{1,0:T(8,128)}, s32[2,256]{1,0:T(2,128)S(1)}) custom-call(s32[8,1,32]{2,1,0:T(1,128)S(1)} %bitcast.37, s32[8,32]{1,0:T(8,128)S(1)} %bitcast.38), custom_call_target="tpu_custom_call" | custom-call | flops 1000000 | bytes 1000000 | tf_op jit(solution)/shard_map/plan/pallas_call | solution.py:354
  3.1 11.5 %all-to-all-start = ((s32[128,1,16]{2,1,0:T(1,128)}), s32[128,1,16]{2,1,0:T(1,128)S(1)}, u32[]{:S(2)}, u32[]{:S(2)}) async-start(s32[128,1,16]{2,1,0:T(1,128)} %bitcast.3), calls=%async_computation | async-start | bytes 131072 | tf_op jit(solution)/shard_map/all_to_all | solution.py:361
  14.6 0.7 broadcast_subtract_fusion
  15.2 0.8 fusion.2.weight_ref.refs_3_
  16.0 8.1 %all-to-all-done = s32[128,1,16]{2,1,0:T(1,128)S(1)} async-done(((s32[128,1,16]{2,1,0:T(1,128)}), s32[128,1,16]{2,1,0:T(1,128)S(1)}, u32[]{:S(2)}, u32[]{:S(2)}) %all-to-all-start) | async-done | bytes 8224 | tf_op jit(solution)/shard_map/all_to_all | solution.py:361
  24.1 0.0 copy-start.1
  24.1 0.8 copy-done.1
  24.9 0.0 copy-start.4
  24.9 0.8 copy-done.4
  25.7 0.5 provide.1
  26.2 0.0 copy-start
  26.2 1.3 %copy-done = f32[3584,128]{1,0:T(8,128)} copy-done((f32[3584,128]{1,0:T(8,128)}, f32[3584,128]{1,0:T(8,128)S(1)}, u32[]{:S(2)}) %copy-start) | copy-done | bytes 1835032
  27.4 0.0 copy-start.2
  27.4 0.0 copy-start.5
  27.4 0.0 copy-start.9
  27.4 0.0 copy-start.8
  27.4 4.6 %all-to-all-start.1 = ((f32[128,7,4,128]{3,2,1,0:T(4,128)}), f32[128,7,4,128]{3,2,1,0:T(4,128)S(1)}, u32[]{:S(2)}, u32[]{:S(2)}) async-start(f32[128,7,4,128]{3,2,1,0:T(4,128)} %bitcast.22), calls=%async_computation.1 | async-start | bytes 3670016 | tf_op jit(solution)/shard_map/all_to_all | solution.py:393
  32.0 0.0 copy-done.2
  32.0 0.0 copy-done.5
  32.1 3.5 %collective-permute-start = (f32[4,4,128]{2,1,0:T(4,128)S(1)}, f32[4,4,128]{2,1,0:T(4,128)S(1)}, u32[]{:S(2)}, u32[]{:S(2)}) collective-permute-start(f32[4,4,128]{2,1,0:T(4,128)S(1)} %get-tuple-element.17), channel_id=1, source_target_pairs={{0,16},{16,32},{32,48},{48,64},{64,80},{80,96},{96,112},{1,17},{17... | collective-permute-start | bytes 24584 | tf_op jit(solution)/shard_map/ppermute | solution.py:372
  35.7 1.9 %collective-permute-start.1 = (f32[4,4,128]{2,1,0:T(4,128)S(1)}, f32[4,4,128]{2,1,0:T(4,128)S(1)}, u32[]{:S(2)}, u32[]{:S(2)}) collective-permute-start(f32[4,4,128]{2,1,0:T(4,128)S(1)} %get-tuple-element.16), channel_id=1, source_target_pairs={{16,0},{32,16},{48,32},{64,48},{80,64},{96,80},{112,96},{17,1},{33... | collective-permute-start | bytes 24584 | tf_op jit(solution)/shard_map/ppermute | solution.py:373
  37.6 0.0 copy-done.9
  37.6 0.1 copy.39
  37.7 0.0 copy-done.8
  37.8 1.0 own.1
  38.7 11.7 %collective-permute-done.below_ref = f32[4,4,128]{2,1,0:T(4,128)S(1)} collective-permute-done((f32[4,4,128]{2,1,0:T(4,128)S(1)}, f32[4,4,128]{2,1,0:T(4,128)S(1)}, u32[]{:S(2)}, u32[]{:S(2)}) %collective-permute-start) | collective-permute-done | bytes 8224 | tf_op jit(solution)/shard_map/ppermute | solution.py:372
  50.4 3.3 %collective-permute-done.1.above_ref = f32[4,4,128]{2,1,0:T(4,128)S(1)} collective-permute-done((f32[4,4,128]{2,1,0:T(4,128)S(1)}, f32[4,4,128]{2,1,0:T(4,128)S(1)}, u32[]{:S(2)}, u32[]{:S(2)}) %collective-permute-start.1) | collective-permute-done | bytes 8224 | tf_op jit(solution)/shard_map/ppermute | solution.py:373
  53.7 5.0 %contact.1.contact_ref = f32[3,32,128]{2,1,0:T(8,128)S(1)} custom-call(f32[3,32,128]{2,1,0:T(8,128)S(1)} %bitcast.26, f32[3,32,128]{2,1,0:T(8,128)S(1)} %bitcast.33, f32[32,128]{1,0:T(8,128)S(1)} %fusion.2.weight_ref.refs_3_, f32[4,4,128]{2,1,0:T(4,128)S(1)} %collective-permute-done.below_ref, f32[4,4,128]{2,1,0:T(4,128)S(1)} %collective-permute-done.1.above_ref, ...), custom_call_target="tpu_custom_call" | custom-call | flops 20000000 | bytes 1000000 | tf_op jit(solution)/shard_map/contact/pallas_call | solution.py:397
  58.7 0.2 all-to-all-done.1
  58.9 19.2 %pairs.1 = (f32[9,32,128]{2,1,0:T(8,128)}, f32[3,32,128]{2,1,0:T(8,128)S(1)}, f32[1536,128]{1,0:T(8,128)S(1)}) custom-call(s32[2,256]{1,0:T(2,128)S(1)} %get-tuple-element.10.start_ref, f32[3,32,128]{2,1,0:T(8,128)S(1)} %bitcast.27, f32[3,32,128]{2,1,0:T(8,128)S(1)} %bitcast.34, f32[32,128]{1,0:T(8,128)S(1)} %fusion.2.weight_ref.refs_3_, ...), custom_call_target="tpu_custom_call" | custom-call | flops 60000000 | bytes 4000000 | tf_op jit(solution)/shard_map/pairs/pallas_call | solution.py:320
  78.1 0.0 copy-start.3
  78.1 0.9 copy-done.3
  78.9 8.9 %all-to-all-start.2 = ((f32[128,3,4,128]{3,2,1,0:T(4,128)}), f32[128,3,4,128]{3,2,1,0:T(4,128)S(1)}, u32[]{:S(2)}, u32[]{:S(2)}) async-start(f32[128,3,4,128]{3,2,1,0:T(4,128)} %bitcast.31), calls=%async_computation.2 | async-start | bytes 1572864 | tf_op jit(solution)/shard_map/all_to_all | solution.py:409
  87.9 0.1 add_select_fusion
  88.0 0.2 select_n.33.code_ref
  88.2 16.1 %all-to-all-done.2 = f32[128,3,4,128]{3,2,1,0:T(4,128)S(1)} async-done(((f32[128,3,4,128]{3,2,1,0:T(4,128)}), f32[128,3,4,128]{3,2,1,0:T(4,128)S(1)}, u32[]{:S(2)}, u32[]{:S(2)}) %all-to-all-start.2) | async-done | bytes 786464 | tf_op jit(solution)/shard_map/all_to_all | solution.py:409
  104.3 1.0 returned.1
  (7 shorter events, 0.1 us)
Async XLA Ops:
  0.6 0.7 copy-start.6
  1.3 0.7 copy-start.7
  3.1 21.0 %all-to-all-start = ((s32[128,1,16]{2,1,0:T(1,128)}), s32[128,1,16]{2,1,0:T(1,128)S(1)}, u32[]{:S(2)}, u32[]{:S(2)}) async-start(s32[128,1,16]{2,1,0:T(1,128)} %bitcast.3), calls=%async_computation | async-start | bytes 131072 | tf_op jit(solution)/shard_map/all_to_all | solution.py:361
  24.1 0.8 copy-start.1
  24.9 0.8 copy-start.4
  26.2 1.3 %copy-start = (f32[3584,128]{1,0:T(8,128)}, f32[3584,128]{1,0:T(8,128)S(1)}, u32[]{:S(2)}) copy-start(f32[3584,128]{1,0:T(8,128)S(1)} %provide.1) | copy-start | bytes 5505028
  27.4 4.6 %copy-start.2 = (f32[32,3,128]{2,0,1:T(8,128)S(1)}, f32[32,3,128]{2,0,1:T(8,128)}, u32[]{:S(2)}) copy-start(f32[32,3,128]{2,0,1:T(8,128)} %param.8) | copy-start | bytes 147460
  27.4 4.6 %copy-start.5 = (f32[32,3,128]{2,0,1:T(8,128)S(1)}, f32[32,3,128]{2,0,1:T(8,128)}, u32[]{:S(2)}) copy-start(f32[32,3,128]{2,0,1:T(8,128)} %param.9) | copy-start | bytes 147460
  27.4 10.2 %copy-start.9 = (s32[32,2]{0,1:T(2,128)S(1)}, s32[32,2]{0,1:T(2,128)}, u32[]{:S(2)}) copy-start(s32[32,2]{0,1:T(2,128)} %param.15) | copy-start | bytes 772
  27.4 10.3 %copy-start.8 = (f32[32,2,128]{2,1,0:T(2,128)S(1)}, f32[32,2,128]{2,1,0:T(2,128)}, u32[]{:S(2)}) copy-start(f32[32,2,128]{2,1,0:T(2,128)} %param.11) | copy-start | bytes 98308
  27.4 31.4 %all-to-all-start.1 = ((f32[128,7,4,128]{3,2,1,0:T(4,128)}), f32[128,7,4,128]{3,2,1,0:T(4,128)S(1)}, u32[]{:S(2)}, u32[]{:S(2)}) async-start(f32[128,7,4,128]{3,2,1,0:T(4,128)} %bitcast.22), calls=%async_computation.1 | async-start | bytes 3670016 | tf_op jit(solution)/shard_map/all_to_all | solution.py:393
  32.1 18.3 %collective-permute-start = (f32[4,4,128]{2,1,0:T(4,128)S(1)}, f32[4,4,128]{2,1,0:T(4,128)S(1)}, u32[]{:S(2)}, u32[]{:S(2)}) collective-permute-start(f32[4,4,128]{2,1,0:T(4,128)S(1)} %get-tuple-element.17), channel_id=1, source_target_pairs={{0,16},{16,32},{32,48},{48,64},{64,80},{80,96},{96,112},{1,17},{17... | collective-permute-start | bytes 24584 | tf_op jit(solution)/shard_map/ppermute | solution.py:372
  35.7 18.0 %collective-permute-start.1 = (f32[4,4,128]{2,1,0:T(4,128)S(1)}, f32[4,4,128]{2,1,0:T(4,128)S(1)}, u32[]{:S(2)}, u32[]{:S(2)}) collective-permute-start(f32[4,4,128]{2,1,0:T(4,128)S(1)} %get-tuple-element.16), channel_id=1, source_target_pairs={{16,0},{32,16},{48,32},{64,48},{80,64},{96,80},{112,96},{17,1},{33... | collective-permute-start | bytes 24584 | tf_op jit(solution)/shard_map/ppermute | solution.py:373
  78.1 0.9 copy-start.3
  78.9 25.4 %all-to-all-start.2 = ((f32[128,3,4,128]{3,2,1,0:T(4,128)}), f32[128,3,4,128]{3,2,1,0:T(4,128)S(1)}, u32[]{:S(2)}, u32[]{:S(2)}) async-start(f32[128,3,4,128]{3,2,1,0:T(4,128)} %bitcast.31), calls=%async_computation.2 | async-start | bytes 1572864 | tf_op jit(solution)/shard_map/all_to_all | solution.py:409

commit v3 on v2

--- a/solution.py
+++ b/solution.py
@@ -39,10 +39,18 @@
     return lax.dot_general(a, b, dims, preferred_element_type=F32)
 
 
-def plan_kernel(owner_ref, local_ref, ask_ref, start_ref, rows, *, cap):
+def plan_kernel(owner_hbm, local_hbm, ask_ref, start_ref, owner_ref, local_ref, rows, sem, *, cap):
+    copies = [
+        pltpu.make_async_copy(owner_hbm, owner_ref, sem.at[0]),
+        pltpu.make_async_copy(local_hbm, local_ref, sem.at[1]),
+    ]
+    for c in copies:
+        c.start()
     fanout, blocks = local_ref.shape
     devices, width = ask_ref.shape
     total = fanout * blocks
+    for c in copies:
+        c.wait()
     for k in range(fanout):
         cols = pl.ds(k * blocks, blocks)
         rows[0:1, cols] = owner_ref[k]
@@ -66,35 +74,41 @@
     start_ref[1:2, :] = owner * (cap * 3) + place
 
 
-def provide_kernel(ask_ref, pos_ref, disp_ref, weight_ref, out_ref, wide, *, cap):
+def provide_kernel(ask_ref, data_ref, out_hbm, wide, out, sem, *, cap):
     devices = ask_ref.shape[0]
-    blocks, lanes = weight_ref.shape
-    depth = 3 * blocks
-    cols = []
-    for c in range(ROWS):
-        x = weight_ref[...] if c == 6 else (pos_ref if c < 3 else disp_ref)[c % 3]
-        cols.append(jnp.concatenate(parts(x, 3), axis=0).astype(BF16))
-    data = jnp.concatenate(cols, axis=1)
+    depth = data_ref.shape[0]
+    lanes = data_ref.shape[1] // ROWS
+    blocks = depth // 3
     for s in range(cap):
         wide[pl.ds(s, devices, stride=cap), :] = jnp.broadcast_to(
             ask_ref[:, s : s + 1], (devices, lanes)
         )
     step = 64
     local = lax.broadcasted_iota(jnp.int32, (step, depth), 1) % blocks
+    copies = []
     for i in range(devices * cap // step):
         hot = (wide[pl.ds(i * step, step), 0:depth] == local).astype(F32).astype(BF16)
-        got = mm(hot, data, NN)
+        got = mm(hot, data_ref[...], NN)
         for j in range(step // cap):
             r = i * (step // cap) + j
             for c in range(ROWS):
-                out_ref[pl.ds((r * ROWS + c) * cap, cap), :] = got[
+                out[pl.ds((r * ROWS + c) * cap, cap), :] = got[
                     j * cap : (j + 1) * cap, c * lanes : (c + 1) * lanes
                 ]
-
-
-def own_kernel(pos_ref, at_ref, centre_ref, side):
+        if i % 2:
+            rows = pl.ds((i - 1) * step * ROWS, 2 * step * ROWS)
+            copies.append(pltpu.make_async_copy(out.at[rows], out_hbm.at[rows], sem.at[i // 2]))
+            copies[-1].start()
+    for c in copies:
+        c.wait()
+
+
+def own_kernel(pos_ref, disp_ref, weight_ref, at_ref, centre_ref, data_ref, side):
     _, blocks, lanes = pos_ref.shape
     inv = 1.0 / SUPPORT_SQ
+    for c in range(ROWS):
+        x = weight_ref[...] if c == 6 else (pos_ref if c < 3 else disp_ref)[c % 3]
+        data_ref[:, c * lanes : (c + 1) * lanes] = jnp.concatenate(parts(x, 3), axis=0).astype(BF16)
     side[...] = jnp.zeros_like(side)
     centre_ref[...] = jnp.zeros_like(centre_ref)
     ones = jnp.ones((GROUP, lanes), F32)
@@ -122,7 +136,9 @@
     lax.fori_loop(0, blocks // GROUP, group, 0)
 
 
-def contact_kernel(pos_ref, disp_ref, weight_ref, below_ref, above_ref, pick_ref, out_ref, wide, cur):
+def contact_kernel(
+    pos_ref, disp_ref, weight_ref, below_ref, above_ref, pick_ref, force_ref, out_ref, wide, cur
+):
     blocks, lanes = weight_ref.shape
     half = below_ref.shape[0]
     for c in range(3):
@@ -148,16 +164,17 @@
                 total = [total[c] + push * gap[c] for c in range(3)]
         scale = PENALTY * (weight_ref[pl.ds(b, 1), :] > 0).astype(F32)
         for c in range(3):
-            out_ref[c, pl.ds(b, 1), :] = scale * jnp.sum(total[c], axis=0, keepdims=True)
+            push = scale * jnp.sum(total[c], axis=0, keepdims=True)
+            out_ref[c, pl.ds(b, 1), :] = force_ref[c, pl.ds(b, 1), :] + push
         return 0
 
     lax.fori_loop(0, blocks, block, 0)
 
 
 def main_kernel(
-    start_ref, pos_ref, disp_ref, weight_ref, lame_ref, contact_ref, at_ref, centre_ref, got_ref,
-    piola_ref, force_ref, back_ref,
-    raw, far, b_all, f_all, k_all, ss, gs,
+    start_ref, pos_ref, disp_ref, weight_ref, lame_ref, at_ref, centre_ref, got_ref,
+    piola_ref, force_ref, back_hbm,
+    raw, far, b_all, f_all, k_all, ss, gs, back_ref, sem,
 ):
     blocks, lanes = weight_ref.shape
     fanout = far.shape[1]
@@ -191,7 +208,6 @@
             ).astype(BF16)
         return 0
 
-    lax.fori_loop(0, blocks, far_side, 0, unroll=2)
 
     def group(g, _):
         start = pl.multiple_of(g * GROUP, GROUP)
@@ -199,9 +215,10 @@
 
         def forward(q, _):
             b = start + q
+            far_side(b, 0)
             sums = jnp.zeros((64, 2 * lanes), F32)
-            for k in range(0, fanout, 2):
-                cols = pl.ds(k * lanes, 2 * lanes)
+            for k in range(0, fanout, 8):
+                cols = pl.ds(k * lanes, 8 * lanes)
                 near = jnp.maximum(mm(at_ref[b], b_all[b, :, cols], NN), 0.0)
                 near = near * near
                 hi = near.astype(BF16)
@@ -213,7 +230,7 @@
             ss[pl.ds(pl.multiple_of(q * 32, 32), 32), :] = sums[0:32] + sums[32:64]
             return 0
 
-        lax.fori_loop(0, GROUP, forward, 0, unroll=4)
+        lax.fori_loop(0, GROUP, forward, 0, unroll=8)
 
         def total(f):
             return ss[pl.ds(f, GROUP, stride=32), :]
@@ -252,7 +269,7 @@
                 scaled[a][c] = weight * v
         for a in range(3):
             own = sum(scaled[a][c] * column[c] for c in range(3))
-            force_ref[a, rows, :] = own + contact_ref[a, rows, :]
+            force_ref[a, rows, :] = own
             feats = scaled[a] + [sum(scaled[a][c] * here[c] for c in range(3))]
             for f, v in enumerate(feats):
                 h, l = parts(v, 2)
@@ -274,10 +291,13 @@
                     back_ref[pl.ds(first, 3, stride=cap), :] = v[0:3] + v[4:7]
             return 0
 
-        lax.fori_loop(0, GROUP, backward, 0, unroll=4)
+        lax.fori_loop(0, GROUP, backward, 0, unroll=8)
         return 0
 
     lax.fori_loop(0, blocks // GROUP, group, 0)
+    copy = pltpu.make_async_copy(back_ref, back_hbm, sem)
+    copy.start()
+    copy.wait()
 
 
 def returned_kernel(code_ref, got_ref, force_ref, out_ref):
@@ -296,23 +316,24 @@
 
 
 SMEM = pl.BlockSpec(memory_space=pltpu.SMEM)
-
-
-def call(body, name, out, in_specs, scratch=(), mib=8, flops=1_000_000, size=1_000_000):
+ANY = pl.BlockSpec(memory_space=pl.ANY)
+
+
+def call(body, name, out, in_specs, scratch=(), kib=8192, flops=1_000_000, size=1_000_000, out_any=False):
     many = isinstance(out, tuple)
     return pl.pallas_call(
         body,
         out_shape=out,
         in_specs=in_specs,
-        out_specs=tuple(vmem(len(out))) if many else vmem(1)[0],
+        out_specs=(tuple(vmem(len(out) - out_any) + [ANY] * out_any) if many else ANY if out_any else vmem(1)[0]),
         scratch_shapes=list(scratch),
-        compiler_params=pltpu.CompilerParams(vmem_limit_bytes=mib * 2**20),
+        compiler_params=pltpu.CompilerParams(vmem_limit_bytes=kib * 2**10),
         cost_estimate=pl.CostEstimate(flops=flops, bytes_accessed=size, transcendentals=0),
         name=name,
     )
 
 
-def main_call(start, pos_t, disp_t, weight, lame_t, contact, at, centre, got):
+def main_call(start, pos_t, disp_t, weight, lame_t, at, centre, got):
     blocks, lanes = weight.shape
     fanout = start.shape[1] // blocks
     wide = fanout * lanes
@@ -325,7 +346,7 @@
             jax.ShapeDtypeStruct((3, blocks, lanes), F32),
             jax.ShapeDtypeStruct((back, lanes), F32),
         ),
-        [SMEM] + vmem(8),
+        [SMEM] + vmem(7),
         [
             pltpu.VMEM((fanout, 8, lanes), F32),
             pltpu.VMEM((blocks, fanout, 8, lanes), F32),
@@ -334,11 +355,14 @@
             pltpu.VMEM((GROUP, 2 * lanes, wide), BF16),
             pltpu.VMEM((GROUP * 32, lanes), F32),
             pltpu.VMEM((GROUP * 32, lanes), F32),
+            pltpu.VMEM((back, lanes), F32),
+            pltpu.SemaphoreType.DMA,
         ],
-        mib=28,
+        out_any=True,
+        kib=28672,
         flops=60_000_000,
         size=4_000_000,
-    )(start, pos_t, disp_t, weight, lame_t, contact, at, centre, got)
+    )(start, pos_t, disp_t, weight, lame_t, at, centre, got)
 
 
 def per_device(ref_pos, disp, volume, lame, pad_count, nbr_owner, nbr_local, contact_block):
@@ -355,8 +379,14 @@
         lambda *refs: plan_kernel(*refs, cap=cap),
         "plan",
         (shape((devices, 16), jnp.int32), shape((2, total), jnp.int32)),
-        vmem(2),
-        [pltpu.VMEM((8, total), jnp.int32)],
+        [ANY] * 2,
+        [
+            pltpu.VMEM((fanout, 1, blocks), jnp.int32),
+            pltpu.VMEM((fanout, blocks), jnp.int32),
+            pltpu.VMEM((8, total), jnp.int32),
+            pltpu.SemaphoreType.DMA((2,)),
+        ],
+        kib=65472,
     )(jnp.transpose(nbr_owner, (1, 2, 0)), jnp.transpose(nbr_local))
     asked = lax.all_to_all(ask, AXES, split_axis=0, concat_axis=0, tiled=True)
 
@@ -375,40 +405,47 @@
     row = contact_block // blocks // deep
     pick = jnp.where(row < lax.axis_index("gx"), local - (blocks - SH), SH + local)
 
-    at, centre = call(
+    at, centre, data = call(
         own_kernel,
         "own",
-        (shape((blocks, lanes, SIDE), BF16), shape((blocks * 8, lanes), F32)),
-        vmem(1),
+        (
+            shape((blocks, lanes, SIDE), BF16),
+            shape((blocks * 8, lanes), F32),
+            shape((3 * blocks, ROWS * lanes), BF16),
+        ),
+        vmem(3),
         [pltpu.VMEM((GROUP * SIDE, lanes), F32)],
-    )(pos_t)
+    )(pos_t, disp_t, weight)
 
     picked = call(
         lambda *refs: provide_kernel(*refs, cap=cap),
         "provide",
         shape((devices * cap * ROWS, lanes), F32),
-        vmem(4),
-        [pltpu.VMEM((devices * cap, lanes), jnp.int32)],
-    )(asked, pos_t, disp_t, weight)
+        vmem(2),
+        [
+            pltpu.VMEM((devices * cap, lanes), jnp.int32),
+            pltpu.VMEM((devices * cap * ROWS, lanes), F32),
+            pltpu.SemaphoreType.DMA((devices * cap // 128,)),
+        ],
+        out_any=True,
+        kib=64000,
+    )(asked, data)
     got = lax.all_to_all(
         picked.reshape(devices, ROWS, cap, lanes), AXES, split_axis=0, concat_axis=0, tiled=True
     ).reshape(devices * cap * ROWS, lanes)
 
-    contact = call(
+    piola, force, back = main_call(start, pos_t, disp_t, weight, lame_t, at, centre, got)
+    received = lax.all_to_all(
+        back.reshape(devices, 3, cap, lanes), AXES, split_axis=0, concat_axis=0, tiled=True
+    )
+    force = call(
         contact_kernel,
         "contact",
         shape((3, blocks, lanes), F32),
-        vmem(5) + [SMEM],
+        vmem(5) + [SMEM] + vmem(1),
         [pltpu.VMEM((2 * SH, 4, lanes, lanes), F32), pltpu.VMEM((3, blocks, lanes), F32)],
         flops=20_000_000,
-    )(pos_t, disp_t, weight, below, above, pick)
-
-    piola, force, back = main_call(
-        start, pos_t, disp_t, weight, lame_t, contact, at, centre, got
-    )
-    received = lax.all_to_all(
-        back.reshape(devices, 3, cap, lanes), AXES, split_axis=0, concat_axis=0, tiled=True
-    )
+    )(pos_t, disp_t, weight, below, above, pick, force)
     ids = asked[:, None, 0:cap]
     code = jnp.where(ids >= 0, ids + blocks * jnp.arange(3)[None, :, None], -1).reshape(1, -1)
     force = call(returned_kernel, "returned", shape((3, blocks, lanes), F32), vmem(3))(

time: 106 us -> 96.1 us (0.907)
  starting transfers between devices: 30.4 us -> 26.8 us
  Pallas kernels: 27.6 us -> 25.1 us
  waiting for transfers between devices: 39.4 us -> 37 us
  local copies, waits for them, and re-layouts: 5.42 us -> 4.12 us
    all_to_all x1, waiting for transfers between devices: 0.19 us -> 21 us  [per_device(): lax.all_to_all(picked.reshape(devices, ROWS, cap, lanes), AXES, split_axi...]
    ppermute x1, waiting for transfers between devices: 11.7 us -> 0.01 us  [per_device(): below = lax.ppermute(surface[blocks - SH:], 'gx', up)]
    pallas_call x1, Pallas kernels: 19.2 us -> 13.7 us  [main_call(): call(main_kernel, 'pairs', (jax.ShapeDtypeStruct((9, blocks, lanes), F32)...]
    all_to_all x1, waiting for transfers between devices: 16.1 us -> 11.2 us  [per_device(): lax.all_to_all(back.reshape(devices, 3, cap, lanes), AXES, split_axis=0,...]
    all_to_all x1, starting transfers between devices: 8.91 us -> 4.89 us  [per_device(): lax.all_to_all(back.reshape(devices, 3, cap, lanes), AXES, split_axis=0,...]
    all_to_all x1, waiting for transfers between devices: 8.08 us -> 4.81 us  [per_device(): asked = lax.all_to_all(ask, AXES, split_axis=0, concat_axis=0, tiled=True)]
    ppermute x1, waiting for transfers between devices: 3.27 us -> 0.01 us  [per_device(): above = lax.ppermute(surface[:SH], 'gx', down)]
    pallas_call x1, Pallas kernels: 0.46 us -> 2.54 us  [per_device(): call(lambda *refs: provide_kernel(*refs, cap=cap), 'provide', shape((devi...]
  transfers between devices with their start and end apart: 5 -> 5, of which waited for: 5 -> 3; matrix products, arithmetic and copies ran while one was open for 2% -> 2% of each run, Pallas kernels for 6% -> 21%
where the time goes in v3:
time: 96.1 us; the launch traced here: 95.6 us
  waiting for transfers between devices  37 us (39%)
  starting transfers between devices  26.8 us (28%)
  Pallas kernels  25.1 us (26%)
  local copies, waits for them, and re-layouts  4.12 us (4%)
  other arithmetic  1.67 us (2%)
    all_to_all x1, waiting for transfers between devices, per_device(): lax.all_to_all(picked.reshape(devices, ROWS, cap, lanes), AXES, split_axi...  21 us
    pallas_call x1, Pallas kernels, main_call(): call(main_kernel, 'pairs', (jax.ShapeDtypeStruct((9, blocks, lanes), F32)...  13.7 us
    all_to_all x1, starting transfers between devices, per_device(): asked = lax.all_to_all(ask, AXES, split_axis=0, concat_axis=0, tiled=True)  11.5 us
    all_to_all x1, waiting for transfers between devices, per_device(): lax.all_to_all(back.reshape(devices, 3, cap, lanes), AXES, split_axis=0,...  11.2 us
    pallas_call x1, Pallas kernels, per_device(): call(contact_kernel, 'contact', shape((3, blocks, lanes), F32), vmem(5) +...  5.03 us
    all_to_all x1, starting transfers between devices, per_device(): lax.all_to_all(picked.reshape(devices, ROWS, cap, lanes), AXES, split_axi...  4.96 us
    all_to_all x1, starting transfers between devices, per_device(): lax.all_to_all(back.reshape(devices, 3, cap, lanes), AXES, split_axis=0,...  4.89 us
    all_to_all x1, waiting for transfers between devices, per_device(): asked = lax.all_to_all(ask, AXES, split_axis=0, concat_axis=0, tiled=True)  4.81 us
  transfers between devices with their start and end apart: 5, of which 3 were waited for; matrix products, arithmetic and copies ran while one was open for 2% of the time, Pallas kernels for 21%

profile of v3, /device:TPU:1, one launch (start us, length us, event | category | flops | bytes accessed | tf_op | source)
XLA Modules:
  0.0 95.6 jit_solution(12783915264056858095)
XLA Ops:
  0.6 1.8 %plan.1 = (s32[128,16]{1,0:T(8,128)}, s32[2,256]{1,0:T(2,128)}) custom-call(s32[8,1,32]{2,1,0:T(1,128)} %bitcast.36, s32[8,32]{1,0:T(8,128)} %bitcast.37), custom_call_target="tpu_custom_call" | custom-call | flops 1000000 | bytes 1000000 | tf_op jit(solution)/shard_map/plan/pallas_call | solution.py:378
  2.4 11.5 %all-to-all-start = ((s32[128,1,16]{2,1,0:T(1,128)}), s32[128,1,16]{2,1,0:T(1,128)S(1)}, u32[]{:S(2)}, u32[]{:S(2)}) async-start(s32[128,1,16]{2,1,0:T(1,128)} %bitcast.34), calls=%async_computation | async-start | bytes 131072 | tf_op jit(solution)/shard_map/all_to_all | solution.py:391
  13.9 0.7 broadcast_subtract_fusion
  14.6 0.8 fusion.2.weight_ref
  15.4 0.0 copy-start.1
  15.4 0.8 copy-done.1
  16.2 0.0 copy-start.3
  16.2 0.8 copy-done.3
  17.0 1.0 %own.1 = (bf16[32,128,48]{2,1,0:T(8,128)(2,1)S(1)}, f32[256,128]{1,0:T(8,128)S(1)}, bf16[96,896]{1,0:T(8,128)(2,1)S(1)}) custom-call(f32[3,32,128]{2,1,0:T(8,128)S(1)} %bitcast.22, f32[3,32,128]{2,1,0:T(8,128)S(1)} %bitcast.25, f32[32,128]{1,0:T(8,128)S(1)} %fusion.2.weight_ref), custom_call_target="tpu_custom_call" | custom-call | flops 1000000 | bytes 1000000 | tf_op jit(solution)/shard_map/own/pallas_call | solution.py:408
  18.0 0.0 copy-start.5
  18.0 0.7 copy-done.5
  18.6 4.8 %all-to-all-done = s32[128,1,16]{2,1,0:T(1,128)S(1)} async-done(((s32[128,1,16]{2,1,0:T(1,128)}), s32[128,1,16]{2,1,0:T(1,128)S(1)}, u32[]{:S(2)}, u32[]{:S(2)}) %all-to-all-start) | async-done | bytes 8224 | tf_op jit(solution)/shard_map/all_to_all | solution.py:391
  23.5 0.0 copy-start.7
  23.5 0.6 copy-done.7
  24.1 2.5 %provide.1 = f32[3584,128]{1,0:T(8,128)} custom-call(s32[128,16]{1,0:T(8,128)} %bitcast.31, bf16[96,896]{1,0:T(8,128)(2,1)} %copy-done.5), custom_call_target="tpu_custom_call" | custom-call | flops 1000000 | bytes 1000000 | tf_op jit(solution)/shard_map/provide/pallas_call | solution.py:420
  26.6 0.0 copy-start.2
  26.6 0.0 copy-start.4
  26.7 0.0 copy-start.9
  26.7 0.0 copy-start.10
  26.7 0.0 copy-start.6
  26.7 5.0 %all-to-all-start.1 = ((f32[128,7,4,128]{3,2,1,0:T(4,128)}), f32[128,7,4,128]{3,2,1,0:T(4,128)S(1)}, u32[]{:S(2)}, u32[]{:S(2)}) async-start(f32[128,7,4,128]{3,2,1,0:T(4,128)} %bitcast.30), calls=%async_computation.1 | async-start | bytes 3670016 | tf_op jit(solution)/shard_map/all_to_all | solution.py:433
  31.7 0.0 copy-done.2
  31.7 0.0 copy-done.4
  31.8 3.5 %collective-permute-start = (f32[4,4,128]{2,1,0:T(4,128)S(1)}, f32[4,4,128]{2,1,0:T(4,128)S(1)}, u32[]{:S(2)}, u32[]{:S(2)}) collective-permute-start(f32[4,4,128]{2,1,0:T(4,128)S(1)} %get-tuple-element.19), channel_id=1, source_target_pairs={{0,16},{16,32},{32,48},{48,64},{64,80},{80,96},{96,112},{1,17},{17... | collective-permute-start | bytes 24584 | tf_op jit(solution)/shard_map/ppermute | solution.py:402
  35.3 1.9 %collective-permute-start.1 = (f32[4,4,128]{2,1,0:T(4,128)S(1)}, f32[4,4,128]{2,1,0:T(4,128)S(1)}, u32[]{:S(2)}, u32[]{:S(2)}) collective-permute-start(f32[4,4,128]{2,1,0:T(4,128)S(1)} %get-tuple-element.18), channel_id=1, source_target_pairs={{16,0},{32,16},{48,32},{64,48},{80,64},{96,80},{112,96},{17,1},{33... | collective-permute-start | bytes 24584 | tf_op jit(solution)/shard_map/ppermute | solution.py:403
  37.2 0.0 copy-done.9
  37.3 0.0 copy-done.10
  37.3 0.1 copy.35
  37.4 21.0 %all-to-all-done.1 = f32[128,7,4,128]{3,2,1,0:T(4,128)S(1)} async-done(((f32[128,7,4,128]{3,2,1,0:T(4,128)}), f32[128,7,4,128]{3,2,1,0:T(4,128)S(1)}, u32[]{:S(2)}, u32[]{:S(2)}) %all-to-all-start.1) | async-done | bytes 1835040 | tf_op jit(solution)/shard_map/all_to_all | solution.py:433
  58.4 0.0 copy-done.6
  58.4 0.0 copy-start.8
  58.4 13.7 %pairs.1 = (f32[9,32,128]{2,1,0:T(8,128)}, f32[3,32,128]{2,1,0:T(8,128)S(1)}, f32[1536,128]{1,0:T(8,128)S(1)}) custom-call(s32[2,256]{1,0:T(2,128)S(1)} %copy-done.6, f32[3,32,128]{2,1,0:T(8,128)S(1)} %bitcast.23, f32[3,32,128]{2,1,0:T(8,128)S(1)} %bitcast.26, f32[32,128]{1,0:T(8,128)S(1)} %fusion.2.weight_ref, f32[2,32,128]{2,1,0:T(8,128)S(1)} %bitcast.29, ...), custom_call_target="tpu_custom_call" | custom-call | flops 60000000 | bytes 4000000 | tf_op jit(solution)/shard_map/pairs/pallas_call | solution.py:341
  72.2 0.0 copy-start
  72.2 0.9 copy-done
  73.0 4.9 %all-to-all-start.2 = ((f32[128,3,4,128]{3,2,1,0:T(4,128)}), f32[128,3,4,128]{3,2,1,0:T(4,128)S(1)}, u32[]{:S(2)}, u32[]{:S(2)}) async-start(f32[128,3,4,128]{3,2,1,0:T(4,128)} %bitcast.21), calls=%async_computation.2 | async-start | bytes 1572864 | tf_op jit(solution)/shard_map/all_to_all | solution.py:438
  78.0 0.0 copy-done.8
  78.0 0.1 add_select_fusion
  78.2 0.2 select_n.33.code_ref
  78.4 0.0 collective-permute-done.below_ref
  78.4 0.0 collective-permute-done.1.above_ref
  78.4 5.0 %contact.1.force_ref = f32[3,32,128]{2,1,0:T(8,128)S(1)} custom-call(f32[3,32,128]{2,1,0:T(8,128)S(1)} %bitcast.24, f32[3,32,128]{2,1,0:T(8,128)S(1)} %bitcast.27, f32[32,128]{1,0:T(8,128)S(1)} %fusion.2.weight_ref, f32[4,4,128]{2,1,0:T(4,128)S(1)} %collective-permute-done.below_ref, f32[4,4,128]{2,1,0:T(4,128)S(1)} %collective-permute-done.1.above_ref, ...), custom_call_target="tpu_custom_call" | custom-call | flops 20000000 | bytes 1000000 | tf_op jit(solution)/shard_map/contact/pallas_call | solution.py:441
  83.4 11.2 %all-to-all-done.2 = f32[128,3,4,128]{3,2,1,0:T(4,128)S(1)} async-done(((f32[128,3,4,128]{3,2,1,0:T(4,128)}), f32[128,3,4,128]{3,2,1,0:T(4,128)S(1)}, u32[]{:S(2)}, u32[]{:S(2)}) %all-to-all-start.2) | async-done | bytes 786464 | tf_op jit(solution)/shard_map/all_to_all | solution.py:438
  94.6 1.0 %returned.1 = f32[3,32,128]{2,1,0:T(8,128)} custom-call(s32[1,1536]{1,0:T(1,128)S(1)} %select_n.33.code_ref, f32[1536,128]{1,0:T(8,128)S(1)} %bitcast.20, f32[3,32,128]{2,1,0:T(8,128)S(1)} %contact.1.force_ref), custom_call_target="tpu_custom_call" | custom-call | flops 1000000 | bytes 1000000 | tf_op jit(solution)/shard_map/returned/pallas_call | solution.py:451
  (7 shorter events, 0.1 us)
Async XLA Ops:
  2.4 21.0 %all-to-all-start = ((s32[128,1,16]{2,1,0:T(1,128)}), s32[128,1,16]{2,1,0:T(1,128)S(1)}, u32[]{:S(2)}, u32[]{:S(2)}) async-start(s32[128,1,16]{2,1,0:T(1,128)} %bitcast.34), calls=%async_computation | async-start | bytes 131072 | tf_op jit(solution)/shard_map/all_to_all | solution.py:391
  15.4 0.8 copy-start.1
  16.2 0.8 copy-start.3
  18.0 0.7 copy-start.5
  23.5 0.6 copy-start.7
  26.6 5.0 %copy-start.2 = (f32[32,3,128]{2,0,1:T(8,128)S(1)}, f32[32,3,128]{2,0,1:T(8,128)}, u32[]{:S(2)}) copy-start(f32[32,3,128]{2,0,1:T(8,128)} %param.8) | copy-start | bytes 147460
  26.6 5.0 %copy-start.4 = (f32[32,3,128]{2,0,1:T(8,128)S(1)}, f32[32,3,128]{2,0,1:T(8,128)}, u32[]{:S(2)}) copy-start(f32[32,3,128]{2,0,1:T(8,128)} %param.9) | copy-start | bytes 147460
  26.7 10.6 %copy-start.9 = (f32[32,2,128]{2,1,0:T(2,128)S(1)}, f32[32,2,128]{2,1,0:T(2,128)}, u32[]{:S(2)}) copy-start(f32[32,2,128]{2,1,0:T(2,128)} %param.11) | copy-start | bytes 98308
  26.7 10.6 %copy-start.10 = (s32[32,2]{0,1:T(2,128)S(1)}, s32[32,2]{0,1:T(2,128)}, u32[]{:S(2)}) copy-start(s32[32,2]{0,1:T(2,128)} %param.15) | copy-start | bytes 772
  26.7 31.7 %copy-start.6 = (s32[2,256]{1,0:T(2,128)S(1)}, s32[2,256]{1,0:T(2,128)}, u32[]{:S(2)}) copy-start(s32[2,256]{1,0:T(2,128)} %get-tuple-element.11.start_ref) | copy-start | bytes 6148
  26.7 31.7 %all-to-all-start.1 = ((f32[128,7,4,128]{3,2,1,0:T(4,128)}), f32[128,7,4,128]{3,2,1,0:T(4,128)S(1)}, u32[]{:S(2)}, u32[]{:S(2)}) async-start(f32[128,7,4,128]{3,2,1,0:T(4,128)} %bitcast.30), calls=%async_computation.1 | async-start | bytes 3670016 | tf_op jit(solution)/shard_map/all_to_all | solution.py:433
  31.8 46.6 %collective-permute-start = (f32[4,4,128]{2,1,0:T(4,128)S(1)}, f32[4,4,128]{2,1,0:T(4,128)S(1)}, u32[]{:S(2)}, u32[]{:S(2)}) collective-permute-start(f32[4,4,128]{2,1,0:T(4,128)S(1)} %get-tuple-element.19), channel_id=1, source_target_pairs={{0,16},{16,32},{32,48},{48,64},{64,80},{80,96},{96,112},{1,17},{17... | collective-permute-start | bytes 24584 | tf_op jit(solution)/shard_map/ppermute | solution.py:402
  35.3 43.1 %collective-permute-start.1 = (f32[4,4,128]{2,1,0:T(4,128)S(1)}, f32[4,4,128]{2,1,0:T(4,128)S(1)}, u32[]{:S(2)}, u32[]{:S(2)}) collective-permute-start(f32[4,4,128]{2,1,0:T(4,128)S(1)} %get-tuple-element.18), channel_id=1, source_target_pairs={{16,0},{32,16},{48,32},{64,48},{80,64},{96,80},{112,96},{17,1},{33... | collective-permute-start | bytes 24584 | tf_op jit(solution)/shard_map/ppermute | solution.py:403
  58.4 19.6 %copy-start.8 = (s32[128,1,16]{2,1,0:T(1,128)S(1)}, s32[128,1,16]{2,1,0:T(1,128)}, u32[]{:S(2)}) copy-start(s32[128,1,16]{2,1,0:T(1,128)} %copy-done.7) | copy-start | bytes 24580
  72.2 0.9 copy-start
  73.0 21.5 %all-to-all-start.2 = ((f32[128,3,4,128]{3,2,1,0:T(4,128)}), f32[128,3,4,128]{3,2,1,0:T(4,128)S(1)}, u32[]{:S(2)}, u32[]{:S(2)}) async-start(f32[128,3,4,128]{3,2,1,0:T(4,128)} %bitcast.21), calls=%async_computation.2 | async-start | bytes 1572864 | tf_op jit(solution)/shard_map/all_to_all | solution.py:438

commit v4 on v3

--- a/solution.py
+++ b/solution.py
@@ -49,6 +49,10 @@
     fanout, blocks = local_ref.shape
     devices, width = ask_ref.shape
     total = fanout * blocks
+    earlier = lax.broadcasted_iota(jnp.int32, (total, total), 0) < lax.broadcasted_iota(
+        jnp.int32, (total, total), 1
+    )
+    earlier = earlier.astype(F32).astype(BF16)
     for c in copies:
         c.wait()
     for k in range(fanout):
@@ -59,10 +63,7 @@
     local = (rows[1:2, :] + 1).astype(F32)
     named = owner == lax.broadcasted_iota(jnp.int32, (devices, total), 0)
     hot = named.astype(F32)
-    earlier = lax.broadcasted_iota(jnp.int32, (total, total), 0) < lax.broadcasted_iota(
-        jnp.int32, (total, total), 1
-    )
-    rank = mm(hot.astype(BF16), earlier.astype(F32).astype(BF16), NN)
+    rank = mm(hot.astype(BF16), earlier, NN)
     lane = lax.broadcasted_iota(jnp.int32, (width, total), 0)
     ask = jnp.zeros((devices, width), F32)
     for s in range(cap):
@@ -74,7 +75,7 @@
     start_ref[1:2, :] = owner * (cap * 3) + place
 
 
-def provide_kernel(ask_ref, data_ref, out_hbm, wide, out, sem, *, cap):
+def provide_kernel(ask_ref, data_ref, out, wide, *, cap):
     devices = ask_ref.shape[0]
     depth = data_ref.shape[0]
     lanes = data_ref.shape[1] // ROWS
@@ -85,7 +86,6 @@
         )
     step = 64
     local = lax.broadcasted_iota(jnp.int32, (step, depth), 1) % blocks
-    copies = []
     for i in range(devices * cap // step):
         hot = (wide[pl.ds(i * step, step), 0:depth] == local).astype(F32).astype(BF16)
         got = mm(hot, data_ref[...], NN)
@@ -95,12 +95,6 @@
                 out[pl.ds((r * ROWS + c) * cap, cap), :] = got[
                     j * cap : (j + 1) * cap, c * lanes : (c + 1) * lanes
                 ]
-        if i % 2:
-            rows = pl.ds((i - 1) * step * ROWS, 2 * step * ROWS)
-            copies.append(pltpu.make_async_copy(out.at[rows], out_hbm.at[rows], sem.at[i // 2]))
-            copies[-1].start()
-    for c in copies:
-        c.wait()
 
 
 def own_kernel(pos_ref, disp_ref, weight_ref, at_ref, centre_ref, data_ref, side):
@@ -173,8 +167,8 @@
 
 def main_kernel(
     start_ref, pos_ref, disp_ref, weight_ref, lame_ref, at_ref, centre_ref, got_ref,
-    piola_ref, force_ref, back_hbm,
-    raw, far, b_all, f_all, k_all, ss, gs, back_ref, sem,
+    piola_ref, force_ref, back_ref,
+    raw, far, b_all, f_all, k_all, ss, gs,
 ):
     blocks, lanes = weight_ref.shape
     fanout = far.shape[1]
@@ -212,28 +206,29 @@
     def group(g, _):
         start = pl.multiple_of(g * GROUP, GROUP)
         rows = pl.ds(start, GROUP)
+        turn = g % 2
 
         def forward(q, _):
             b = start + q
             far_side(b, 0)
-            sums = jnp.zeros((64, 2 * lanes), F32)
-            for k in range(0, fanout, 8):
-                cols = pl.ds(k * lanes, 8 * lanes)
-                near = jnp.maximum(mm(at_ref[b], b_all[b, :, cols], NN), 0.0)
-                near = near * near
-                hi = near.astype(BF16)
-                lo = (near - hi.astype(F32)).astype(BF16)
-                both = jnp.concatenate([hi, lo], axis=0)
-                k_all[q, :, cols] = both
-                sums = sums + mm(f_all[b, :, cols], both, NT)
-            sums = sums[:, 0:lanes] + sums[:, lanes:]
-            ss[pl.ds(pl.multiple_of(q * 32, 32), 32), :] = sums[0:32] + sums[32:64]
+            near = jnp.maximum(mm(at_ref[b], b_all[b], NN), 0.0)
+            near = near * near
+            hi = near.astype(BF16)
+            lo = (near - hi.astype(F32)).astype(BF16)
+            k_all[turn * GROUP + q, 0:lanes, :] = hi
+            k_all[turn * GROUP + q, lanes:, :] = lo
+            feat = f_all[b]
+            sums = mm(
+                jnp.concatenate([hi, lo], axis=1), jnp.concatenate([feat, feat], axis=1), NT
+            )
+            sums = jnp.transpose(sums)
+            ss[turn, pl.ds(pl.multiple_of(q * 32, 32), 32), :] = sums[0:32] + sums[32:64]
             return 0
 
         lax.fori_loop(0, GROUP, forward, 0, unroll=8)
 
         def total(f):
-            return ss[pl.ds(f, GROUP, stride=32), :]
+            return ss[turn, pl.ds(f, GROUP, stride=32), :]
 
         mass = total(6)
         weight = weight_ref[rows, :]
@@ -273,20 +268,20 @@
             feats = scaled[a] + [sum(scaled[a][c] * here[c] for c in range(3))]
             for f, v in enumerate(feats):
                 h, l = parts(v, 2)
-                gs[pl.ds(f * 8 + a, GROUP, stride=32), :] = h
-                gs[pl.ds(f * 8 + 4 + a, GROUP, stride=32), :] = l
+                gs[turn, pl.ds(f * 8 + a, GROUP, stride=32), :] = h
+                gs[turn, pl.ds(f * 8 + 4 + a, GROUP, stride=32), :] = l
 
         def backward(q, _):
             b = start + q
-            feat = gs[pl.ds(pl.multiple_of(q * 32, 32), 32), :].astype(BF16)
+            feat = gs[turn, pl.ds(pl.multiple_of(q * 32, 32), 32), :].astype(BF16)
             feat = jnp.concatenate([feat, feat], axis=1)
             for k in range(0, fanout, 2):
-                sums = mm(feat, k_all[q, :, pl.ds(k * lanes, 2 * lanes)], NN)
+                sums = mm(feat, k_all[turn * GROUP + q, :, pl.ds(k * lanes, 2 * lanes)], NN)
                 for j in range(2):
-                    t = far[b, k + j]
                     back = [sums[8 * f : 8 * f + 8, j * lanes : (j + 1) * lanes] for f in range(4)]
-                    v = back[3] - sum(t[c : c + 1] * back[c] for c in range(3))
-                    v = (-coeff * t[6:7]) * v
+                    cast = [far[b, k + j, pl.ds(c, 8, stride=0), :] for c in (0, 1, 2, 6)]
+                    v = back[3] - sum(cast[c] * back[c] for c in range(3))
+                    v = (-coeff * cast[3]) * v
                     first = start_ref[1, (k + j) * blocks + b]
                     back_ref[pl.ds(first, 3, stride=cap), :] = v[0:3] + v[4:7]
             return 0
@@ -294,10 +289,7 @@
         lax.fori_loop(0, GROUP, backward, 0, unroll=8)
         return 0
 
-    lax.fori_loop(0, blocks // GROUP, group, 0)
-    copy = pltpu.make_async_copy(back_ref, back_hbm, sem)
-    copy.start()
-    copy.wait()
+    lax.fori_loop(0, blocks // GROUP, group, 0, unroll=4)
 
 
 def returned_kernel(code_ref, got_ref, force_ref, out_ref):
@@ -319,13 +311,13 @@
 ANY = pl.BlockSpec(memory_space=pl.ANY)
 
 
-def call(body, name, out, in_specs, scratch=(), kib=8192, flops=1_000_000, size=1_000_000, out_any=False):
+def call(body, name, out, in_specs, scratch=(), kib=8192, flops=1_000_000, size=1_000_000):
     many = isinstance(out, tuple)
     return pl.pallas_call(
         body,
         out_shape=out,
         in_specs=in_specs,
-        out_specs=(tuple(vmem(len(out) - out_any) + [ANY] * out_any) if many else ANY if out_any else vmem(1)[0]),
+        out_specs=tuple(vmem(len(out))) if many else vmem(1)[0],
         scratch_shapes=list(scratch),
         compiler_params=pltpu.CompilerParams(vmem_limit_bytes=kib * 2**10),
         cost_estimate=pl.CostEstimate(flops=flops, bytes_accessed=size, transcendentals=0),
@@ -352,14 +344,11 @@
             pltpu.VMEM((blocks, fanout, 8, lanes), F32),
             pltpu.VMEM((blocks, SIDE, wide), BF16),
             pltpu.VMEM((blocks, 64, wide), BF16),
-            pltpu.VMEM((GROUP, 2 * lanes, wide), BF16),
-            pltpu.VMEM((GROUP * 32, lanes), F32),
-            pltpu.VMEM((GROUP * 32, lanes), F32),
-            pltpu.VMEM((back, lanes), F32),
-            pltpu.SemaphoreType.DMA,
+            pltpu.VMEM((2 * GROUP, 2 * lanes, wide), BF16),
+            pltpu.VMEM((2, GROUP * 32, lanes), F32),
+            pltpu.VMEM((2, GROUP * 32, lanes), F32),
         ],
-        out_any=True,
-        kib=28672,
+        kib=36000,
         flops=60_000_000,
         size=4_000_000,
     )(start, pos_t, disp_t, weight, lame_t, at, centre, got)
@@ -422,13 +411,7 @@
         "provide",
         shape((devices * cap * ROWS, lanes), F32),
         vmem(2),
-        [
-            pltpu.VMEM((devices * cap, lanes), jnp.int32),
-            pltpu.VMEM((devices * cap * ROWS, lanes), F32),
-            pltpu.SemaphoreType.DMA((devices * cap // 128,)),
-        ],
-        out_any=True,
-        kib=64000,
+        [pltpu.VMEM((devices * cap, lanes), jnp.int32)],
     )(asked, data)
     got = lax.all_to_all(
         picked.reshape(devices, ROWS, cap, lanes), AXES, split_axis=0, concat_axis=0, tiled=True

time: 96.1 us -> 93.2 us (0.970)
  Pallas kernels: 25.1 us -> 21.9 us
    pallas_call x1, Pallas kernels: 2.54 us -> 0.47 us  [per_device(): call(lambda *refs: provide_kernel(*refs, cap=cap), 'provide', shape((devi...]
    pallas_call x1, Pallas kernels: 13.7 us -> 12.7 us  [main_call(): call(main_kernel, 'pairs', (jax.ShapeDtypeStruct((9, blocks, lanes), F32)...]
    unnamed x24 -> x20, local copies, waits for them, and re-layouts: 3.89 us -> 3.83 us
  transfers between devices with their start and end apart: 5 -> 5, of which waited for: 3 -> 3; matrix products, arithmetic and copies ran while one was open for 2% -> 2% of each run, Pallas kernels for 21% -> 20%
where the time goes in v4:
time: 93.2 us; the launch traced here: 92.7 us
  waiting for transfers between devices  37.6 us (40%)
  starting transfers between devices  26.6 us (29%)
  Pallas kernels  21.9 us (23%)
  local copies, waits for them, and re-layouts  4.06 us (4%)
  other arithmetic  1.67 us (2%)
    all_to_all x1, waiting for transfers between devices, per_device(): lax.all_to_all(picked.reshape(devices, ROWS, cap, lanes), AXES, split_axi...  21 us
    pallas_call x1, Pallas kernels, main_call(): call(main_kernel, 'pairs', (jax.ShapeDtypeStruct((9, blocks, lanes), F32)...  12.7 us
    all_to_all x1, starting transfers between devices, per_device(): asked = lax.all_to_all(ask, AXES, split_axis=0, concat_axis=0, tiled=True)  11.5 us
    all_to_all x1, waiting for transfers between devices, per_device(): lax.all_to_all(back.reshape(devices, 3, cap, lanes), AXES, split_axis=0,...  11.2 us
    all_to_all x1, waiting for transfers between devices, per_device(): asked = lax.all_to_all(ask, AXES, split_axis=0, concat_axis=0, tiled=True)  5.48 us
    pallas_call x1, Pallas kernels, per_device(): call(contact_kernel, 'contact', shape((3, blocks, lanes), F32), vmem(5) +...  5.03 us
    all_to_all x1, starting transfers between devices, per_device(): lax.all_to_all(back.reshape(devices, 3, cap, lanes), AXES, split_axis=0,...  4.88 us
    all_to_all x1, starting transfers between devices, per_device(): lax.all_to_all(picked.reshape(devices, ROWS, cap, lanes), AXES, split_axi...  4.55 us
  transfers between devices with their start and end apart: 5, of which 3 were waited for; matrix products, arithmetic and copies ran while one was open for 2% of the time, Pallas kernels for 20%

profile of v4, /device:TPU:1, one launch (start us, length us, event | category | flops | bytes accessed | tf_op | source)
XLA Modules:
  0.0 92.7 jit_solution(8577604554926058662)
XLA Ops:
  0.6 1.8 %plan.1 = (s32[128,16]{1,0:T(8,128)}, s32[2,256]{1,0:T(2,128)}) custom-call(s32[8,1,32]{2,1,0:T(1,128)} %bitcast.36, s32[8,32]{1,0:T(8,128)} %bitcast.37), custom_call_target="tpu_custom_call" | custom-call | flops 1000000 | bytes 1000000 | tf_op jit(solution)/shard_map/plan/pallas_call | solution.py:367
  2.4 11.5 %all-to-all-start = ((s32[128,1,16]{2,1,0:T(1,128)}), s32[128,1,16]{2,1,0:T(1,128)S(1)}, u32[]{:S(2)}, u32[]{:S(2)}) async-start(s32[128,1,16]{2,1,0:T(1,128)} %bitcast.34), calls=%async_computation | async-start | bytes 131072 | tf_op jit(solution)/shard_map/all_to_all | solution.py:380
  13.9 0.7 broadcast_subtract_fusion
  14.6 0.8 fusion.2.weight_ref
  15.4 0.0 copy-start.2
  15.4 0.8 copy-done.2
  16.2 0.0 copy-start.4
  16.2 0.8 copy-done.4
  17.0 1.0 %own.1 = (bf16[32,128,48]{2,1,0:T(8,128)(2,1)S(1)}, f32[256,128]{1,0:T(8,128)S(1)}, bf16[96,896]{1,0:T(8,128)(2,1)S(1)}) custom-call(f32[3,32,128]{2,1,0:T(8,128)S(1)} %bitcast.26, f32[3,32,128]{2,1,0:T(8,128)S(1)} %bitcast.29, f32[32,128]{1,0:T(8,128)S(1)} %fusion.2.weight_ref), custom_call_target="tpu_custom_call" | custom-call | flops 1000000 | bytes 1000000 | tf_op jit(solution)/shard_map/own/pallas_call | solution.py:397
  18.0 5.5 %all-to-all-done = s32[128,1,16]{2,1,0:T(1,128)S(1)} async-done(((s32[128,1,16]{2,1,0:T(1,128)}), s32[128,1,16]{2,1,0:T(1,128)S(1)}, u32[]{:S(2)}, u32[]{:S(2)}) %all-to-all-start) | async-done | bytes 8224 | tf_op jit(solution)/shard_map/all_to_all | solution.py:380
  23.5 0.5 provide.1
  23.9 0.0 copy-start
  23.9 1.2 %copy-done = f32[3584,128]{1,0:T(8,128)} copy-done((f32[3584,128]{1,0:T(8,128)}, f32[3584,128]{1,0:T(8,128)S(1)}, u32[]{:S(2)}) %copy-start) | copy-done | bytes 1835032
  25.2 0.0 copy-start.3
  25.2 0.0 copy-start.5
  25.2 0.0 copy-start.7
  25.2 0.0 copy-start.8
  25.2 0.0 copy-start.6
  25.2 4.6 %all-to-all-start.1 = ((f32[128,7,4,128]{3,2,1,0:T(4,128)}), f32[128,7,4,128]{3,2,1,0:T(4,128)S(1)}, u32[]{:S(2)}, u32[]{:S(2)}) async-start(f32[128,7,4,128]{3,2,1,0:T(4,128)} %bitcast.20), calls=%async_computation.1 | async-start | bytes 3670016 | tf_op jit(solution)/shard_map/all_to_all | solution.py:416
  29.8 0.0 copy-done.3
  29.8 0.0 copy-done.5
  29.9 3.5 %collective-permute-start = (f32[4,4,128]{2,1,0:T(4,128)S(1)}, f32[4,4,128]{2,1,0:T(4,128)S(1)}, u32[]{:S(2)}, u32[]{:S(2)}) collective-permute-start(f32[4,4,128]{2,1,0:T(4,128)S(1)} %get-tuple-element.19), channel_id=1, source_target_pairs={{0,16},{16,32},{32,48},{48,64},{64,80},{80,96},{96,112},{1,17},{17... | collective-permute-start | bytes 24584 | tf_op jit(solution)/shard_map/ppermute | solution.py:391
  33.4 2.1 %collective-permute-start.1 = (f32[4,4,128]{2,1,0:T(4,128)S(1)}, f32[4,4,128]{2,1,0:T(4,128)S(1)}, u32[]{:S(2)}, u32[]{:S(2)}) collective-permute-start(f32[4,4,128]{2,1,0:T(4,128)S(1)} %get-tuple-element.18), channel_id=1, source_target_pairs={{16,0},{32,16},{48,32},{64,48},{80,64},{96,80},{112,96},{17,1},{33... | collective-permute-start | bytes 24584 | tf_op jit(solution)/shard_map/ppermute | solution.py:392
  35.5 0.0 copy-done.7
  35.6 0.0 copy-done.8
  35.6 0.1 copy.35
  35.7 21.0 %all-to-all-done.1 = f32[128,7,4,128]{3,2,1,0:T(4,128)S(1)} async-done(((f32[128,7,4,128]{3,2,1,0:T(4,128)}), f32[128,7,4,128]{3,2,1,0:T(4,128)S(1)}, u32[]{:S(2)}, u32[]{:S(2)}) %all-to-all-start.1) | async-done | bytes 1835040 | tf_op jit(solution)/shard_map/all_to_all | solution.py:416
  56.6 0.0 copy-done.6
  56.6 12.7 %pairs.1 = (f32[9,32,128]{2,1,0:T(8,128)}, f32[3,32,128]{2,1,0:T(8,128)S(1)}, f32[1536,128]{1,0:T(8,128)S(1)}) custom-call(s32[2,256]{1,0:T(2,128)S(1)} %copy-done.6, f32[3,32,128]{2,1,0:T(8,128)S(1)} %bitcast.27, f32[3,32,128]{2,1,0:T(8,128)S(1)} %bitcast.30, f32[32,128]{1,0:T(8,128)S(1)} %fusion.2.weight_ref, f32[2,32,128]{2,1,0:T(8,128)S(1)} %bitcast.33, ...), custom_call_target="tpu_custom_call" | custom-call | flops 60000000 | bytes 4000000 | tf_op jit(solution)/shard_map/pairs/pallas_call | solution.py:333
  69.3 0.0 copy-start.1
  69.3 0.9 copy-done.1
  70.2 4.9 %all-to-all-start.2 = ((f32[128,3,4,128]{3,2,1,0:T(4,128)}), f32[128,3,4,128]{3,2,1,0:T(4,128)S(1)}, u32[]{:S(2)}, u32[]{:S(2)}) async-start(f32[128,3,4,128]{3,2,1,0:T(4,128)} %bitcast.25), calls=%async_computation.2 | async-start | bytes 1572864 | tf_op jit(solution)/shard_map/all_to_all | solution.py:421
  75.1 0.1 add_select_fusion
  75.3 0.2 select_n.33.code_ref
  75.5 0.0 collective-permute-done.below_ref
  75.5 0.0 collective-permute-done.1.above_ref
  75.5 5.0 %contact.1.force_ref = f32[3,32,128]{2,1,0:T(8,128)S(1)} custom-call(f32[3,32,128]{2,1,0:T(8,128)S(1)} %bitcast.28, f32[3,32,128]{2,1,0:T(8,128)S(1)} %bitcast.31, f32[32,128]{1,0:T(8,128)S(1)} %fusion.2.weight_ref, f32[4,4,128]{2,1,0:T(4,128)S(1)} %collective-permute-done.below_ref, f32[4,4,128]{2,1,0:T(4,128)S(1)} %collective-permute-done.1.above_ref, ...), custom_call_target="tpu_custom_call" | custom-call | flops 20000000 | bytes 1000000 | tf_op jit(solution)/shard_map/contact/pallas_call | solution.py:424
  80.5 11.2 %all-to-all-done.2 = f32[128,3,4,128]{3,2,1,0:T(4,128)S(1)} async-done(((f32[128,3,4,128]{3,2,1,0:T(4,128)}), f32[128,3,4,128]{3,2,1,0:T(4,128)S(1)}, u32[]{:S(2)}, u32[]{:S(2)}) %all-to-all-start.2) | async-done | bytes 786464 | tf_op jit(solution)/shard_map/all_to_all | solution.py:421
  91.7 1.0 %returned.1 = f32[3,32,128]{2,1,0:T(8,128)} custom-call(s32[1,1536]{1,0:T(1,128)S(1)} %select_n.33.code_ref, f32[1536,128]{1,0:T(8,128)S(1)} %bitcast.21, f32[3,32,128]{2,1,0:T(8,128)S(1)} %contact.1.force_ref), custom_call_target="tpu_custom_call" | custom-call | flops 1000000 | bytes 1000000 | tf_op jit(solution)/shard_map/returned/pallas_call | solution.py:434
  (7 shorter events, 0.1 us)
Async XLA Ops:
  2.4 21.0 %all-to-all-start = ((s32[128,1,16]{2,1,0:T(1,128)}), s32[128,1,16]{2,1,0:T(1,128)S(1)}, u32[]{:S(2)}, u32[]{:S(2)}) async-start(s32[128,1,16]{2,1,0:T(1,128)} %bitcast.34), calls=%async_computation | async-start | bytes 131072 | tf_op jit(solution)/shard_map/all_to_all | solution.py:380
  15.4 0.8 copy-start.2
  16.2 0.8 copy-start.4
  23.9 1.2 %copy-start = (f32[3584,128]{1,0:T(8,128)}, f32[3584,128]{1,0:T(8,128)S(1)}, u32[]{:S(2)}) copy-start(f32[3584,128]{1,0:T(8,128)S(1)} %provide.1) | copy-start | bytes 5505028
  25.2 4.6 %copy-start.3 = (f32[32,3,128]{2,0,1:T(8,128)S(1)}, f32[32,3,128]{2,0,1:T(8,128)}, u32[]{:S(2)}) copy-start(f32[32,3,128]{2,0,1:T(8,128)} %param.8) | copy-start | bytes 147460
  25.2 4.6 %copy-start.5 = (f32[32,3,128]{2,0,1:T(8,128)S(1)}, f32[32,3,128]{2,0,1:T(8,128)}, u32[]{:S(2)}) copy-start(f32[32,3,128]{2,0,1:T(8,128)} %param.9) | copy-start | bytes 147460
  25.2 10.4 %copy-start.7 = (f32[32,2,128]{2,1,0:T(2,128)S(1)}, f32[32,2,128]{2,1,0:T(2,128)}, u32[]{:S(2)}) copy-start(f32[32,2,128]{2,1,0:T(2,128)} %param.11) | copy-start | bytes 98308
  25.2 10.4 %copy-start.8 = (s32[32,2]{0,1:T(2,128)S(1)}, s32[32,2]{0,1:T(2,128)}, u32[]{:S(2)}) copy-start(s32[32,2]{0,1:T(2,128)} %param.15) | copy-start | bytes 772
  25.2 31.5 %copy-start.6 = (s32[2,256]{1,0:T(2,128)S(1)}, s32[2,256]{1,0:T(2,128)}, u32[]{:S(2)}) copy-start(s32[2,256]{1,0:T(2,128)} %get-tuple-element.11.start_ref) | copy-start | bytes 6148
  25.2 31.4 %all-to-all-start.1 = ((f32[128,7,4,128]{3,2,1,0:T(4,128)}), f32[128,7,4,128]{3,2,1,0:T(4,128)S(1)}, u32[]{:S(2)}, u32[]{:S(2)}) async-start(f32[128,7,4,128]{3,2,1,0:T(4,128)} %bitcast.20), calls=%async_computation.1 | async-start | bytes 3670016 | tf_op jit(solution)/shard_map/all_to_all | solution.py:416
  29.9 45.6 %collective-permute-start = (f32[4,4,128]{2,1,0:T(4,128)S(1)}, f32[4,4,128]{2,1,0:T(4,128)S(1)}, u32[]{:S(2)}, u32[]{:S(2)}) collective-permute-start(f32[4,4,128]{2,1,0:T(4,128)S(1)} %get-tuple-element.19), channel_id=1, source_target_pairs={{0,16},{16,32},{32,48},{48,64},{64,80},{80,96},{96,112},{1,17},{17... | collective-permute-start | bytes 24584 | tf_op jit(solution)/shard_map/ppermute | solution.py:391
  33.4 42.1 %collective-permute-start.1 = (f32[4,4,128]{2,1,0:T(4,128)S(1)}, f32[4,4,128]{2,1,0:T(4,128)S(1)}, u32[]{:S(2)}, u32[]{:S(2)}) collective-permute-start(f32[4,4,128]{2,1,0:T(4,128)S(1)} %get-tuple-element.18), channel_id=1, source_target_pairs={{16,0},{32,16},{48,32},{64,48},{80,64},{96,80},{112,96},{17,1},{33... | collective-permute-start | bytes 24584 | tf_op jit(solution)/shard_map/ppermute | solution.py:392
  69.3 0.9 copy-start.1
  70.2 21.5 %all-to-all-start.2 = ((f32[128,3,4,128]{3,2,1,0:T(4,128)}), f32[128,3,4,128]{3,2,1,0:T(4,128)S(1)}, u32[]{:S(2)}, u32[]{:S(2)}) async-start(f32[128,3,4,128]{3,2,1,0:T(4,128)} %bitcast.25), calls=%async_computation.2 | async-start | bytes 1572864 | tf_op jit(solution)/shard_map/all_to_all | solution.py:421

commit v5 on v4

--- a/solution.py
+++ b/solution.py
@@ -203,29 +203,26 @@
         return 0
 
 
-    def group(g, _):
-        start = pl.multiple_of(g * GROUP, GROUP)
-        rows = pl.ds(start, GROUP)
+    def forward(g, q):
         turn = g % 2
-
-        def forward(q, _):
-            b = start + q
-            far_side(b, 0)
-            near = jnp.maximum(mm(at_ref[b], b_all[b], NN), 0.0)
-            near = near * near
-            hi = near.astype(BF16)
-            lo = (near - hi.astype(F32)).astype(BF16)
-            k_all[turn * GROUP + q, 0:lanes, :] = hi
-            k_all[turn * GROUP + q, lanes:, :] = lo
-            feat = f_all[b]
-            sums = mm(
-                jnp.concatenate([hi, lo], axis=1), jnp.concatenate([feat, feat], axis=1), NT
-            )
-            sums = jnp.transpose(sums)
-            ss[turn, pl.ds(pl.multiple_of(q * 32, 32), 32), :] = sums[0:32] + sums[32:64]
-            return 0
-
-        lax.fori_loop(0, GROUP, forward, 0, unroll=8)
+        b = g * GROUP + q
+        far_side(b, 0)
+        near = jnp.maximum(mm(at_ref[b], b_all[b], NN), 0.0)
+        near = near * near
+        hi = near.astype(BF16)
+        lo = (near - hi.astype(F32)).astype(BF16)
+        k_all[turn * GROUP + q, 0:lanes, :] = hi
+        k_all[turn * GROUP + q, lanes:, :] = lo
+        feat = f_all[b]
+        sums = mm(
+            jnp.concatenate([hi, lo], axis=1), jnp.concatenate([feat, feat], axis=1), NT
+        )
+        sums = jnp.transpose(sums)
+        ss[turn, pl.ds(pl.multiple_of(q * 32, 32), 32), :] = sums[0:32] + sums[32:64]
+
+    def middle(g):
+        turn = g % 2
+        rows = pl.ds(pl.multiple_of(g * GROUP, GROUP), GROUP)
 
         def total(f):
             return ss[turn, pl.ds(f, GROUP, stride=32), :]
@@ -271,25 +268,44 @@
                 gs[turn, pl.ds(f * 8 + a, GROUP, stride=32), :] = h
                 gs[turn, pl.ds(f * 8 + 4 + a, GROUP, stride=32), :] = l
 
-        def backward(q, _):
-            b = start + q
-            feat = gs[turn, pl.ds(pl.multiple_of(q * 32, 32), 32), :].astype(BF16)
-            feat = jnp.concatenate([feat, feat], axis=1)
-            for k in range(0, fanout, 2):
-                sums = mm(feat, k_all[turn * GROUP + q, :, pl.ds(k * lanes, 2 * lanes)], NN)
-                for j in range(2):
-                    back = [sums[8 * f : 8 * f + 8, j * lanes : (j + 1) * lanes] for f in range(4)]
-                    cast = [far[b, k + j, pl.ds(c, 8, stride=0), :] for c in (0, 1, 2, 6)]
-                    v = back[3] - sum(cast[c] * back[c] for c in range(3))
-                    v = (-coeff * cast[3]) * v
-                    first = start_ref[1, (k + j) * blocks + b]
-                    back_ref[pl.ds(first, 3, stride=cap), :] = v[0:3] + v[4:7]
+    def backward(g, q):
+        turn = g % 2
+        b = g * GROUP + q
+        feat = gs[turn, pl.ds(pl.multiple_of(q * 32, 32), 32), :].astype(BF16)
+        feat = jnp.concatenate([feat, feat], axis=1)
+        for k in range(0, fanout, 2):
+            sums = mm(feat, k_all[turn * GROUP + q, :, pl.ds(k * lanes, 2 * lanes)], NN)
+            for j in range(2):
+                back = [sums[8 * f : 8 * f + 8, j * lanes : (j + 1) * lanes] for f in range(4)]
+                cast = [far[b, k + j, pl.ds(c, 8, stride=0), :] for c in (0, 1, 2, 6)]
+                v = back[3] - sum(cast[c] * back[c] for c in range(3))
+                v = (-coeff * cast[3]) * v
+                first = start_ref[1, (k + j) * blocks + b]
+                back_ref[pl.ds(first, 3, stride=cap), :] = v[0:3] + v[4:7]
+
+    def first(q, _):
+        forward(0, q)
+        return 0
+
+    def both(g, _):
+        def block(q, _):
+            forward(g, q)
+            backward(g - 1, q)
             return 0
 
-        lax.fori_loop(0, GROUP, backward, 0, unroll=8)
-        return 0
-
-    lax.fori_loop(0, blocks // GROUP, group, 0, unroll=4)
+        lax.fori_loop(0, GROUP, block, 0, unroll=GROUP)
+        middle(g)
+        return 0
+
+    def last(q, _):
+        backward(groups - 1, q)
+        return 0
+
+    groups = blocks // GROUP
+    lax.fori_loop(0, GROUP, first, 0, unroll=GROUP)
+    middle(0)
+    lax.fori_loop(1, groups, both, 0, unroll=3)
+    lax.fori_loop(0, GROUP, last, 0, unroll=GROUP)
 
 
 def returned_kernel(code_ref, got_ref, force_ref, out_ref):

time: 93.2 us -> 92.6 us (level)
  no operation moved by 1% of the time
where the time goes in v5:
time: 92.6 us; the launch traced here: 92 us
  waiting for transfers between devices  37.6 us (41%)
  starting transfers between devices  26.6 us (29%)
  Pallas kernels  21.3 us (23%)
  local copies, waits for them, and re-layouts  4.06 us (4%)
  other arithmetic  1.67 us (2%)
    all_to_all x1, waiting for transfers between devices, per_device(): lax.all_to_all(picked.reshape(devices, ROWS, cap, lanes), AXES, split_axi...  21 us
    pallas_call x1, Pallas kernels, main_call(): call(main_kernel, 'pairs', (jax.ShapeDtypeStruct((9, blocks, lanes), F32)...  12 us
    all_to_all x1, starting transfers between devices, per_device(): asked = lax.all_to_all(ask, AXES, split_axis=0, concat_axis=0, tiled=True)  11.5 us
    all_to_all x1, waiting for transfers between devices, per_device(): lax.all_to_all(back.reshape(devices, 3, cap, lanes), AXES, split_axis=0,...  11.2 us
    all_to_all x1, waiting for transfers between devices, per_device(): asked = lax.all_to_all(ask, AXES, split_axis=0, concat_axis=0, tiled=True)  5.48 us
    pallas_call x1, Pallas kernels, per_device(): call(contact_kernel, 'contact', shape((3, blocks, lanes), F32), vmem(5) +...  5.03 us
    all_to_all x1, starting transfers between devices, per_device(): lax.all_to_all(back.reshape(devices, 3, cap, lanes), AXES, split_axis=0,...  4.89 us
    all_to_all x1, starting transfers between devices, per_device(): lax.all_to_all(picked.reshape(devices, ROWS, cap, lanes), AXES, split_axi...  4.55 us
  transfers between devices with their start and end apart: 5, of which 3 were waited for; matrix products, arithmetic and copies ran while one was open for 2% of the time, Pallas kernels for 20%

profile of v5, /device:TPU:1, one launch (start us, length us, event | category | flops | bytes accessed | tf_op | source)
XLA Modules:
  0.0 92.0 jit_solution(5622685530807147136)
XLA Ops:
  0.6 1.8 %plan.1 = (s32[128,16]{1,0:T(8,128)}, s32[2,256]{1,0:T(2,128)}) custom-call(s32[8,1,32]{2,1,0:T(1,128)} %bitcast.36, s32[8,32]{1,0:T(8,128)} %bitcast.37), custom_call_target="tpu_custom_call" | custom-call | flops 1000000 | bytes 1000000 | tf_op jit(solution)/shard_map/plan/pallas_call | solution.py:383
  2.4 11.5 %all-to-all-start = ((s32[128,1,16]{2,1,0:T(1,128)}), s32[128,1,16]{2,1,0:T(1,128)S(1)}, u32[]{:S(2)}, u32[]{:S(2)}) async-start(s32[128,1,16]{2,1,0:T(1,128)} %bitcast.34), calls=%async_computation | async-start | bytes 131072 | tf_op jit(solution)/shard_map/all_to_all | solution.py:396
  13.9 0.7 broadcast_subtract_fusion
  14.6 0.8 fusion.2.weight_ref
  15.4 0.0 copy-start.2
  15.4 0.8 copy-done.2
  16.2 0.0 copy-start.4
  16.2 0.8 copy-done.4
  17.0 1.0 %own.1 = (bf16[32,128,48]{2,1,0:T(8,128)(2,1)S(1)}, f32[256,128]{1,0:T(8,128)S(1)}, bf16[96,896]{1,0:T(8,128)(2,1)S(1)}) custom-call(f32[3,32,128]{2,1,0:T(8,128)S(1)} %bitcast.26, f32[3,32,128]{2,1,0:T(8,128)S(1)} %bitcast.29, f32[32,128]{1,0:T(8,128)S(1)} %fusion.2.weight_ref), custom_call_target="tpu_custom_call" | custom-call | flops 1000000 | bytes 1000000 | tf_op jit(solution)/shard_map/own/pallas_call | solution.py:413
  18.0 5.5 %all-to-all-done = s32[128,1,16]{2,1,0:T(1,128)S(1)} async-done(((s32[128,1,16]{2,1,0:T(1,128)}), s32[128,1,16]{2,1,0:T(1,128)S(1)}, u32[]{:S(2)}, u32[]{:S(2)}) %all-to-all-start) | async-done | bytes 8224 | tf_op jit(solution)/shard_map/all_to_all | solution.py:396
  23.5 0.5 provide.1
  23.9 0.0 copy-start
  23.9 1.2 %copy-done = f32[3584,128]{1,0:T(8,128)} copy-done((f32[3584,128]{1,0:T(8,128)}, f32[3584,128]{1,0:T(8,128)S(1)}, u32[]{:S(2)}) %copy-start) | copy-done | bytes 1835032
  25.2 0.0 copy-start.3
  25.2 0.0 copy-start.5
  25.2 0.0 copy-start.7
  25.2 0.0 copy-start.8
  25.2 0.0 copy-start.6
  25.2 4.6 %all-to-all-start.1 = ((f32[128,7,4,128]{3,2,1,0:T(4,128)}), f32[128,7,4,128]{3,2,1,0:T(4,128)S(1)}, u32[]{:S(2)}, u32[]{:S(2)}) async-start(f32[128,7,4,128]{3,2,1,0:T(4,128)} %bitcast.20), calls=%async_computation.1 | async-start | bytes 3670016 | tf_op jit(solution)/shard_map/all_to_all | solution.py:432
  29.8 0.0 copy-done.3
  29.8 0.0 copy-done.5
  29.9 3.5 %collective-permute-start = (f32[4,4,128]{2,1,0:T(4,128)S(1)}, f32[4,4,128]{2,1,0:T(4,128)S(1)}, u32[]{:S(2)}, u32[]{:S(2)}) collective-permute-start(f32[4,4,128]{2,1,0:T(4,128)S(1)} %get-tuple-element.19), channel_id=1, source_target_pairs={{0,16},{16,32},{32,48},{48,64},{64,80},{80,96},{96,112},{1,17},{17... | collective-permute-start | bytes 24584 | tf_op jit(solution)/shard_map/ppermute | solution.py:407
  33.4 2.1 %collective-permute-start.1 = (f32[4,4,128]{2,1,0:T(4,128)S(1)}, f32[4,4,128]{2,1,0:T(4,128)S(1)}, u32[]{:S(2)}, u32[]{:S(2)}) collective-permute-start(f32[4,4,128]{2,1,0:T(4,128)S(1)} %get-tuple-element.18), channel_id=1, source_target_pairs={{16,0},{32,16},{48,32},{64,48},{80,64},{96,80},{112,96},{17,1},{33... | collective-permute-start | bytes 24584 | tf_op jit(solution)/shard_map/ppermute | solution.py:408
  35.5 0.0 copy-done.7
  35.6 0.0 copy-done.8
  35.6 0.1 copy.35
  35.7 21.0 %all-to-all-done.1 = f32[128,7,4,128]{3,2,1,0:T(4,128)S(1)} async-done(((f32[128,7,4,128]{3,2,1,0:T(4,128)}), f32[128,7,4,128]{3,2,1,0:T(4,128)S(1)}, u32[]{:S(2)}, u32[]{:S(2)}) %all-to-all-start.1) | async-done | bytes 1835040 | tf_op jit(solution)/shard_map/all_to_all | solution.py:432
  56.6 0.0 copy-done.6
  56.6 12.0 %pairs.1 = (f32[9,32,128]{2,1,0:T(8,128)}, f32[3,32,128]{2,1,0:T(8,128)S(1)}, f32[1536,128]{1,0:T(8,128)S(1)}) custom-call(s32[2,256]{1,0:T(2,128)S(1)} %copy-done.6, f32[3,32,128]{2,1,0:T(8,128)S(1)} %bitcast.27, f32[3,32,128]{2,1,0:T(8,128)S(1)} %bitcast.30, f32[32,128]{1,0:T(8,128)S(1)} %fusion.2.weight_ref, f32[2,32,128]{2,1,0:T(8,128)S(1)} %bitcast.33, ...), custom_call_target="tpu_custom_call" | custom-call | flops 60000000 | bytes 4000000 | tf_op jit(solution)/shard_map/pairs/pallas_call | solution.py:349
  68.6 0.0 copy-start.1
  68.6 0.9 copy-done.1
  69.5 4.9 %all-to-all-start.2 = ((f32[128,3,4,128]{3,2,1,0:T(4,128)}), f32[128,3,4,128]{3,2,1,0:T(4,128)S(1)}, u32[]{:S(2)}, u32[]{:S(2)}) async-start(f32[128,3,4,128]{3,2,1,0:T(4,128)} %bitcast.25), calls=%async_computation.2 | async-start | bytes 1572864 | tf_op jit(solution)/shard_map/all_to_all | solution.py:437
  74.5 0.1 add_select_fusion
  74.6 0.2 select_n.33.code_ref
  74.8 0.0 collective-permute-done.below_ref
  74.8 0.0 collective-permute-done.1.above_ref
  74.9 5.0 %contact.1.force_ref = f32[3,32,128]{2,1,0:T(8,128)S(1)} custom-call(f32[3,32,128]{2,1,0:T(8,128)S(1)} %bitcast.28, f32[3,32,128]{2,1,0:T(8,128)S(1)} %bitcast.31, f32[32,128]{1,0:T(8,128)S(1)} %fusion.2.weight_ref, f32[4,4,128]{2,1,0:T(4,128)S(1)} %collective-permute-done.below_ref, f32[4,4,128]{2,1,0:T(4,128)S(1)} %collective-permute-done.1.above_ref, ...), custom_call_target="tpu_custom_call" | custom-call | flops 20000000 | bytes 1000000 | tf_op jit(solution)/shard_map/contact/pallas_call | solution.py:440
  79.9 11.2 %all-to-all-done.2 = f32[128,3,4,128]{3,2,1,0:T(4,128)S(1)} async-done(((f32[128,3,4,128]{3,2,1,0:T(4,128)}), f32[128,3,4,128]{3,2,1,0:T(4,128)S(1)}, u32[]{:S(2)}, u32[]{:S(2)}) %all-to-all-start.2) | async-done | bytes 786464 | tf_op jit(solution)/shard_map/all_to_all | solution.py:437
  91.0 1.0 %returned.1 = f32[3,32,128]{2,1,0:T(8,128)} custom-call(s32[1,1536]{1,0:T(1,128)S(1)} %select_n.33.code_ref, f32[1536,128]{1,0:T(8,128)S(1)} %bitcast.21, f32[3,32,128]{2,1,0:T(8,128)S(1)} %contact.1.force_ref), custom_call_target="tpu_custom_call" | custom-call | flops 1000000 | bytes 1000000 | tf_op jit(solution)/shard_map/returned/pallas_call | solution.py:450
  (7 shorter events, 0.1 us)
Async XLA Ops:
  2.4 21.0 %all-to-all-start = ((s32[128,1,16]{2,1,0:T(1,128)}), s32[128,1,16]{2,1,0:T(1,128)S(1)}, u32[]{:S(2)}, u32[]{:S(2)}) async-start(s32[128,1,16]{2,1,0:T(1,128)} %bitcast.34), calls=%async_computation | async-start | bytes 131072 | tf_op jit(solution)/shard_map/all_to_all | solution.py:396
  15.4 0.8 copy-start.2
  16.2 0.8 copy-start.4
  23.9 1.2 %copy-start = (f32[3584,128]{1,0:T(8,128)}, f32[3584,128]{1,0:T(8,128)S(1)}, u32[]{:S(2)}) copy-start(f32[3584,128]{1,0:T(8,128)S(1)} %provide.1) | copy-start | bytes 5505028
  25.2 4.6 %copy-start.3 = (f32[32,3,128]{2,0,1:T(8,128)S(1)}, f32[32,3,128]{2,0,1:T(8,128)}, u32[]{:S(2)}) copy-start(f32[32,3,128]{2,0,1:T(8,128)} %param.8) | copy-start | bytes 147460
  25.2 4.6 %copy-start.5 = (f32[32,3,128]{2,0,1:T(8,128)S(1)}, f32[32,3,128]{2,0,1:T(8,128)}, u32[]{:S(2)}) copy-start(f32[32,3,128]{2,0,1:T(8,128)} %param.9) | copy-start | bytes 147460
  25.2 10.4 %copy-start.7 = (f32[32,2,128]{2,1,0:T(2,128)S(1)}, f32[32,2,128]{2,1,0:T(2,128)}, u32[]{:S(2)}) copy-start(f32[32,2,128]{2,1,0:T(2,128)} %param.11) | copy-start | bytes 98308
  25.2 10.4 %copy-start.8 = (s32[32,2]{0,1:T(2,128)S(1)}, s32[32,2]{0,1:T(2,128)}, u32[]{:S(2)}) copy-start(s32[32,2]{0,1:T(2,128)} %param.15) | copy-start | bytes 772
  25.2 31.5 %copy-start.6 = (s32[2,256]{1,0:T(2,128)S(1)}, s32[2,256]{1,0:T(2,128)}, u32[]{:S(2)}) copy-start(s32[2,256]{1,0:T(2,128)} %get-tuple-element.11.start_ref) | copy-start | bytes 6148
  25.2 31.4 %all-to-all-start.1 = ((f32[128,7,4,128]{3,2,1,0:T(4,128)}), f32[128,7,4,128]{3,2,1,0:T(4,128)S(1)}, u32[]{:S(2)}, u32[]{:S(2)}) async-start(f32[128,7,4,128]{3,2,1,0:T(4,128)} %bitcast.20), calls=%async_computation.1 | async-start | bytes 3670016 | tf_op jit(solution)/shard_map/all_to_all | solution.py:432
  29.9 45.0 %collective-permute-start = (f32[4,4,128]{2,1,0:T(4,128)S(1)}, f32[4,4,128]{2,1,0:T(4,128)S(1)}, u32[]{:S(2)}, u32[]{:S(2)}) collective-permute-start(f32[4,4,128]{2,1,0:T(4,128)S(1)} %get-tuple-element.19), channel_id=1, source_target_pairs={{0,16},{16,32},{32,48},{48,64},{64,80},{80,96},{96,112},{1,17},{17... | collective-permute-start | bytes 24584 | tf_op jit(solution)/shard_map/ppermute | solution.py:407
  33.4 41.4 %collective-permute-start.1 = (f32[4,4,128]{2,1,0:T(4,128)S(1)}, f32[4,4,128]{2,1,0:T(4,128)S(1)}, u32[]{:S(2)}, u32[]{:S(2)}) collective-permute-start(f32[4,4,128]{2,1,0:T(4,128)S(1)} %get-tuple-element.18), channel_id=1, source_target_pairs={{16,0},{32,16},{48,32},{64,48},{80,64},{96,80},{112,96},{17,1},{33... | collective-permute-start | bytes 24584 | tf_op jit(solution)/shard_map/ppermute | solution.py:408
  68.6 0.9 copy-start.1
  69.5 21.5 %all-to-all-start.2 = ((f32[128,3,4,128]{3,2,1,0:T(4,128)}), f32[128,3,4,128]{3,2,1,0:T(4,128)S(1)}, u32[]{:S(2)}, u32[]{:S(2)}) async-start(f32[128,3,4,128]{3,2,1,0:T(4,128)} %bitcast.25), calls=%async_computation.2 | async-start | bytes 1572864 | tf_op jit(solution)/shard_map/all_to_all | solution.py:437

commit v6 on v5

--- a/solution.py
+++ b/solution.py
@@ -193,9 +193,9 @@
             h, m, l = parts(place, 3)
             cols = pl.ds(k * lanes, lanes)
             b_all[b, :, cols] = jnp.concatenate([h, h, h, m, m, l], axis=0).astype(BF16)
-            weight = t[6:7]
-            plain = jnp.where(row == 6, 1.0, t)
-            feats = [weight * plain] + [(weight * t[3 + a : 4 + a]) * plain for a in range(3)]
+            weight = raw[k, pl.ds(6, 8, stride=0), :]
+            heavy = weight * jnp.where(row == 6, 1.0, t)
+            feats = [heavy] + [raw[k, pl.ds(3 + a, 8, stride=0), :] * heavy for a in range(3)]
             split = [parts(v, 2) for v in feats]
             f_all[b, :, cols] = jnp.concatenate(
                 [v[0] for v in split] + [v[1] for v in split], axis=0
@@ -288,13 +288,14 @@
         return 0
 
     def both(g, _):
-        def block(q, _):
+        for q in range(2):
             forward(g, q)
+        middle(g - 1)
+        for q in range(2, GROUP):
+            forward(g, q)
+            backward(g - 1, q - 2)
+        for q in range(GROUP - 2, GROUP):
             backward(g - 1, q)
-            return 0
-
-        lax.fori_loop(0, GROUP, block, 0, unroll=GROUP)
-        middle(g)
         return 0
 
     def last(q, _):
@@ -303,8 +304,8 @@
 
     groups = blocks // GROUP
     lax.fori_loop(0, GROUP, first, 0, unroll=GROUP)
-    middle(0)
-    lax.fori_loop(1, groups, both, 0, unroll=3)
+    lax.fori_loop(1, groups, both, 0, unroll=groups - 1)
+    middle(groups - 1)
     lax.fori_loop(0, GROUP, last, 0, unroll=GROUP)
 
 

time: 92.6 us -> 91.6 us (0.989)
  Pallas kernels: 21.3 us -> 20.3 us
    pallas_call x1, Pallas kernels: 12 us -> 11 us  [main_call(): call(main_kernel, 'pairs', (jax.ShapeDtypeStruct((9, blocks, lanes), F32)...]
  transfers between devices with their start and end apart: 5 -> 5, of which waited for: 3 -> 3; matrix products, arithmetic and copies ran while one was open for 2% -> 2% of each run, Pallas kernels for 20% -> 19%
where the time goes in v6:
time: 91.6 us; the launch traced here: 91 us
  waiting for transfers between devices  37.8 us (41%)
  starting transfers between devices  26.4 us (29%)
  Pallas kernels  20.3 us (22%)
  local copies, waits for them, and re-layouts  4.06 us (4%)
  other arithmetic  1.67 us (2%)
    all_to_all x1, waiting for transfers between devices, per_device(): lax.all_to_all(picked.reshape(devices, ROWS, cap, lanes), AXES, split_axi...  21.2 us
    all_to_all x1, starting transfers between devices, per_device(): asked = lax.all_to_all(ask, AXES, split_axis=0, concat_axis=0, tiled=True)  11.5 us
    all_to_all x1, waiting for transfers between devices, per_device(): lax.all_to_all(back.reshape(devices, 3, cap, lanes), AXES, split_axis=0,...  11.2 us
    pallas_call x1, Pallas kernels, main_call(): call(main_kernel, 'pairs', (jax.ShapeDtypeStruct((9, blocks, lanes), F32)...  11 us
    all_to_all x1, waiting for transfers between devices, per_device(): asked = lax.all_to_all(ask, AXES, split_axis=0, concat_axis=0, tiled=True)  5.48 us
    pallas_call x1, Pallas kernels, per_device(): call(contact_kernel, 'contact', shape((3, blocks, lanes), F32), vmem(5) +...  5.03 us
    all_to_all x1, starting transfers between devices, per_device(): lax.all_to_all(back.reshape(devices, 3, cap, lanes), AXES, split_axis=0,...  4.88 us
    all_to_all x1, starting transfers between devices, per_device(): lax.all_to_all(picked.reshape(devices, ROWS, cap, lanes), AXES, split_axi...  4.56 us
  transfers between devices with their start and end apart: 5, of which 3 were waited for; matrix products, arithmetic and copies ran while one was open for 2% of the time, Pallas kernels for 19%

profile of v6, /device:TPU:1, one launch (start us, length us, event | category | flops | bytes accessed | tf_op | source)
XLA Modules:
  0.0 91.0 jit_solution(14534890210341143208)
XLA Ops:
  0.6 1.8 %plan.1 = (s32[128,16]{1,0:T(8,128)}, s32[2,256]{1,0:T(2,128)}) custom-call(s32[8,1,32]{2,1,0:T(1,128)} %bitcast.36, s32[8,32]{1,0:T(8,128)} %bitcast.37), custom_call_target="tpu_custom_call" | custom-call | flops 1000000 | bytes 1000000 | tf_op jit(solution)/shard_map/plan/pallas_call | solution.py:384
  2.4 11.5 %all-to-all-start = ((s32[128,1,16]{2,1,0:T(1,128)}), s32[128,1,16]{2,1,0:T(1,128)S(1)}, u32[]{:S(2)}, u32[]{:S(2)}) async-start(s32[128,1,16]{2,1,0:T(1,128)} %bitcast.34), calls=%async_computation | async-start | bytes 131072 | tf_op jit(solution)/shard_map/all_to_all | solution.py:397
  13.9 0.7 broadcast_subtract_fusion
  14.6 0.8 fusion.2.weight_ref
  15.4 0.0 copy-start.2
  15.4 0.8 copy-done.2
  16.2 0.0 copy-start.4
  16.2 0.8 copy-done.4
  17.0 1.0 %own.1 = (bf16[32,128,48]{2,1,0:T(8,128)(2,1)S(1)}, f32[256,128]{1,0:T(8,128)S(1)}, bf16[96,896]{1,0:T(8,128)(2,1)S(1)}) custom-call(f32[3,32,128]{2,1,0:T(8,128)S(1)} %bitcast.26, f32[3,32,128]{2,1,0:T(8,128)S(1)} %bitcast.29, f32[32,128]{1,0:T(8,128)S(1)} %fusion.2.weight_ref), custom_call_target="tpu_custom_call" | custom-call | flops 1000000 | bytes 1000000 | tf_op jit(solution)/shard_map/own/pallas_call | solution.py:414
  18.0 5.5 %all-to-all-done = s32[128,1,16]{2,1,0:T(1,128)S(1)} async-done(((s32[128,1,16]{2,1,0:T(1,128)}), s32[128,1,16]{2,1,0:T(1,128)S(1)}, u32[]{:S(2)}, u32[]{:S(2)}) %all-to-all-start) | async-done | bytes 8224 | tf_op jit(solution)/shard_map/all_to_all | solution.py:397
  23.5 0.5 provide.1
  23.9 0.0 copy-start
  23.9 1.2 %copy-done = f32[3584,128]{1,0:T(8,128)} copy-done((f32[3584,128]{1,0:T(8,128)}, f32[3584,128]{1,0:T(8,128)S(1)}, u32[]{:S(2)}) %copy-start) | copy-done | bytes 1835032
  25.2 0.0 copy-start.3
  25.2 0.0 copy-start.5
  25.2 0.0 copy-start.7
  25.2 0.0 copy-start.8
  25.2 0.0 copy-start.6
  25.2 4.6 %all-to-all-start.1 = ((f32[128,7,4,128]{3,2,1,0:T(4,128)}), f32[128,7,4,128]{3,2,1,0:T(4,128)S(1)}, u32[]{:S(2)}, u32[]{:S(2)}) async-start(f32[128,7,4,128]{3,2,1,0:T(4,128)} %bitcast.20), calls=%async_computation.1 | async-start | bytes 3670016 | tf_op jit(solution)/shard_map/all_to_all | solution.py:433
  29.8 0.0 copy-done.3
  29.8 0.0 copy-done.5
  29.9 3.5 %collective-permute-start = (f32[4,4,128]{2,1,0:T(4,128)S(1)}, f32[4,4,128]{2,1,0:T(4,128)S(1)}, u32[]{:S(2)}, u32[]{:S(2)}) collective-permute-start(f32[4,4,128]{2,1,0:T(4,128)S(1)} %get-tuple-element.19), channel_id=1, source_target_pairs={{0,16},{16,32},{32,48},{48,64},{64,80},{80,96},{96,112},{1,17},{17... | collective-permute-start | bytes 24584 | tf_op jit(solution)/shard_map/ppermute | solution.py:408
  33.4 1.9 %collective-permute-start.1 = (f32[4,4,128]{2,1,0:T(4,128)S(1)}, f32[4,4,128]{2,1,0:T(4,128)S(1)}, u32[]{:S(2)}, u32[]{:S(2)}) collective-permute-start(f32[4,4,128]{2,1,0:T(4,128)S(1)} %get-tuple-element.18), channel_id=1, source_target_pairs={{16,0},{32,16},{48,32},{64,48},{80,64},{96,80},{112,96},{17,1},{33... | collective-permute-start | bytes 24584 | tf_op jit(solution)/shard_map/ppermute | solution.py:409
  35.4 0.0 copy-done.7
  35.4 0.0 copy-done.8
  35.4 0.1 copy.35
  35.5 21.2 %all-to-all-done.1 = f32[128,7,4,128]{3,2,1,0:T(4,128)S(1)} async-done(((f32[128,7,4,128]{3,2,1,0:T(4,128)}), f32[128,7,4,128]{3,2,1,0:T(4,128)S(1)}, u32[]{:S(2)}, u32[]{:S(2)}) %all-to-all-start.1) | async-done | bytes 1835040 | tf_op jit(solution)/shard_map/all_to_all | solution.py:433
  56.6 0.0 copy-done.6
  56.6 11.0 %pairs.1 = (f32[9,32,128]{2,1,0:T(8,128)}, f32[3,32,128]{2,1,0:T(8,128)S(1)}, f32[1536,128]{1,0:T(8,128)S(1)}) custom-call(s32[2,256]{1,0:T(2,128)S(1)} %copy-done.6, f32[3,32,128]{2,1,0:T(8,128)S(1)} %bitcast.27, f32[3,32,128]{2,1,0:T(8,128)S(1)} %bitcast.30, f32[32,128]{1,0:T(8,128)S(1)} %fusion.2.weight_ref, f32[2,32,128]{2,1,0:T(8,128)S(1)} %bitcast.33, ...), custom_call_target="tpu_custom_call" | custom-call | flops 60000000 | bytes 4000000 | tf_op jit(solution)/shard_map/pairs/pallas_call | solution.py:350
  67.6 0.0 copy-start.1
  67.6 0.9 copy-done.1
  68.5 4.9 %all-to-all-start.2 = ((f32[128,3,4,128]{3,2,1,0:T(4,128)}), f32[128,3,4,128]{3,2,1,0:T(4,128)S(1)}, u32[]{:S(2)}, u32[]{:S(2)}) async-start(f32[128,3,4,128]{3,2,1,0:T(4,128)} %bitcast.25), calls=%async_computation.2 | async-start | bytes 1572864 | tf_op jit(solution)/shard_map/all_to_all | solution.py:438
  73.5 0.1 add_select_fusion
  73.6 0.2 select_n.33.code_ref
  73.8 0.0 collective-permute-done.below_ref
  73.8 0.0 collective-permute-done.1.above_ref
  73.8 5.0 %contact.1.force_ref = f32[3,32,128]{2,1,0:T(8,128)S(1)} custom-call(f32[3,32,128]{2,1,0:T(8,128)S(1)} %bitcast.28, f32[3,32,128]{2,1,0:T(8,128)S(1)} %bitcast.31, f32[32,128]{1,0:T(8,128)S(1)} %fusion.2.weight_ref, f32[4,4,128]{2,1,0:T(4,128)S(1)} %collective-permute-done.below_ref, f32[4,4,128]{2,1,0:T(4,128)S(1)} %collective-permute-done.1.above_ref, ...), custom_call_target="tpu_custom_call" | custom-call | flops 20000000 | bytes 1000000 | tf_op jit(solution)/shard_map/contact/pallas_call | solution.py:441
  78.9 11.2 %all-to-all-done.2 = f32[128,3,4,128]{3,2,1,0:T(4,128)S(1)} async-done(((f32[128,3,4,128]{3,2,1,0:T(4,128)}), f32[128,3,4,128]{3,2,1,0:T(4,128)S(1)}, u32[]{:S(2)}, u32[]{:S(2)}) %all-to-all-start.2) | async-done | bytes 786464 | tf_op jit(solution)/shard_map/all_to_all | solution.py:438
  90.0 1.0 %returned.1 = f32[3,32,128]{2,1,0:T(8,128)} custom-call(s32[1,1536]{1,0:T(1,128)S(1)} %select_n.33.code_ref, f32[1536,128]{1,0:T(8,128)S(1)} %bitcast.21, f32[3,32,128]{2,1,0:T(8,128)S(1)} %contact.1.force_ref), custom_call_target="tpu_custom_call" | custom-call | flops 1000000 | bytes 1000000 | tf_op jit(solution)/shard_map/returned/pallas_call | solution.py:451
  (7 shorter events, 0.1 us)
Async XLA Ops:
  2.4 21.0 %all-to-all-start = ((s32[128,1,16]{2,1,0:T(1,128)}), s32[128,1,16]{2,1,0:T(1,128)S(1)}, u32[]{:S(2)}, u32[]{:S(2)}) async-start(s32[128,1,16]{2,1,0:T(1,128)} %bitcast.34), calls=%async_computation | async-start | bytes 131072 | tf_op jit(solution)/shard_map/all_to_all | solution.py:397
  15.4 0.8 copy-start.2
  16.2 0.8 copy-start.4
  23.9 1.2 %copy-start = (f32[3584,128]{1,0:T(8,128)}, f32[3584,128]{1,0:T(8,128)S(1)}, u32[]{:S(2)}) copy-start(f32[3584,128]{1,0:T(8,128)S(1)} %provide.1) | copy-start | bytes 5505028
  25.2 4.6 %copy-start.3 = (f32[32,3,128]{2,0,1:T(8,128)S(1)}, f32[32,3,128]{2,0,1:T(8,128)}, u32[]{:S(2)}) copy-start(f32[32,3,128]{2,0,1:T(8,128)} %param.8) | copy-start | bytes 147460
  25.2 4.6 %copy-start.5 = (f32[32,3,128]{2,0,1:T(8,128)S(1)}, f32[32,3,128]{2,0,1:T(8,128)}, u32[]{:S(2)}) copy-start(f32[32,3,128]{2,0,1:T(8,128)} %param.9) | copy-start | bytes 147460
  25.2 10.2 %copy-start.7 = (f32[32,2,128]{2,1,0:T(2,128)S(1)}, f32[32,2,128]{2,1,0:T(2,128)}, u32[]{:S(2)}) copy-start(f32[32,2,128]{2,1,0:T(2,128)} %param.11) | copy-start | bytes 98308
  25.2 10.2 %copy-start.8 = (s32[32,2]{0,1:T(2,128)S(1)}, s32[32,2]{0,1:T(2,128)}, u32[]{:S(2)}) copy-start(s32[32,2]{0,1:T(2,128)} %param.15) | copy-start | bytes 772
  25.2 31.5 %copy-start.6 = (s32[2,256]{1,0:T(2,128)S(1)}, s32[2,256]{1,0:T(2,128)}, u32[]{:S(2)}) copy-start(s32[2,256]{1,0:T(2,128)} %get-tuple-element.11.start_ref) | copy-start | bytes 6148
  25.2 31.4 %all-to-all-start.1 = ((f32[128,7,4,128]{3,2,1,0:T(4,128)}), f32[128,7,4,128]{3,2,1,0:T(4,128)S(1)}, u32[]{:S(2)}, u32[]{:S(2)}) async-start(f32[128,7,4,128]{3,2,1,0:T(4,128)} %bitcast.20), calls=%async_computation.1 | async-start | bytes 3670016 | tf_op jit(solution)/shard_map/all_to_all | solution.py:433
  29.9 44.0 %collective-permute-start = (f32[4,4,128]{2,1,0:T(4,128)S(1)}, f32[4,4,128]{2,1,0:T(4,128)S(1)}, u32[]{:S(2)}, u32[]{:S(2)}) collective-permute-start(f32[4,4,128]{2,1,0:T(4,128)S(1)} %get-tuple-element.19), channel_id=1, source_target_pairs={{0,16},{16,32},{32,48},{48,64},{64,80},{80,96},{96,112},{1,17},{17... | collective-permute-start | bytes 24584 | tf_op jit(solution)/shard_map/ppermute | solution.py:408
  33.4 40.4 %collective-permute-start.1 = (f32[4,4,128]{2,1,0:T(4,128)S(1)}, f32[4,4,128]{2,1,0:T(4,128)S(1)}, u32[]{:S(2)}, u32[]{:S(2)}) collective-permute-start(f32[4,4,128]{2,1,0:T(4,128)S(1)} %get-tuple-element.18), channel_id=1, source_target_pairs={{16,0},{32,16},{48,32},{64,48},{80,64},{96,80},{112,96},{17,1},{33... | collective-permute-start | bytes 24584 | tf_op jit(solution)/shard_map/ppermute | solution.py:409
  67.6 0.9 copy-start.1
  68.5 21.5 %all-to-all-start.2 = ((f32[128,3,4,128]{3,2,1,0:T(4,128)}), f32[128,3,4,128]{3,2,1,0:T(4,128)S(1)}, u32[]{:S(2)}, u32[]{:S(2)}) async-start(f32[128,3,4,128]{3,2,1,0:T(4,128)} %bitcast.25), calls=%async_computation.2 | async-start | bytes 1572864 | tf_op jit(solution)/shard_map/all_to_all | solution.py:438

commit v7 on v6

--- a/solution.py
+++ b/solution.py
@@ -64,13 +64,11 @@
     named = owner == lax.broadcasted_iota(jnp.int32, (devices, total), 0)
     hot = named.astype(F32)
     rank = mm(hot.astype(BF16), earlier, NN)
-    lane = lax.broadcasted_iota(jnp.int32, (width, total), 0)
-    ask = jnp.zeros((devices, width), F32)
-    for s in range(cap):
-        chosen = jnp.where(rank == float(s), hot, 0.0).astype(BF16)
-        ask = ask + mm(chosen, jnp.where(lane == s, local, 0.0).astype(BF16), NT)
-    ask_ref[...] = ask.astype(jnp.int32) - 1
-    place = jnp.sum(hot * rank, axis=0, keepdims=True).astype(jnp.int32)
+    place = jnp.sum(hot * rank, axis=0, keepdims=True)
+    lane = lax.broadcasted_iota(jnp.int32, (width, total), 0).astype(F32)
+    chosen = jnp.where(lane == place, local, 0.0).astype(BF16)
+    ask_ref[...] = mm(hot.astype(BF16), chosen, NT).astype(jnp.int32) - 1
+    place = place.astype(jnp.int32)
     start_ref[0:1, :] = owner * (cap * ROWS) + place
     start_ref[1:2, :] = owner * (cap * 3) + place
 

time: 91.6 us -> 91.5 us (level)
  no operation moved by 1% of the time
where the time goes in v7:
time: 91.5 us; the launch traced here: 91 us
  waiting for transfers between devices  37.8 us (41%)
  starting transfers between devices  26.4 us (29%)
  Pallas kernels  20.2 us (22%)
  local copies, waits for them, and re-layouts  4.06 us (4%)
  other arithmetic  1.67 us (2%)
    all_to_all x1, waiting for transfers between devices, per_device(): lax.all_to_all(picked.reshape(devices, ROWS, cap, lanes), AXES, split_axi...  21.2 us
    all_to_all x1, starting transfers between devices, per_device(): asked = lax.all_to_all(ask, AXES, split_axis=0, concat_axis=0, tiled=True)  11.5 us
    all_to_all x1, waiting for transfers between devices, per_device(): lax.all_to_all(back.reshape(devices, 3, cap, lanes), AXES, split_axis=0,...  11.2 us
    pallas_call x1, Pallas kernels, main_call(): call(main_kernel, 'pairs', (jax.ShapeDtypeStruct((9, blocks, lanes), F32)...  11 us
    all_to_all x1, waiting for transfers between devices, per_device(): asked = lax.all_to_all(ask, AXES, split_axis=0, concat_axis=0, tiled=True)  5.48 us
    pallas_call x1, Pallas kernels, per_device(): call(contact_kernel, 'contact', shape((3, blocks, lanes), F32), vmem(5) +...  5.03 us
    all_to_all x1, starting transfers between devices, per_device(): lax.all_to_all(back.reshape(devices, 3, cap, lanes), AXES, split_axis=0,...  4.89 us
    all_to_all x1, starting transfers between devices, per_device(): lax.all_to_all(picked.reshape(devices, ROWS, cap, lanes), AXES, split_axi...  4.56 us
  transfers between devices with their start and end apart: 5, of which 3 were waited for; matrix products, arithmetic and copies ran while one was open for 2% of the time, Pallas kernels for 19%

profile of v7, /device:TPU:1, one launch (start us, length us, event | category | flops | bytes accessed | tf_op | source)
XLA Modules:
  0.0 91.0 jit_solution(15194673040068459314)
XLA Ops:
  0.6 1.7 %plan.1 = (s32[128,16]{1,0:T(8,128)}, s32[2,256]{1,0:T(2,128)}) custom-call(s32[8,1,32]{2,1,0:T(1,128)} %bitcast.36, s32[8,32]{1,0:T(8,128)} %bitcast.37), custom_call_target="tpu_custom_call" | custom-call | flops 1000000 | bytes 1000000 | tf_op jit(solution)/shard_map/plan/pallas_call | solution.py:382
  2.4 11.5 %all-to-all-start = ((s32[128,1,16]{2,1,0:T(1,128)}), s32[128,1,16]{2,1,0:T(1,128)S(1)}, u32[]{:S(2)}, u32[]{:S(2)}) async-start(s32[128,1,16]{2,1,0:T(1,128)} %bitcast.34), calls=%async_computation | async-start | bytes 131072 | tf_op jit(solution)/shard_map/all_to_all | solution.py:395
  13.9 0.7 broadcast_subtract_fusion
  14.5 0.8 fusion.2.weight_ref
  15.3 0.0 copy-start.2
  15.3 0.8 copy-done.2
  16.1 0.0 copy-start.4
  16.1 0.8 copy-done.4
  16.9 1.0 %own.1 = (bf16[32,128,48]{2,1,0:T(8,128)(2,1)S(1)}, f32[256,128]{1,0:T(8,128)S(1)}, bf16[96,896]{1,0:T(8,128)(2,1)S(1)}) custom-call(f32[3,32,128]{2,1,0:T(8,128)S(1)} %bitcast.26, f32[3,32,128]{2,1,0:T(8,128)S(1)} %bitcast.29, f32[32,128]{1,0:T(8,128)S(1)} %fusion.2.weight_ref), custom_call_target="tpu_custom_call" | custom-call | flops 1000000 | bytes 1000000 | tf_op jit(solution)/shard_map/own/pallas_call | solution.py:412
  17.9 5.5 %all-to-all-done = s32[128,1,16]{2,1,0:T(1,128)S(1)} async-done(((s32[128,1,16]{2,1,0:T(1,128)}), s32[128,1,16]{2,1,0:T(1,128)S(1)}, u32[]{:S(2)}, u32[]{:S(2)}) %all-to-all-start) | async-done | bytes 8224 | tf_op jit(solution)/shard_map/all_to_all | solution.py:395
  23.4 0.5 provide.1
  23.9 0.0 copy-start
  23.9 1.2 %copy-done = f32[3584,128]{1,0:T(8,128)} copy-done((f32[3584,128]{1,0:T(8,128)}, f32[3584,128]{1,0:T(8,128)S(1)}, u32[]{:S(2)}) %copy-start) | copy-done | bytes 1835032
  25.1 0.0 copy-start.3
  25.1 0.0 copy-start.5
  25.1 0.0 copy-start.7
  25.1 0.0 copy-start.8
  25.1 0.0 copy-start.6
  25.2 4.6 %all-to-all-start.1 = ((f32[128,7,4,128]{3,2,1,0:T(4,128)}), f32[128,7,4,128]{3,2,1,0:T(4,128)S(1)}, u32[]{:S(2)}, u32[]{:S(2)}) async-start(f32[128,7,4,128]{3,2,1,0:T(4,128)} %bitcast.20), calls=%async_computation.1 | async-start | bytes 3670016 | tf_op jit(solution)/shard_map/all_to_all | solution.py:431
  29.7 0.0 copy-done.3
  29.7 0.0 copy-done.5
  29.8 3.5 %collective-permute-start = (f32[4,4,128]{2,1,0:T(4,128)S(1)}, f32[4,4,128]{2,1,0:T(4,128)S(1)}, u32[]{:S(2)}, u32[]{:S(2)}) collective-permute-start(f32[4,4,128]{2,1,0:T(4,128)S(1)} %get-tuple-element.19), channel_id=1, source_target_pairs={{0,16},{16,32},{32,48},{48,64},{64,80},{80,96},{96,112},{1,17},{17... | collective-permute-start | bytes 24584 | tf_op jit(solution)/shard_map/ppermute | solution.py:406
  33.4 1.9 %collective-permute-start.1 = (f32[4,4,128]{2,1,0:T(4,128)S(1)}, f32[4,4,128]{2,1,0:T(4,128)S(1)}, u32[]{:S(2)}, u32[]{:S(2)}) collective-permute-start(f32[4,4,128]{2,1,0:T(4,128)S(1)} %get-tuple-element.18), channel_id=1, source_target_pairs={{16,0},{32,16},{48,32},{64,48},{80,64},{96,80},{112,96},{17,1},{33... | collective-permute-start | bytes 24584 | tf_op jit(solution)/shard_map/ppermute | solution.py:407
  35.3 0.0 copy-done.7
  35.3 0.0 copy-done.8
  35.3 0.1 copy.35
  35.4 21.2 %all-to-all-done.1 = f32[128,7,4,128]{3,2,1,0:T(4,128)S(1)} async-done(((f32[128,7,4,128]{3,2,1,0:T(4,128)}), f32[128,7,4,128]{3,2,1,0:T(4,128)S(1)}, u32[]{:S(2)}, u32[]{:S(2)}) %all-to-all-start.1) | async-done | bytes 1835040 | tf_op jit(solution)/shard_map/all_to_all | solution.py:431
  56.6 0.0 copy-done.6
  56.6 11.0 %pairs.1 = (f32[9,32,128]{2,1,0:T(8,128)}, f32[3,32,128]{2,1,0:T(8,128)S(1)}, f32[1536,128]{1,0:T(8,128)S(1)}) custom-call(s32[2,256]{1,0:T(2,128)S(1)} %copy-done.6, f32[3,32,128]{2,1,0:T(8,128)S(1)} %bitcast.27, f32[3,32,128]{2,1,0:T(8,128)S(1)} %bitcast.30, f32[32,128]{1,0:T(8,128)S(1)} %fusion.2.weight_ref, f32[2,32,128]{2,1,0:T(8,128)S(1)} %bitcast.33, ...), custom_call_target="tpu_custom_call" | custom-call | flops 60000000 | bytes 4000000 | tf_op jit(solution)/shard_map/pairs/pallas_call | solution.py:348
  67.6 0.0 copy-start.1
  67.6 0.9 copy-done.1
  68.5 4.9 %all-to-all-start.2 = ((f32[128,3,4,128]{3,2,1,0:T(4,128)}), f32[128,3,4,128]{3,2,1,0:T(4,128)S(1)}, u32[]{:S(2)}, u32[]{:S(2)}) async-start(f32[128,3,4,128]{3,2,1,0:T(4,128)} %bitcast.25), calls=%async_computation.2 | async-start | bytes 1572864 | tf_op jit(solution)/shard_map/all_to_all | solution.py:436
  73.4 0.1 add_select_fusion
  73.6 0.2 select_n.33.code_ref
  73.8 0.0 collective-permute-done.below_ref
  73.8 0.0 collective-permute-done.1.above_ref
  73.8 5.0 %contact.1.force_ref = f32[3,32,128]{2,1,0:T(8,128)S(1)} custom-call(f32[3,32,128]{2,1,0:T(8,128)S(1)} %bitcast.28, f32[3,32,128]{2,1,0:T(8,128)S(1)} %bitcast.31, f32[32,128]{1,0:T(8,128)S(1)} %fusion.2.weight_ref, f32[4,4,128]{2,1,0:T(4,128)S(1)} %collective-permute-done.below_ref, f32[4,4,128]{2,1,0:T(4,128)S(1)} %collective-permute-done.1.above_ref, ...), custom_call_target="tpu_custom_call" | custom-call | flops 20000000 | bytes 1000000 | tf_op jit(solution)/shard_map/contact/pallas_call | solution.py:439
  78.8 11.2 %all-to-all-done.2 = f32[128,3,4,128]{3,2,1,0:T(4,128)S(1)} async-done(((f32[128,3,4,128]{3,2,1,0:T(4,128)}), f32[128,3,4,128]{3,2,1,0:T(4,128)S(1)}, u32[]{:S(2)}, u32[]{:S(2)}) %all-to-all-start.2) | async-done | bytes 786464 | tf_op jit(solution)/shard_map/all_to_all | solution.py:436
  90.0 1.0 %returned.1 = f32[3,32,128]{2,1,0:T(8,128)} custom-call(s32[1,1536]{1,0:T(1,128)S(1)} %select_n.33.code_ref, f32[1536,128]{1,0:T(8,128)S(1)} %bitcast.21, f32[3,32,128]{2,1,0:T(8,128)S(1)} %contact.1.force_ref), custom_call_target="tpu_custom_call" | custom-call | flops 1000000 | bytes 1000000 | tf_op jit(solution)/shard_map/returned/pallas_call | solution.py:449
  (7 shorter events, 0.1 us)
Async XLA Ops:
  2.4 21.0 %all-to-all-start = ((s32[128,1,16]{2,1,0:T(1,128)}), s32[128,1,16]{2,1,0:T(1,128)S(1)}, u32[]{:S(2)}, u32[]{:S(2)}) async-start(s32[128,1,16]{2,1,0:T(1,128)} %bitcast.34), calls=%async_computation | async-start | bytes 131072 | tf_op jit(solution)/shard_map/all_to_all | solution.py:395
  15.3 0.8 copy-start.2
  16.1 0.8 copy-start.4
  23.9 1.2 %copy-start = (f32[3584,128]{1,0:T(8,128)}, f32[3584,128]{1,0:T(8,128)S(1)}, u32[]{:S(2)}) copy-start(f32[3584,128]{1,0:T(8,128)S(1)} %provide.1) | copy-start | bytes 5505028
  25.1 4.6 %copy-start.3 = (f32[32,3,128]{2,0,1:T(8,128)S(1)}, f32[32,3,128]{2,0,1:T(8,128)}, u32[]{:S(2)}) copy-start(f32[32,3,128]{2,0,1:T(8,128)} %param.8) | copy-start | bytes 147460
  25.1 4.6 %copy-start.5 = (f32[32,3,128]{2,0,1:T(8,128)S(1)}, f32[32,3,128]{2,0,1:T(8,128)}, u32[]{:S(2)}) copy-start(f32[32,3,128]{2,0,1:T(8,128)} %param.9) | copy-start | bytes 147460
  25.1 10.2 %copy-start.7 = (f32[32,2,128]{2,1,0:T(2,128)S(1)}, f32[32,2,128]{2,1,0:T(2,128)}, u32[]{:S(2)}) copy-start(f32[32,2,128]{2,1,0:T(2,128)} %param.11) | copy-start | bytes 98308
  25.1 10.2 %copy-start.8 = (s32[32,2]{0,1:T(2,128)S(1)}, s32[32,2]{0,1:T(2,128)}, u32[]{:S(2)}) copy-start(s32[32,2]{0,1:T(2,128)} %param.15) | copy-start | bytes 772
  25.1 31.5 %copy-start.6 = (s32[2,256]{1,0:T(2,128)S(1)}, s32[2,256]{1,0:T(2,128)}, u32[]{:S(2)}) copy-start(s32[2,256]{1,0:T(2,128)} %get-tuple-element.11.start_ref) | copy-start | bytes 6148
  25.2 31.4 %all-to-all-start.1 = ((f32[128,7,4,128]{3,2,1,0:T(4,128)}), f32[128,7,4,128]{3,2,1,0:T(4,128)S(1)}, u32[]{:S(2)}, u32[]{:S(2)}) async-start(f32[128,7,4,128]{3,2,1,0:T(4,128)} %bitcast.20), calls=%async_computation.1 | async-start | bytes 3670016 | tf_op jit(solution)/shard_map/all_to_all | solution.py:431
  29.8 44.0 %collective-permute-start = (f32[4,4,128]{2,1,0:T(4,128)S(1)}, f32[4,4,128]{2,1,0:T(4,128)S(1)}, u32[]{:S(2)}, u32[]{:S(2)}) collective-permute-start(f32[4,4,128]{2,1,0:T(4,128)S(1)} %get-tuple-element.19), channel_id=1, source_target_pairs={{0,16},{16,32},{32,48},{48,64},{64,80},{80,96},{96,112},{1,17},{17... | collective-permute-start | bytes 24584 | tf_op jit(solution)/shard_map/ppermute | solution.py:406
  33.4 40.4 %collective-permute-start.1 = (f32[4,4,128]{2,1,0:T(4,128)S(1)}, f32[4,4,128]{2,1,0:T(4,128)S(1)}, u32[]{:S(2)}, u32[]{:S(2)}) collective-permute-start(f32[4,4,128]{2,1,0:T(4,128)S(1)} %get-tuple-element.18), channel_id=1, source_target_pairs={{16,0},{32,16},{48,32},{64,48},{80,64},{96,80},{112,96},{17,1},{33... | collective-permute-start | bytes 24584 | tf_op jit(solution)/shard_map/ppermute | solution.py:407
  67.6 0.9 copy-start.1
  68.5 21.5 %all-to-all-start.2 = ((f32[128,3,4,128]{3,2,1,0:T(4,128)}), f32[128,3,4,128]{3,2,1,0:T(4,128)S(1)}, u32[]{:S(2)}, u32[]{:S(2)}) async-start(f32[128,3,4,128]{3,2,1,0:T(4,128)} %bitcast.25), calls=%async_computation.2 | async-start | bytes 1572864 | tf_op jit(solution)/shard_map/all_to_all | solution.py:436
